TPU v7x, 256 devices: a whole 4x4x8 slice. The times are simulated.
256 devices in a mesh: depth: 128 (over x, y, z), slab: 2 (over core).
Axes of the slice: x: 4, y: 4, z: 8, core: 2. Of those that a mesh axis runs over, the one named last changes fastest.
Arguments:
- ref_feat: bfloat16 [4, 32, 128], P('slab'), may hold values from -9 to 9
- src_feat: bfloat16 [20480, 32, 128], P('depth'), may hold values from -9 to 9
- tile_owner: int32 [10240, 1], P(('depth', 'slab')), may hold values from 0 to 127; in each aligned block of 40 rows (0 to 39, 40 to 79, ...) at most 2 rows name the same one
- tile_local: int32 [10240], P(('depth', 'slab')), may hold values from 0 to 159
- col_shift: int32 [10240], P(('depth', 'slab')), may hold values from -16 to 16
- w_gates: bfloat16 [9, 64, 8], replicated, may hold values from -1.4375 to 1.4375
- bias_z: float32 [32], replicated
- bias_c: float32 [32], replicated, may hold values from -3 to 3
- w_out: float32 [32], replicated
Outputs:
- probability: float32 [512, 4, 128], P('depth', 'slab')
- depth_map: float32 [4, 128], P('slab')
Inputs may be any that keep to these rules, and one draw needn't show every extreme that they name: `tile_owner`: among the requests of one device no owner is named more than 2 times; in some devices one owner is named exactly 2 times.
All inputs are finite; a program needn't handle non-finite values.
Results may differ from a plain program's by a relative error of at most 0.00085.
Values may be sent and summed in bfloat16 or wider, within the bound.
No kernel may reach another device: no remote copies, remote signals or barrier semaphores. Data moves between devices by JAX's collectives and lax.ppermute only.
A program may use at most 64 MiB of HBM per device.

v0:
```python
import jax
import jax.numpy as jnp
from jax import lax
from jax.sharding import PartitionSpec as P

VIEWS = 5
PD = 4


def padded_2(cells, sides, width):
    for axis, dim in sides:
        count = lax.axis_size(axis)
        ends = count - 1
        head = lax.slice_in_dim(cells, 0, width, axis=dim)
        tail = lax.slice_in_dim(cells, cells.shape[dim] - width, cells.shape[dim], axis=dim)
        cells = jnp.concatenate(
            [
                lax.ppermute(tail, axis, [(i, (i + 1) % count) for i in range(ends)]),
                cells,
                lax.ppermute(head, axis, [((i + 1) % count, i) for i in range(ends)]),
            ],
            axis=dim,
        )
    return cells


def prefix_2(shard, axis, combine, identity):
    count, index = (lax.axis_size(axis), lax.axis_index(axis))
    everything = jax.tree.map(lambda part: lax.all_gather(part, axis), shard)
    start = jax.tree.map(
        lambda part, zero: jnp.broadcast_to(jnp.asarray(zero, part.dtype), part.shape),
        shard,
        identity,
    )

    def turn(k, before):
        reached = k < index
        new = combine(before, jax.tree.map(lambda part: part[k], everything))
        return jax.tree.map(lambda a, b: jnp.where(reached, a, b), new, before)

    return lax.fori_loop(0, count, turn, start)


def warp_tiles(tile_rows, shift_cols):
    col_count = tile_rows.shape[-1]
    positions = jnp.arange(col_count, dtype=jnp.int32)
    source_col = positions[None, :] - shift_cols[..., None, None]
    selector = (positions[:, None] == source_col).astype(tile_rows.dtype)
    moved = jnp.einsum(
        "...cy,...yx->...cx", tile_rows, selector, preferred_element_type=jnp.float32
    )
    return moved.astype(tile_rows.dtype)


def correlate(warped, ref_rows, groups):
    leading = warped.shape[:-2]
    feat_count = warped.shape[-2]
    col_count = warped.shape[-1]
    split_shape = leading + (groups, feat_count // groups, col_count)
    product = warped.astype(jnp.float32) * ref_rows.astype(jnp.float32)
    return jnp.sum(product.reshape(split_shape), axis=-2)


def body(ref_feat, src_feat, tile_owner, tile_local, col_shift, w_gates, bias_z, bias_c, w_out):
    owners = lax.axis_size("depth")
    row_count, feat_count, col_count = ref_feat.shape
    groups = w_gates.shape[2]
    hidden = w_gates.shape[1] // 2
    requests = tile_owner.shape[0]
    capacity = max(2, (3 * requests + 2 * owners - 1) // (2 * owners))
    owner_of = tile_owner[:, 0]
    onehot = (owner_of[:, None] == jnp.arange(owners, dtype=jnp.int32)[None, :]).astype(jnp.int32)
    slot_of = jnp.sum((jnp.cumsum(onehot, axis=0) - onehot) * onehot, axis=1)
    empty_ids = jnp.zeros((owners, capacity), jnp.int32)
    send_ids = empty_ids.at[owner_of, slot_of].set(tile_local)
    ref_rows = jnp.broadcast_to(
        ref_feat[None, None], (PD, VIEWS, row_count, feat_count, col_count)
    ).reshape(requests, feat_count, col_count)
    send_shift = empty_ids.at[owner_of, slot_of].set(col_shift)
    send_rows = (
        jnp.zeros((owners, capacity, feat_count, col_count), jnp.bfloat16)
        .at[owner_of, slot_of]
        .set(ref_rows)
    )
    slot_ids = lax.all_to_all(send_ids, "depth", split_axis=0, concat_axis=0, tiled=True)
    slot_shift = lax.all_to_all(send_shift, "depth", split_axis=0, concat_axis=0, tiled=True)
    slot_rows = lax.all_to_all(send_rows, "depth", split_axis=0, concat_axis=0, tiled=True)
    tile_rows = jnp.take(src_feat, slot_ids, axis=0)
    group_terms = correlate(warp_tiles(tile_rows, slot_shift), slot_rows, groups)
    answers = lax.all_to_all(group_terms, "depth", split_axis=0, concat_axis=0, tiled=True)
    per_request = answers[owner_of, slot_of]
    summed = per_request.reshape(PD, VIEWS, row_count, groups, col_count).sum(axis=1)
    cost = summed / (VIEWS * (feat_count // groups))
    rimmed = padded_2(cost, (("slab", 1),), 1)
    padded = jnp.pad(rimmed, ((0, 0), (0, 0), (0, 0), (1, 1)))
    windows = []
    for tap_index in range(9):
        row_step = tap_index // 3
        col_step = tap_index % 3
        windows.append(
            padded[:, row_step : row_step + row_count, :, col_step : col_step + col_count]
        )
    stacked = (
        jnp.stack(windows).transpose(0, 3, 1, 2, 4).reshape(9 * groups, PD * row_count * col_count)
    )
    gate_matrix = w_gates.astype(jnp.float32).transpose(1, 0, 2).reshape(2 * hidden, 9 * groups)
    preact = jnp.dot(
        gate_matrix, stacked, precision=lax.Precision.HIGHEST, preferred_element_type=jnp.float32
    )
    preact = preact.reshape(2 * hidden, PD, row_count, col_count)
    retain = jax.nn.sigmoid(preact[:hidden] + bias_z[:, None, None, None])
    candidate = jnp.tanh(preact[hidden:] + bias_c[:, None, None, None])
    fresh = (1.0 - retain) * candidate
    decay_all = jnp.ones((hidden, row_count, col_count), jnp.float32)
    offset_all = jnp.zeros((hidden, row_count, col_count), jnp.float32)
    for plane in range(PD):
        decay_all = retain[:, plane] * decay_all
        offset_all = retain[:, plane] * offset_all + fresh[:, plane]

    def combine(earlier, latter):
        return (latter[0] * earlier[0], latter[0] * earlier[1] + latter[1])

    prefix = prefix_2(
        (decay_all, offset_all),
        "depth",
        combine,
        (jnp.ones_like(decay_all), jnp.zeros_like(offset_all)),
    )
    current = prefix[1]
    score_list = []
    for plane in range(PD):
        current = retain[:, plane] * current + fresh[:, plane]
        score_list.append(jnp.sum(current * w_out[:, None, None], axis=0))
    scores = jnp.stack(score_list)
    plane_index = lax.axis_index("depth") * PD + jnp.arange(PD, dtype=jnp.int32)
    depth_value = 1.0 / (0.1 + 0.9 * plane_index.astype(jnp.float32) / (PD * owners - 1))
    local_max = jnp.max(scores, axis=0)
    highest = lax.pmax(local_max, "depth")
    weights = jnp.exp(scores - highest[None])
    totals, depth_sum = lax.psum(
        (jnp.sum(weights, axis=0), jnp.sum(weights * depth_value[:, None, None], axis=0)), "depth"
    )
    probability = weights / totals[None]
    return (probability, depth_sum / totals)


def solution(mesh):
    return jax.shard_map(
        body,
        mesh=mesh,
        in_specs=(
            P("slab", None, None),
            P("depth", None, None),
            P(("depth", "slab"), None),
            P(("depth", "slab")),
            P(("depth", "slab")),
            P(),
            P(),
            P(),
            P(),
        ),
        out_specs=(P("depth", "slab", None), P("slab", None)),
        check_vma=False,
    )
```

profile of v0, /device:TPU:32, one launch (start us, length us, event | category | flops | bytes accessed | tf_op | source)
XLA Modules:
  0.0 1213.0 jit_solution(11218281772155030469)
XLA Ops:
  7.2 0.8 fusion.34
  8.1 0.8 select_reduce_fusion
  9.6 4.5 scatter_fusion
  14.8 15.0 %all-to-all-start = ((s32[128,1,2]{2,1,0:T(1,128)}), s32[128,1,2]{2,1,0:T(1,128)S(1)}, u32[]{:S(2)}, u32[]{:S(2)}) async-start(s32[128,1,2]{2,1,0:T(1,128)} %copy.29), calls=%async_computation | async-start | bytes 131072 | tf_op jit(solution)/shard_map/all_to_all | solution.py:85
  29.8 4.5 scatter_fusion.1
  35.0 5.9 all-to-all-done
  41.0 7.9 all-to-all-start.1
  48.9 1.9 broadcast_in_dim.22
  50.8 5.6 scatter_fusion.2
  56.4 3.6 all-to-all-done.1
  59.9 10.2 all-to-all-start.2
  71.0 1.0 reshape.235
  72.3 2.2 gather_fusion
  74.5 0.8 iota_subtract_fusion
  75.3 47.6 %all-to-all-done.2 = bf16[128,2,32,128]{3,2,1,0:T(8,128)(2,1)S(1)} async-done(((bf16[128,2,32,128]{3,2,1,0:T(8,128)(2,1)}), bf16[128,2,32,128]{3,2,1,0:T(8,128)(2,1)S(1)}, u32[]{:S(2)}, u32[]{:S(2)}) %all-to-all-start.2) | async-done | bytes 2097184 | tf_op jit(solution)/shard_map/all_to_all | solution.py:87
  122.9 7.0 convert_multiply_fusion
  129.9 4.9 reduce_sum.85
  134.8 35.2 %all_to_all.34 = f32[128,2,8,128]{3,2,1,0:T(8,128)S(1)} all-to-all(f32[128,2,8,128]{3,2,1,0:T(8,128)S(1)} %reduce_sum.85), channel_id=1, replica_groups=mesh['depth'=128,'slab'=2] {'depth'}, dimensions={0} | all-to-all | bytes 2097152 | tf_op jit(solution)/shard_map/all_to_all | solution.py:90
  170.9 1.3 collective-permute-start
  172.2 1.3 collective-permute-start.1
  173.5 1.8 collective-permute-done.1
  177.8 109.4 %all-gather.3.cloned.1.call-done = f32[128,32,2,128]{3,1,2,0:T(8,128)} async-done(((f32[1,32,2,128]{3,1,2,0:T(8,128)}), f32[128,32,2,128]{3,1,2,0:T(8,128)}) %all-gather.3.cloned.1.call-update) | async-done | bytes 4194320 | tf_op jit(solution)/shard_map/all_gather | solution.py:29
  287.3 117.6 %all-gather.5.cloned.1.call-done = f32[128,32,2,128]{3,1,2,0:T(8,128)} async-done(((f32[1,32,2,128]{3,1,2,0:T(8,128)}), f32[128,32,2,128]{3,1,2,0:T(8,128)}) %all-gather.5.cloned.1.call-update) | async-done | bytes 4194320 | tf_op jit(solution)/shard_map/all_gather | solution.py:29
  404.9 109.9 %while.14 = (s32[]{:T(128)}, f32[32,2,128]{2,1,0:T(2,128)S(1)}, s32[]{:T(128)}, f32[128,32,2,128]{3,1,2,0:T(8,128)}, f32[128,32,2,128]{3,1,2,0:T(8,128)}, /*index=5*/s32[]{:T(128)}, s32[]{:T(128)}) while((s32[]{:T(128)}, f32[32,2,128]{2,1,0:T(2,128)S(1)}, s32[]{:T(128)}, f32[128,32,2,128]{3,1,2,0:T(8,128)}, ...), condition=%wide.region_8.9_spmd.clone, body=%wide.region_7.8_spmd.clone.sunk | while | flops 32772 | bytes 262245 | solution.py:41
  406.6 0.8 constant_dynamic-slice_fusion.3
  407.5 0.8 constant_dynamic-slice_fusion.3
  408.3 0.8 constant_dynamic-slice_fusion.3
  409.2 0.8 constant_dynamic-slice_fusion.3
  410.1 0.8 constant_dynamic-slice_fusion.3
  410.9 0.8 constant_dynamic-slice_fusion.3
  411.8 0.8 constant_dynamic-slice_fusion.3
  413.5 0.8 constant_dynamic-slice_fusion.3
  414.3 0.8 constant_dynamic-slice_fusion.3
  416.1 0.8 constant_dynamic-slice_fusion.3
  416.9 0.8 constant_dynamic-slice_fusion.3
  417.8 0.8 constant_dynamic-slice_fusion.3
  418.6 0.8 constant_dynamic-slice_fusion.3
  419.5 0.8 constant_dynamic-slice_fusion.3
  420.4 0.8 constant_dynamic-slice_fusion.3
  421.2 0.8 constant_dynamic-slice_fusion.3
  422.9 0.8 constant_dynamic-slice_fusion.3
  423.8 0.8 constant_dynamic-slice_fusion.3
  424.7 0.8 constant_dynamic-slice_fusion.3
  425.5 0.8 constant_dynamic-slice_fusion.3
  426.4 0.8 constant_dynamic-slice_fusion.3
  427.2 0.8 constant_dynamic-slice_fusion.3
  428.1 0.8 constant_dynamic-slice_fusion.3
  429.8 0.8 constant_dynamic-slice_fusion.3
  430.7 0.8 constant_dynamic-slice_fusion.3
  432.4 0.8 constant_dynamic-slice_fusion.3
  433.2 0.8 constant_dynamic-slice_fusion.3
  434.1 0.8 constant_dynamic-slice_fusion.3
  435.0 0.8 constant_dynamic-slice_fusion.3
  435.8 0.8 constant_dynamic-slice_fusion.3
  436.7 0.8 constant_dynamic-slice_fusion.3
  437.5 0.8 constant_dynamic-slice_fusion.3
  439.3 0.8 constant_dynamic-slice_fusion.3
  440.1 0.8 constant_dynamic-slice_fusion.3
  441.0 0.8 constant_dynamic-slice_fusion.3
  441.8 0.8 constant_dynamic-slice_fusion.3
  442.7 0.8 constant_dynamic-slice_fusion.3
  443.6 0.8 constant_dynamic-slice_fusion.3
  515.0 343.5 %pmax.7 = f32[2,128]{1,0:T(2,128)S(1)} all-reduce(f32[2,128]{1,0:T(2,128)S(1)} %maximum_maximum_fusion), channel_id=1, replica_groups=mesh['depth'=128,'slab'=2] {'depth'}, use_global_device_ids=true, to_apply=%region_13.14 | all-reduce | flops 256 | bytes 2048 | tf_op jit(solution)/shard_map/pmax | solution.py:138
  858.6 346.4 %all-reduce.1 = (f32[2,128]{1,0:T(2,128)S(1)}, f32[2,128]{1,0:T(2,128)S(1)}) all-reduce(f32[2,128]{1,0:T(2,128)S(1)} %get-tuple-element.130, f32[2,128]{1,0:T(2,128)S(1)} %get-tuple-element.129), channel_id=1, replica_groups=mesh['depth'=128,'slab'=2] {'depth'}, use_global_device_ids=true, to_apply=%region_15.16 | all-reduce | flops 512 | bytes 4096 | tf_op jit(solution)/shard_map/psum | solution.py:140
  (276 shorter events, 86.6 us)
Async XLA Ops:
  7.2 65.1 %copy-start = (bf16[160,32,128]{2,1,0:T(8,128)(2,1)S(1)}, bf16[160,32,128]{2,1,0:T(8,128)(2,1)}, u32[]{:S(2)}) copy-start(bf16[160,32,128]{2,1,0:T(8,128)(2,1)} %param.12) | copy-start | bytes 3932164
  7.2 41.7 %copy-start.2 = (bf16[2,32,128]{2,1,0:T(8,128)(2,1)S(1)}, bf16[2,32,128]{2,1,0:T(8,128)(2,1)}, u32[]{:S(2)}) copy-start(bf16[2,32,128]{2,1,0:T(8,128)(2,1)} %param.11) | copy-start | bytes 49156
  14.8 26.2 %all-to-all-start = ((s32[128,1,2]{2,1,0:T(1,128)}), s32[128,1,2]{2,1,0:T(1,128)S(1)}, u32[]{:S(2)}, u32[]{:S(2)}) async-start(s32[128,1,2]{2,1,0:T(1,128)} %copy.29), calls=%async_computation | async-start | bytes 131072 | tf_op jit(solution)/shard_map/all_to_all | solution.py:85
  41.0 19.0 %all-to-all-start.1 = ((s32[128,1,2]{2,1,0:T(1,128)}), s32[128,1,2]{2,1,0:T(1,128)S(1)}, u32[]{:S(2)}, u32[]{:S(2)}) async-start(s32[128,1,2]{2,1,0:T(1,128)} %copy.32), calls=%async_computation.1 | async-start | bytes 131072 | tf_op jit(solution)/shard_map/all_to_all | solution.py:86
  59.9 62.9 %all-to-all-start.2 = ((bf16[128,2,32,128]{3,2,1,0:T(8,128)(2,1)}), bf16[128,2,32,128]{3,2,1,0:T(8,128)(2,1)S(1)}, u32[]{:S(2)}, u32[]{:S(2)}) async-start(bf16[128,2,32,128]{3,2,1,0:T(8,128)(2,1)} %scatter_fusion.2), calls=%async_computation.2 | async-start | bytes 4194304 | tf_op jit(solution)/shard_map/all_to_all | solution.py:87
  70.2 217.1 %all-gather.3.cloned.1.call-start = ((), (), s32[]{:S(2)}) async-start(), calls=%async_computation.4 | async-start | bytes 4227072 | tf_op jit(solution)/shard_map/all_gather | solution.py:29
  134.8 40.8 %copy-start.1 = (bf16[9,64,8]{1,2,0:T(8,128)(2,1)S(1)}, bf16[9,64,8]{1,2,0:T(8,128)(2,1)}, u32[]{:S(2)}) copy-start(bf16[9,64,8]{1,2,0:T(8,128)(2,1)} %param.16) | copy-start | bytes 27652
  134.8 41.4 %copy-start.4 = (f32[32]{0:T(128)S(1)}, f32[32]{0:T(128)}, u32[]{:S(2)}) copy-start(f32[32]{0:T(128)} %param.18) | copy-start | bytes 388
  134.8 41.4 %copy-start.5 = (f32[32]{0:T(128)S(1)}, f32[32]{0:T(128)}, u32[]{:S(2)}) copy-start(f32[32]{0:T(128)} %param.17) | copy-start | bytes 388
  170.9 2.6 collective-permute-start
  172.2 3.1 collective-permute-start.1
  175.6 339.2 %copy-start.3 = (f32[32]{0:T(128)S(1)}, f32[32]{0:T(128)}, u32[]{:S(2)}) copy-start(f32[32]{0:T(128)} %param.19) | copy-start | bytes 388
  177.1 227.8 %all-gather.5.cloned.1.call-start = ((), (), s32[]{:S(2)}) async-start(), calls=%async_computation.5 | async-start | bytes 4227072 | tf_op jit(solution)/shard_map/all_gather | solution.py:29
Sparse Core Ops, SparseCore 0:
  177.2 110.0 all-gather.2
  290.9 113.9 all-gather.4
where the time goes:
time: 1220 us; the launch traced here: 1210 us
  blocking collectives  725 us (59%)
  waiting for transfers between devices  287 us (24%)
  local copies, waits for them, and re-layouts  123 us (10%)
  starting transfers between devices  36 us (3%)
  other arithmetic  19.1 us (2%)
  between operations  14.4 us (1%)
    psum x1, blocking collectives, body(): lax.psum((jnp.sum(weights, axis=0), jnp.sum(weights * depth_value[:, None...  346 us
    pmax x1, blocking collectives, body(): highest = lax.pmax(local_max, 'depth')  344 us
    all_gather x2, waiting for transfers between devices, prefix_2(): everything = jax.tree.map(lambda part: lax.all_gather(part, axis), shard)  227 us
    dynamic_slice x128, local copies, waits for them, and re-layouts, turn(): new = combine(before, jax.tree.map(lambda part: part[k], everything))  100 us
    all_to_all x1, waiting for transfers between devices, body(): lax.all_to_all(send_rows, 'depth', split_axis=0, concat_axis=0, tiled=True)  47.6 us
    all_to_all x1, blocking collectives, body(): lax.all_to_all(group_terms, 'depth', split_axis=0, concat_axis=0, tiled=T...  35.2 us
  transfers between devices with their start and end apart: 7, of which 6 were waited for; matrix products, arithmetic and copies ran while one was open for 1% of the time, Pallas kernels for 0%

commit v1 on v0

v1 whole, which is shorter than its diff:
```python
import jax
import jax.numpy as jnp
from jax import lax
from jax.experimental import pallas as pl
from jax.experimental.pallas import tpu as pltpu
from jax.sharding import PartitionSpec as P

VIEWS = 5
PD = 4
MAXSHIFT = 16
F32 = jnp.float32
BF16 = jnp.bfloat16
VMEM_LIMIT = 40 * 1024 * 1024


def params():
    return pltpu.CompilerParams(vmem_limit_bytes=VMEM_LIMIT)


def vspec():
    return pl.BlockSpec(memory_space=pltpu.VMEM)


def sspec():
    return pl.BlockSpec(memory_space=pltpu.SMEM)


def prepare_kernel(ref_ref, src_ref, tab_ref, srce_ref, ref32, src32):
    rows, feat, cols = ref_ref.shape
    tiles = src_ref.shape[0]
    cpg = feat // 8
    for r in range(rows):
        ref32[pl.ds(r * feat, feat), :] = ref_ref[r].astype(F32)
    lane = lax.broadcasted_iota(jnp.int32, (8, cols), 1)
    for r in range(rows):
        for e in range(cpg):
            base = ref32[pl.ds(r * feat + e, 8, stride=cpg), :]
            for k in range(2 * MAXSHIFT + 1):
                shift = k - MAXSHIFT
                moved = base if shift == 0 else pltpu.roll(base, (-shift) % cols, 1)
                inside = (lane + shift >= 0) & (lane + shift < cols)
                tab_ref[r * (2 * MAXSHIFT + 1) + k, pl.ds(e * 8, 8), :] = jnp.where(inside, moved, 0.0)

    def widen(n, c):
        src32[pl.ds(n * feat, feat), :] = src_ref[n].astype(F32)
        return c

    lax.fori_loop(0, tiles, widen, 0, unroll=8)

    def reorder(n, c):
        parts = [src32[pl.ds(n * feat + e, 8, stride=cpg), :] for e in range(cpg)]
        srce_ref[n] = jnp.concatenate(parts, axis=0).astype(BF16)
        return c

    lax.fori_loop(0, tiles, reorder, 0, unroll=8)


def answer_kernel(requests, req_ref, tab_ref, srce_ref, out_ref, codes, table, sem):
    owners = req_ref.shape[0]
    cols = out_ref.shape[-1]
    me = lax.axis_index("depth")
    flat = req_ref[...].T
    owner = flat[0:requests]
    local = flat[requests : 2 * requests]
    shift = flat[2 * requests : 3 * requests]
    q = lax.broadcasted_iota(jnp.int32, (requests, owners), 0)
    hit = owner == me
    first = jnp.min(jnp.where(hit, q, requests), axis=0, keepdims=True)
    last = jnp.max(jnp.where(hit, q, -1), axis=0, keepdims=True)
    value = local + (shift + MAXSHIFT) * 256 + (q % 2) * 16384
    zero = jnp.zeros_like(value)
    code0 = jnp.sum(jnp.where(hit & (q == first), value, zero), axis=0, keepdims=True)
    code1 = jnp.sum(jnp.where(hit & (q == last) & (q > first), value, zero), axis=0, keepdims=True)
    sub = lax.broadcasted_iota(jnp.int32, (8, owners), 0)
    codes[...] = jnp.where(sub == 0, code0, jnp.where(sub == 1, code1, 0))
    copy = pltpu.make_async_copy(codes, table, sem)
    copy.start()
    copy.wait()

    def one(i, s):
        code = table[s, i]
        loc = code & 255
        moved = (code >> 8) & 63
        row = code >> 14
        tile = srce_ref[loc].astype(F32) * tab_ref[row * (2 * MAXSHIFT + 1) + moved]
        total = (tile[0:8] + tile[8:16]) + (tile[16:24] + tile[24:32])
        out_ref[i * 2 + s] = pltpu.roll(total, (moved + cols - MAXSHIFT) % cols, 1)

    def step(i, c):
        one(i, 0)
        one(i, 1)
        return c

    lax.fori_loop(0, owners, step, 0, unroll=8)


def cost_kernel(idx_ref, ans_ref, out_ref):
    cols = ans_ref.shape[-1]
    lane = lax.broadcasted_iota(jnp.int32, (8, cols), 1)
    for h in range(2):
        rows = []
        for pp in range(2):
            for r in range(2):
                acc = None
                for v in range(VIEWS):
                    part = ans_ref[idx_ref[(2 * h + pp) * 2 * VIEWS + v * 2 + r]]
                    acc = part if acc is None else acc + part
                c = acc / (VIEWS * 4.0)
                rows.append(jnp.where(lane == 0, 0.0, pltpu.roll(c, 1, 1)))
                rows.append(c)
                rows.append(jnp.where(lane == cols - 1, 0.0, pltpu.roll(c, cols - 1, 1)))
        rows.append(jnp.zeros((32, cols), F32))
        block = jnp.concatenate(rows, axis=0).T
        out_ref[pl.ds(h, cols, stride=4), :] = block
        out_ref[pl.ds(2 + h, cols, stride=4), :] = block


def column_kernel(x_ref, w_ref, bias_ref, wo_ref, out_ref, d_s, o_s, hb_s, dp_s, op_s):
    n = x_ref.shape[0] // 4
    tops = []
    for h in range(2):
        tops.append(
            jnp.concatenate(
                [x_ref[pl.ds(h, n, stride=4), :], x_ref[pl.ds(2 + h, n, stride=4), :]], axis=1
            )
        )
    x = jnp.concatenate(tops, axis=0)
    w = w_ref[...]
    hi = x.astype(BF16)
    rest = x - hi.astype(F32)
    mid = rest.astype(BF16)
    low = (rest - mid.astype(F32)).astype(BF16)
    y = jnp.dot(low, w, preferred_element_type=F32)
    y = y + jnp.dot(mid, w, preferred_element_type=F32)
    y = y + jnp.dot(hi, w, preferred_element_type=F32)
    z = y[:, :128] + bias_ref[0:1, :]
    cand = jnp.tanh(y[:, 128:] + bias_ref[1:2, :])
    small = jnp.exp(-jnp.abs(z))
    big = 1.0 / (1.0 + small)
    small = small * big
    up = z >= 0
    retain = jnp.where(up, big, small)
    fresh = jnp.where(up, small, big) * cand
    lane = lax.broadcasted_iota(jnp.int32, (2 * n, 128), 1)
    low_half = lane < 64
    other_r = pltpu.roll(retain, 64, 1)
    other_f = pltpu.roll(fresh, 64, 1)
    pair_d = retain * other_r
    pair_o = jnp.where(low_half, other_r * fresh + other_f, retain * other_f + fresh)
    d_s[...] = pair_d
    o_s[...] = pair_o
    per = n // 8
    dc = jnp.ones((8, 128), F32)
    oc = jnp.zeros((8, 128), F32)
    for ii in range(per):
        for h in range(2):
            step = ii * 2 + h
            d = d_s[pl.ds(h * n + ii, 8, stride=per), :]
            o = o_s[pl.ds(h * n + ii, 8, stride=per), :]
            dp_s[step] = dc
            op_s[step] = oc
            oc = d * oc + o
            dc = d * dc
    sub = lax.broadcasted_iota(jnp.int32, (8, 128), 0)
    start = jnp.zeros((8, 128), F32)
    for _ in range(7):
        start = jnp.where(sub == 0, 0.0, pltpu.roll(dc * start + oc, 1, 0))
    for ii in range(per):
        for h in range(2):
            step = ii * 2 + h
            hb_s[pl.ds(h * n + ii, 8, stride=per), :] = dp_s[step] * start + op_s[step]
    hb = hb_s[...]
    state = jnp.where(low_half, retain, pair_d) * hb + jnp.where(low_half, fresh, pair_o)
    wide = jnp.concatenate([state[:n], state[n:]], axis=1)
    s = jnp.dot(wide, wo_ref[...], precision=lax.Precision.HIGHEST, preferred_element_type=F32)

    def over(op, v):
        v = jnp.broadcast_to(v, (8, 128))
        v = op(v, pltpu.roll(v, 2, 1))
        return op(v, pltpu.roll(v, 4, 1))[0:1]

    row = lax.broadcasted_iota(jnp.int32, (n, 128), 0)
    col = lax.broadcasted_iota(jnp.int32, (n, 128), 1)
    plane = row * PD + (col % 8) // 2
    value = 1.0 / (0.1 + 0.9 * plane.astype(F32) / (PD * n - 1))
    highest = over(jnp.maximum, jnp.max(s, axis=0, keepdims=True))
    weights = jnp.exp(s - highest)
    total = over(jnp.add, jnp.sum(weights, axis=0, keepdims=True))
    depth = over(jnp.add, jnp.sum(weights * value, axis=0, keepdims=True))
    out_ref[...] = jnp.where(col < 8, weights / total, depth / total)


def output_kernel(x_ref, prob_ref, map_ref):
    t = x_ref[...].T
    for p in range(PD):
        prob_ref[p] = t[p * 2 : p * 2 + 2]
    map_ref[...] = t[8:10]


def gate_matrix(w_gates, slab):
    w = w_gates.reshape(3, 3, 2, 32, 8).transpose(0, 1, 4, 2, 3)
    w = jnp.pad(w, ((2, 2), (0, 0), (0, 0), (0, 0), (0, 0)))
    by_row = [
        lax.dynamic_slice_in_dim(w, 3 - r - 2 * slab, 4, axis=0) for r in range(2)
    ]
    v = jnp.stack(by_row, axis=4).reshape(2, 2, 3, 8, 2, 2, 32)
    same = jnp.eye(2, dtype=w.dtype)
    full = v[:, None, :, :, :, :, None] * same[None, :, None, None, None, None, :, None, None]
    full = full.reshape(2, 96, 256)
    return jnp.pad(full, ((0, 0), (0, 32), (0, 0))).reshape(256, 256)


def body(ref_feat, src_feat, tile_owner, tile_local, col_shift, w_gates, bias_z, bias_c, w_out):
    owners = lax.axis_size("depth")
    row_count, feat, cols = ref_feat.shape
    requests = tile_local.shape[0]
    tiles = src_feat.shape[0]
    owner = tile_owner[:, 0]
    message = jnp.concatenate(
        [owner, tile_local, col_shift, jnp.zeros((128 - 3 * requests,), jnp.int32)]
    )
    message = jnp.broadcast_to(message[None, None, :], (owners, 1, 128))
    asked = lax.all_to_all(message, "depth", split_axis=0, concat_axis=0, tiled=True)

    table, channels = pl.pallas_call(
        prepare_kernel,
        out_shape=(
            jax.ShapeDtypeStruct((row_count * (2 * MAXSHIFT + 1), feat, cols), F32),
            jax.ShapeDtypeStruct((tiles, feat, cols), BF16),
        ),
        in_specs=[vspec(), vspec()],
        out_specs=(vspec(), vspec()),
        scratch_shapes=[
            pltpu.VMEM((row_count * feat, cols), F32),
            pltpu.VMEM((tiles * feat, cols), F32),
        ],
        compiler_params=params(),
        cost_estimate=pl.CostEstimate(flops=2000000, transcendentals=0, bytes_accessed=4000000),
        name="prepare",
    )(ref_feat, src_feat)

    def answers_of(*refs):
        answer_kernel(requests, *refs)

    answers = pl.pallas_call(
        answers_of,
        out_shape=jax.ShapeDtypeStruct((owners * 2, 8, cols), F32),
        in_specs=[vspec(), vspec(), vspec()],
        out_specs=vspec(),
        scratch_shapes=[
            pltpu.VMEM((8, owners), jnp.int32),
            pltpu.SMEM((8, owners), jnp.int32),
            pltpu.SemaphoreType.DMA,
        ],
        compiler_params=params(),
        name="answer",
    )(asked.reshape(owners, 128), table, channels)
    answers = lax.all_to_all(
        answers.reshape(owners, 16, cols), "depth", split_axis=0, concat_axis=0, tiled=True
    )

    q = jnp.arange(requests, dtype=jnp.int32)
    earlier = (owner[:, None] == owner[None, :]) & (q[None, :] < q[:, None])
    index = owner * 2 + jnp.any(earlier, axis=1).astype(jnp.int32)
    costs = pl.pallas_call(
        cost_kernel,
        out_shape=jax.ShapeDtypeStruct((cols * 4, 128), F32),
        in_specs=[sspec(), vspec()],
        out_specs=vspec(),
        compiler_params=params(),
        name="cost",
    )(index, answers.reshape(owners * 2, 8, cols))
    costs = lax.all_to_all(
        costs.reshape(cols * 2, 2, 128), ("depth", "slab"), split_axis=0, concat_axis=0, tiled=True
    )

    slab = lax.axis_index("slab")
    gates = gate_matrix(w_gates, slab)
    bias = jnp.stack([jnp.tile(bias_z, 4), jnp.tile(bias_c, 4)])
    unit_row = jnp.arange(256, dtype=jnp.int32)[:, None] // 32
    score_col = jnp.arange(128, dtype=jnp.int32)[None, :] % 8
    project = jnp.where(unit_row == score_col, jnp.tile(w_out, 8)[:, None], 0.0)
    packed = pl.pallas_call(
        column_kernel,
        out_shape=jax.ShapeDtypeStruct((owners, 128), F32),
        in_specs=[vspec()] * 4,
        out_specs=vspec(),
        scratch_shapes=[
            pltpu.VMEM((2 * owners, 128), F32),
            pltpu.VMEM((2 * owners, 128), F32),
            pltpu.VMEM((2 * owners, 128), F32),
            pltpu.VMEM((owners // 4, 8, 128), F32),
            pltpu.VMEM((owners // 4, 8, 128), F32),
        ],
        compiler_params=params(),
        name="column",
    )(costs.reshape(cols * 4, 128), gates, bias, project)
    packed = lax.all_to_all(
        packed.reshape(owners, 1, 128), "depth", split_axis=0, concat_axis=0, tiled=True
    )
    return pl.pallas_call(
        output_kernel,
        out_shape=(
            jax.ShapeDtypeStruct((PD, row_count, cols), F32),
            jax.ShapeDtypeStruct((row_count, cols), F32),
        ),
        in_specs=[vspec()],
        out_specs=(vspec(), vspec()),
        compiler_params=params(),
        name="output",
    )(packed.reshape(cols, 128))


def solution(mesh):
    return jax.shard_map(
        body,
        mesh=mesh,
        in_specs=(
            P("slab", None, None),
            P("depth", None, None),
            P(("depth", "slab"), None),
            P(("depth", "slab")),
            P(("depth", "slab")),
            P(),
            P(),
            P(),
            P(),
        ),
        out_specs=(P("depth", "slab", None), P("slab", None)),
        check_vma=False,
    )
```

time: 1220 us -> 113 us (0.09)
  blocking collectives: 725 us -> 16.9 us
  waiting for transfers between devices: 287 us -> 52 us
  local copies, waits for them, and re-layouts: 123 us -> 4.16 us
  other arithmetic: 19.1 us -> 1.15 us
  between operations: 14.4 us -> 0.89 us
    psum x1 -> x0, blocking collectives: 346 us -> none  [body(): lax.psum((jnp.sum(weights, axis=0), jnp.sum(weights * depth_value[:, None...]
    pmax x1 -> x0, blocking collectives: 344 us -> none  [body(): highest = lax.pmax(local_max, 'depth')]
    all_gather x2 -> x0, waiting for transfers between devices: 227 us -> none  [prefix_2(): everything = jax.tree.map(lambda part: lax.all_gather(part, axis), shard)]
    dynamic_slice x128 -> x3, local copies, waits for them, and re-layouts: 100 us -> 0.17 us  [gate_matrix(): lax.dynamic_slice_in_dim(w, 3 - r - 2 * slab, 4, axis=0)]
    all_to_all x1, blocking collectives: 35.2 us -> 16.9 us  [body(): lax.all_to_all(packed.reshape(owners, 1, 128), 'depth', split_axis=0, con...]
    scatter x3 -> x0, local copies, waits for them, and re-layouts: 14.5 us -> none  [the longest x1 5.57 us: body(): send_rows = jnp.zeros((owners, capacity, feat_count, col_count), jnp.bflo...]
  transfers between devices with their start and end apart: 7 -> 3, of which waited for: 6 -> 3; matrix products, arithmetic and copies ran while one was open for 1% -> 2% of each run, Pallas kernels for 0% -> 1%
where the time goes in v1:
time: 113 us; the launch traced here: 112 us
  waiting for transfers between devices  52 us (46%)
  starting transfers between devices  28.3 us (25%)
  blocking collectives  16.9 us (15%)
  Pallas kernels  8.26 us (7%)
  local copies, waits for them, and re-layouts  4.16 us (4%)
  other arithmetic  1.15 us (1%)
    all_to_all x1, waiting for transfers between devices, body(): lax.all_to_all(answers.reshape(owners, 16, cols), 'depth', split_axis=0,...  28.5 us
    all_to_all x1, blocking collectives, body(): lax.all_to_all(packed.reshape(owners, 1, 128), 'depth', split_axis=0, con...  16.9 us
    all_to_all x1, waiting for transfers between devices, body(): lax.all_to_all(costs.reshape(cols * 2, 2, 128), ('depth', 'slab'), split_...  15.1 us
    all_to_all x1, starting transfers between devices, body(): lax.all_to_all(message, 'depth', split_axis=0, concat_axis=0, tiled=True)  15 us
    all_to_all x1, waiting for transfers between devices, body(): lax.all_to_all(message, 'depth', split_axis=0, concat_axis=0, tiled=True)  8.45 us
    all_to_all x1, starting transfers between devices, body(): lax.all_to_all(costs.reshape(cols * 2, 2, 128), ('depth', 'slab'), split_...  6.68 us
    all_to_all x1, starting transfers between devices, body(): lax.all_to_all(answers.reshape(owners, 16, cols), 'depth', split_axis=0,...  6.65 us
    pallas_call x1, Pallas kernels, body(): pl.pallas_call(answers_of, out_shape=jax.ShapeDtypeStruct((owners * 2, 8,...  4.24 us
  transfers between devices with their start and end apart: 3, of which 3 were waited for; matrix products, arithmetic and copies ran while one was open for 2% of the time, Pallas kernels for 1%

profile of v1, /device:TPU:32, one launch (start us, length us, event | category | flops | bytes accessed | tf_op | source)
XLA Modules:
  0.0 111.8 jit_solution(3985120371268251905)
XLA Ops:
  0.6 0.8 pad_add_fusion
  1.4 0.7 broadcast_in_dim.12
  2.1 15.0 %all-to-all-start = ((s32[128,1,128]{2,1,0:T(1,128)}), s32[128,1,128]{2,1,0:T(1,128)S(1)}, u32[]{:S(2)}, u32[]{:S(2)}) async-start(s32[128,1,128]{2,1,0:T(1,128)} %broadcast_in_dim.12), calls=%async_computation | async-start | bytes 131072 | tf_op jit(solution)/shard_map/all_to_all | solution.py:223
  17.1 0.0 copy-start
  17.1 1.3 %copy-done = bf16[160,32,128]{2,1,0:T(8,128)(2,1)S(1)} copy-done((bf16[160,32,128]{2,1,0:T(8,128)(2,1)S(1)}, bf16[160,32,128]{2,1,0:T(8,128)(2,1)}, u32[]{:S(2)}) %copy-start) | copy-done | bytes 1310744
  18.4 0.0 copy-start.1
  18.4 0.7 copy-done.1
  19.1 0.6 prepare.1
  19.8 8.4 %all-to-all-done = s32[128,1,128]{2,1,0:T(1,128)S(1)} async-done(((s32[128,1,128]{2,1,0:T(1,128)}), s32[128,1,128]{2,1,0:T(1,128)S(1)}, u32[]{:S(2)}, u32[]{:S(2)}) %all-to-all-start) | async-done | bytes 65568 | tf_op jit(solution)/shard_map/all_to_all | solution.py:223
  28.2 4.2 %answer.1 = f32[256,8,128]{2,1,0:T(8,128)} custom-call(s32[128,128]{1,0:T(8,128)S(1)} %bitcast.22, f32[66,32,128]{2,1,0:T(8,128)S(1)} %get-tuple-element.4.refs_1_, bf16[160,32,128]{2,1,0:T(8,128)(2,1)S(1)} %get-tuple-element.5.refs_2_), custom_call_target="tpu_custom_call" | custom-call | tf_op jit(solution)/shard_map/answer/pallas_call | solution.py:245
  32.5 0.0 copy-start.2
  32.5 6.7 %all-to-all-start.1 = ((f32[128,16,128]{2,1,0:T(8,128)}), f32[128,16,128]{2,1,0:T(8,128)S(1)}, u32[]{:S(2)}, u32[]{:S(2)}) async-start(f32[128,16,128]{2,1,0:T(8,128)} %bitcast.2), calls=%async_computation.1 | async-start | bytes 2097152 | tf_op jit(solution)/shard_map/all_to_all | solution.py:258
  39.2 0.0 copy-start.3
  39.2 0.0 copy-start.4
  39.2 0.0 copy-start.5
  39.2 0.0 copy-done.2
  39.2 0.1 reshape.111
  39.3 0.0 copy-start.6
  39.3 0.2 pad_dynamic-slice_fusion.1
  39.5 0.1 copy.21
  39.6 0.2 mul.36
  39.9 0.3 mul.37
  40.2 0.2 mul.38
  40.3 0.1 mul.39
  40.5 0.0 copy-done.3
  40.5 0.1 stack_tile.7
  40.6 0.0 copy-done.4
  40.6 0.1 stack_tile.6
  40.7 0.0 copy-done.5
  40.7 0.1 broadcast_in_dim.26
  40.8 0.0 copy-done.6
  40.8 0.2 fusion.1
  41.0 28.5 %all-to-all-done.1 = f32[128,16,128]{2,1,0:T(8,128)S(1)} async-done(((f32[128,16,128]{2,1,0:T(8,128)}), f32[128,16,128]{2,1,0:T(8,128)S(1)}, u32[]{:S(2)}, u32[]{:S(2)}) %all-to-all-start.1) | async-done | bytes 1048608 | tf_op jit(solution)/shard_map/all_to_all | solution.py:258
  69.5 1.4 %cost.1 = f32[512,128]{1,0:T(8,128)} custom-call(s32[40]{0:T(128)S(1)} %convert_add_fusion.idx_ref, f32[256,8,128]{2,1,0:T(8,128)S(1)} %bitcast.19), custom_call_target="tpu_custom_call" | custom-call | tf_op jit(solution)/shard_map/cost/pallas_call | solution.py:265
  70.9 6.7 %all-to-all-start.2 = ((f32[256,2,128]{2,1,0:T(2,128)}), f32[256,2,128]{2,1,0:T(2,128)S(1)}, u32[]{:S(2)}, u32[]{:S(2)}) async-start(f32[256,2,128]{2,1,0:T(2,128)} %bitcast.4), calls=%async_computation.2 | async-start | bytes 524288 | tf_op jit(solution)/shard_map/all_to_all | solution.py:273
  77.6 0.1 compare_select_fusion.wo_ref
  77.8 15.1 %all-to-all-done.2 = f32[256,2,128]{2,1,0:T(2,128)S(1)} async-done(((f32[256,2,128]{2,1,0:T(2,128)}), f32[256,2,128]{2,1,0:T(2,128)S(1)}, u32[]{:S(2)}, u32[]{:S(2)}) %all-to-all-start.2) | async-done | bytes 262176 | tf_op jit(solution)/shard_map/all_to_all | solution.py:273
  92.9 1.3 %column.1 = f32[128,128]{1,0:T(8,128)S(1)} custom-call(f32[512,128]{1,0:T(8,128)S(1)} %bitcast.20, bf16[256,256]{1,0:T(8,128)(2,1)S(1)} %bitcast.21, f32[2,128]{1,0:T(2,128)S(1)} %pad_maximum_fusion.bias_ref, f32[256,128]{1,0:T(8,128)S(1)} %compare_select_fusion.wo_ref), custom_call_target="tpu_custom_call" | custom-call | tf_op jit(solution)/shard_map/column/pallas_call | solution.py:283
  94.2 16.9 %all_to_all.20 = f32[128,1,128]{2,1,0:T(1,128)S(1)} all-to-all(f32[128,1,128]{2,1,0:T(1,128)S(1)} %bitcast.23), channel_id=1, replica_groups=mesh['depth'=128,'slab'=2] {'depth'}, dimensions={0} | all-to-all | bytes 131072 | tf_op jit(solution)/shard_map/all_to_all | solution.py:298
  111.1 0.7 output.1
  (14 shorter events, 0.1 us)
Async XLA Ops:
  2.1 26.2 %all-to-all-start = ((s32[128,1,128]{2,1,0:T(1,128)}), s32[128,1,128]{2,1,0:T(1,128)S(1)}, u32[]{:S(2)}, u32[]{:S(2)}) async-start(s32[128,1,128]{2,1,0:T(1,128)} %broadcast_in_dim.12), calls=%async_computation | async-start | bytes 131072 | tf_op jit(solution)/shard_map/all_to_all | solution.py:223
  17.1 1.3 %copy-start = (bf16[160,32,128]{2,1,0:T(8,128)(2,1)S(1)}, bf16[160,32,128]{2,1,0:T(8,128)(2,1)}, u32[]{:S(2)}) copy-start(bf16[160,32,128]{2,1,0:T(8,128)(2,1)} %src_ref.1) | copy-start | bytes 3932164
  18.4 0.7 copy-start.1
  32.5 6.7 %copy-start.2 = (bf16[9,64,8]{1,2,0:T(8,128)(2,1)S(1)}, bf16[9,64,8]{1,2,0:T(8,128)(2,1)}, u32[]{:S(2)}) copy-start(bf16[9,64,8]{1,2,0:T(8,128)(2,1)} %param.14) | copy-start | bytes 27652
  32.5 37.0 %all-to-all-start.1 = ((f32[128,16,128]{2,1,0:T(8,128)}), f32[128,16,128]{2,1,0:T(8,128)S(1)}, u32[]{:S(2)}, u32[]{:S(2)}) async-start(f32[128,16,128]{2,1,0:T(8,128)} %bitcast.2), calls=%async_computation.1 | async-start | bytes 2097152 | tf_op jit(solution)/shard_map/all_to_all | solution.py:258
  39.2 1.3 %copy-start.3 = (f32[32]{0:T(128)S(1)}, f32[32]{0:T(128)}, u32[]{:S(2)}) copy-start(f32[32]{0:T(128)} %param.16) | copy-start | bytes 388
  39.2 1.4 %copy-start.4 = (f32[32]{0:T(128)S(1)}, f32[32]{0:T(128)}, u32[]{:S(2)}) copy-start(f32[32]{0:T(128)} %param.15) | copy-start | bytes 388
  39.2 1.5 %copy-start.5 = (f32[32]{0:T(128)S(1)}, f32[32]{0:T(128)}, u32[]{:S(2)}) copy-start(f32[32]{0:T(128)} %param.17) | copy-start | bytes 388
  39.3 1.5 %copy-start.6 = (s32[40,1]{0,1:T(1,128)S(1)}, s32[40,1]{0,1:T(1,128)}, u32[]{:S(2)}) copy-start(s32[40,1]{0,1:T(1,128)} %param.11) | copy-start | bytes 484
  70.9 22.0 %all-to-all-start.2 = ((f32[256,2,128]{2,1,0:T(2,128)}), f32[256,2,128]{2,1,0:T(2,128)S(1)}, u32[]{:S(2)}, u32[]{:S(2)}) async-start(f32[256,2,128]{2,1,0:T(2,128)} %bitcast.4), calls=%async_computation.2 | async-start | bytes 524288 | tf_op jit(solution)/shard_map/all_to_all | solution.py:273

commit v2 on v1

v2 whole, which is shorter than its diff:
```python
import jax
import jax.numpy as jnp
from jax import lax
from jax.experimental import pallas as pl
from jax.experimental.pallas import tpu as pltpu
from jax.sharding import PartitionSpec as P

VIEWS = 5
PD = 4
MAXSHIFT = 16
F32 = jnp.float32
BF16 = jnp.bfloat16
VMEM_LIMIT = 40 * 1024 * 1024


def params():
    return pltpu.CompilerParams(vmem_limit_bytes=VMEM_LIMIT)


def vspec():
    return pl.BlockSpec(memory_space=pltpu.VMEM)


def sspec():
    return pl.BlockSpec(memory_space=pltpu.SMEM)


def prepare_kernel(ref_ref, src_ref, tab_ref, srce_ref, ref32, src32):
    rows, feat, cols = ref_ref.shape
    tiles = src_ref.shape[0]
    cpg = feat // 8
    for r in range(rows):
        ref32[pl.ds(r * feat, feat), :] = ref_ref[r].astype(F32)
    lane = lax.broadcasted_iota(jnp.int32, (8, cols), 1)
    for r in range(rows):
        for e in range(cpg):
            base = ref32[pl.ds(r * feat + e, 8, stride=cpg), :]
            for k in range(2 * MAXSHIFT + 1):
                shift = k - MAXSHIFT
                moved = base if shift == 0 else pltpu.roll(base, (-shift) % cols, 1)
                inside = (lane + shift >= 0) & (lane + shift < cols)
                tab_ref[r * (2 * MAXSHIFT + 1) + k, pl.ds(e * 8, 8), :] = jnp.where(inside, moved, 0.0)

    def widen(n, c):
        src32[pl.ds(n * feat, feat), :] = src_ref[n].astype(F32)
        return c

    lax.fori_loop(0, tiles, widen, 0, unroll=8)

    def reorder(n, c):
        parts = [src32[pl.ds(n * feat + e, 8, stride=cpg), :] for e in range(cpg)]
        srce_ref[n] = jnp.concatenate(parts, axis=0).astype(BF16)
        return c

    lax.fori_loop(0, tiles, reorder, 0, unroll=8)


def answer_kernel(requests, req_ref, tab_ref, srce_ref, out_ref, codes, table, sem):
    owners = req_ref.shape[0]
    cols = out_ref.shape[-1]
    me = lax.axis_index("depth")
    flat = req_ref[...].T
    owner = flat[0:requests]
    local = flat[requests : 2 * requests]
    shift = flat[2 * requests : 3 * requests]
    q = lax.broadcasted_iota(jnp.int32, (requests, owners), 0)
    hit = owner == me
    first = jnp.min(jnp.where(hit, q, requests), axis=0, keepdims=True)
    last = jnp.max(jnp.where(hit, q, -1), axis=0, keepdims=True)
    value = local + (shift + MAXSHIFT) * 256 + (q % 2) * 16384
    zero = jnp.zeros_like(value)
    code0 = jnp.sum(jnp.where(hit & (q == first), value, zero), axis=0, keepdims=True)
    code1 = jnp.sum(jnp.where(hit & (q == last) & (q > first), value, zero), axis=0, keepdims=True)
    sub = lax.broadcasted_iota(jnp.int32, (8, owners), 0)
    codes[...] = jnp.where(sub == 0, code0, jnp.where(sub == 1, code1, 0))
    copy = pltpu.make_async_copy(codes, table, sem)
    copy.start()
    copy.wait()

    def one(i, s):
        code = table[s, i]
        loc = code & 255
        moved = (code >> 8) & 63
        row = code >> 14
        tile = srce_ref[loc].astype(F32) * tab_ref[row * (2 * MAXSHIFT + 1) + moved]
        total = (tile[0:8] + tile[8:16]) + (tile[16:24] + tile[24:32])
        return pltpu.roll(total, (moved + cols - MAXSHIFT) % cols, 1)

    def step(b, c):
        parts = []
        for il in range(8):
            for s in range(2):
                parts.append(one(b * 8 + il, s))
        block = jnp.concatenate(parts, axis=0).T
        out_ref[pl.ds(b, cols, stride=owners // 8), :] = block
        return c

    lax.fori_loop(0, owners // 8, step, 0, unroll=2)


def table_kernel(requests, req_ref, wd_ref, target_ref, gate_ref, keys):
    owners = req_ref.shape[0]
    blocks = owners // 8
    flat = req_ref[...].T
    owner = flat[0:requests]
    q = lax.broadcasted_iota(jnp.int32, (requests, owners), 0)
    earlier = jnp.zeros((requests, owners), jnp.int32)
    for other in range(requests - 1):
        same = (owner == owner[other : other + 1]) & (q > other)
        earlier = jnp.where(same, 1, earlier)
    key = (owner * 2 + earlier).astype(F32)
    block_row = lax.broadcasted_iota(jnp.int32, (blocks, owners), 0)
    block_of = lax.broadcasted_iota(jnp.int32, (blocks, owners), 1) // 8
    own_block = block_row == block_of
    spread = []
    for n in range(requests):
        row = jnp.broadcast_to(key[n : n + 1], (blocks, owners))
        spread.append(jnp.where(own_block, row, 0.0).astype(BF16))
    inner = lax.broadcasted_iota(jnp.int32, (owners, 128), 0) % 8
    lane = lax.broadcasted_iota(jnp.int32, (owners, 128), 1)
    pick = jnp.where(inner == lane // 16, 1.0, 0.0).astype(BF16)
    wide = jnp.dot(jnp.concatenate(spread, axis=0), pick, preferred_element_type=F32)
    slot = (lax.broadcasted_iota(jnp.int32, (blocks * requests, 128), 1) // 8) % 2
    keys[...] = wide - slot.astype(F32)

    def step(n, c):
        found = [[jnp.full((8, 128), 8.0, F32) for _ in range(blocks // 8)] for _ in range(4)]
        wanted = [(2 * (n * 4 + m)).astype(F32) for m in range(4)]
        for r in range(requests):
            t = float((r // (2 * VIEWS)) * 2 + r % 2)
            for half in range(blocks // 8):
                k = keys[r * blocks + half * 8 : r * blocks + half * 8 + 8, :]
                for m in range(4):
                    found[m][half] = jnp.where(k == wanted[m], t, found[m][half])
        for m in range(4):
            for half in range(blocks // 8):
                target_ref[n * 4 + m, half * 8 : half * 8 + 8, :] = found[m][half]
        return c

    lax.fori_loop(0, owners // 4, step, 0)

    half_of = lax.broadcasted_iota(jnp.int32, (16, 128), 1) // 64
    for source in range(6):
        for zc in range(2):
            part = wd_ref[zc, source * 16 : source * 16 + 16, :]
            for il in range(8):
                mine = jnp.where(half_of == il // 4, part, jnp.zeros_like(part))
                for il3 in range(4):
                    value = mine if il3 == il % 4 else jnp.zeros_like(part)
                    gate_ref[
                        pl.ds(source * 128 + il * 16, 16), pl.ds((zc * 4 + il3) * 128, 128)
                    ] = value


def combine_kernel(ans_ref, target_ref, out_ref):
    owners = ans_ref.shape[0]
    halves = ans_ref.shape[1] // 8

    def step(o, acc):
        acc = list(acc)
        for half in range(halves):
            data = ans_ref[o, half * 8 : half * 8 + 8, :]
            target = target_ref[o, half * 8 : half * 8 + 8, :]
            for t in range(8):
                n = t * halves + half
                acc[n] = acc[n] + jnp.where(target == float(t), data, 0.0)
        return tuple(acc)

    zero = jnp.zeros((8, 128), F32)
    acc = lax.fori_loop(0, owners, step, (zero,) * (8 * halves), unroll=8)
    lane = lax.broadcasted_iota(jnp.int32, (8, 128), 1)
    even = (lane // 8) % 2 == 0
    for p in range(PD):
        for half in range(halves):
            a = acc[(2 * p) * halves + half]
            b = acc[(2 * p + 1) * halves + half]
            a = a + pltpu.roll(a, 120, 1)
            b = b + pltpu.roll(b, 8, 1)
            out_ref[pl.ds((p * halves + half) * 8, 8), :] = jnp.where(even, a, b) / (VIEWS * 4.0)


def column_kernel(left_ref, mid_ref, right_ref, w_ref, bias_ref, wo_ref, out_ref):
    rows = mid_ref.shape[0] // 2
    blocks = rows // PD
    x = jnp.concatenate(
        [ref[pl.ds(j * rows, rows), :] for ref in (left_ref, mid_ref, right_ref) for j in range(2)],
        axis=1,
    )
    hi = x.astype(BF16)
    rest = x - hi.astype(F32)
    mid = rest.astype(BF16)
    low = (rest - mid.astype(F32)).astype(BF16)
    y3 = jnp.dot(
        jnp.concatenate([low, mid, hi], axis=0), w_ref[...], preferred_element_type=F32
    )
    y = (y3[:rows] + y3[rows : 2 * rows]) + y3[2 * rows :]
    z = y[:, :512] + bias_ref[0:1, :]
    cand = jnp.tanh(y[:, 512:] + bias_ref[1:2, :])
    small = jnp.exp(-jnp.abs(z))
    big = 1.0 / (1.0 + small)
    small = small * big
    up = z >= 0
    retain = jnp.where(up, big, small)
    fresh = jnp.where(up, small, big) * cand
    order = [(il3, p) for il3 in range(4) for p in range(PD)]

    def cut(v, il3, p):
        return v[p * blocks : (p + 1) * blocks, il3 * 128 : (il3 + 1) * 128]

    dc = None
    for il3, p in order:
        d, o = cut(retain, il3, p), cut(fresh, il3, p)
        dc, oc = (d, o) if dc is None else (d * dc, d * oc + o)
    lane = lax.broadcasted_iota(jnp.int32, (blocks, 128), 1)
    sub = lax.broadcasted_iota(jnp.int32, (blocks, 128), 0)
    first = lane < 64
    od = pltpu.roll(dc, 64, 1)
    oo = pltpu.roll(oc, 64, 1)
    pd_all = dc * od
    po_all = jnp.where(first, od * oc + oo, dc * oo + oc)
    reach = 1
    while reach < blocks:
        sd = jnp.where(sub < reach, 1.0, pltpu.roll(pd_all, reach, 0))
        so = jnp.where(sub < reach, 0.0, pltpu.roll(po_all, reach, 0))
        po_all = pd_all * so + po_all
        pd_all = pd_all * sd
        reach *= 2
    before = jnp.where(sub < 1, 0.0, pltpu.roll(po_all, 1, 0))
    h = jnp.where(first, before, od * before + oo)
    states = {}
    for il3, p in order:
        h = cut(retain, il3, p) * h + cut(fresh, il3, p)
        states[il3, p] = h
    wide = jnp.concatenate(
        [jnp.concatenate([states[il3, p] for p in range(PD)], axis=1) for il3 in range(4)], axis=0
    )
    s = jnp.dot(wide, wo_ref[...], precision=lax.Precision.HIGHEST, preferred_element_type=F32)

    def over(op, v):
        v = jnp.broadcast_to(v, (8, 128))
        v = op(v, pltpu.roll(v, 2, 1))
        v = op(v, pltpu.roll(v, 4, 1))
        return op(v, pltpu.roll(v, 8, 1))[0:1]

    row = lax.broadcasted_iota(jnp.int32, (rows, 128), 0)
    col = lax.broadcasted_iota(jnp.int32, (rows, 128), 1)
    plane = (row % blocks) * 32 + ((col // 8) % 2) * 16 + (row // blocks) * 4 + (col % 8) // 2
    value = 1.0 / (0.1 + 0.9 * plane.astype(F32) / (PD * 8 * blocks - 1))
    highest = over(jnp.maximum, jnp.max(s, axis=0, keepdims=True))
    weights = jnp.exp(s - highest)
    total = over(jnp.add, jnp.sum(weights, axis=0, keepdims=True))
    depth = over(jnp.add, jnp.sum(weights * value, axis=0, keepdims=True))
    prob = weights / total
    expected = depth / total
    for u in range(2):
        mine = prob if u == 0 else pltpu.roll(prob, 120, 1)
        message = jnp.where(col < 8, mine, expected)
        for il3 in range(4):
            out_ref[pl.ds(u * 4 + il3, blocks, stride=8), :] = message[
                il3 * blocks : (il3 + 1) * blocks
            ]


def output_kernel(x_ref, prob_ref, map_ref):
    t = x_ref[...].T
    for p in range(PD):
        prob_ref[p] = t[p * 2 : p * 2 + 2]
    map_ref[...] = t[8:10]


def gate_rows(w_gates, slab):
    w = w_gates.reshape(3, 3, 2, 32, 8).transpose(0, 1, 4, 2, 3)
    w = jnp.pad(w, ((2, 2), (0, 0), (0, 0), (0, 0), (0, 0)))
    by_row = [lax.dynamic_slice_in_dim(w, 3 - r - 2 * slab, 4, axis=0) for r in range(2)]
    v = jnp.stack(by_row, axis=4).reshape(2, 2, 3, 8, 2, 2, 32)
    v = v.transpose(4, 2, 0, 1, 3, 5, 6).reshape(2, 96, 64)
    return jnp.concatenate([v, v], axis=2)


def body(ref_feat, src_feat, tile_owner, tile_local, col_shift, w_gates, bias_z, bias_c, w_out):
    owners = lax.axis_size("depth")
    row_count, feat, cols = ref_feat.shape
    requests = tile_local.shape[0]
    tiles = src_feat.shape[0]
    blocks = owners // 8
    message = jnp.concatenate(
        [tile_owner[:, 0], tile_local, col_shift, jnp.zeros((128 - 3 * requests,), jnp.int32)]
    )
    message = jnp.broadcast_to(message[None, None, :], (owners, 1, 128))
    asked = lax.all_to_all(message, "depth", split_axis=0, concat_axis=0, tiled=True)
    asked = asked.reshape(owners, 128)

    table, channels = pl.pallas_call(
        prepare_kernel,
        out_shape=(
            jax.ShapeDtypeStruct((row_count * (2 * MAXSHIFT + 1), feat, cols), F32),
            jax.ShapeDtypeStruct((tiles, feat, cols), BF16),
        ),
        in_specs=[vspec(), vspec()],
        out_specs=(vspec(), vspec()),
        scratch_shapes=[
            pltpu.VMEM((row_count * feat, cols), F32),
            pltpu.VMEM((tiles * feat, cols), F32),
        ],
        compiler_params=params(),
        cost_estimate=pl.CostEstimate(flops=2000000, transcendentals=0, bytes_accessed=4000000),
        name="prepare",
    )(ref_feat, src_feat)

    def answers_of(*refs):
        answer_kernel(requests, *refs)

    answers = pl.pallas_call(
        answers_of,
        out_shape=jax.ShapeDtypeStruct((cols * blocks, 128), F32),
        in_specs=[vspec(), vspec(), vspec()],
        out_specs=vspec(),
        scratch_shapes=[
            pltpu.VMEM((8, owners), jnp.int32),
            pltpu.SMEM((8, owners), jnp.int32),
            pltpu.SemaphoreType.DMA,
        ],
        compiler_params=params(),
        name="answer",
    )(asked, table, channels)
    answers = lax.all_to_all(
        answers.reshape(cols, blocks, 128), "depth", split_axis=0, concat_axis=0, tiled=True
    )

    slab = lax.axis_index("slab")

    def tables_of(*refs):
        table_kernel(requests, *refs)

    targets, gates = pl.pallas_call(
        tables_of,
        out_shape=(
            jax.ShapeDtypeStruct((owners, blocks, 128), F32),
            jax.ShapeDtypeStruct((768, 1024), BF16),
        ),
        in_specs=[vspec(), vspec()],
        out_specs=(vspec(), vspec()),
        scratch_shapes=[pltpu.VMEM((requests * blocks, 128), F32)],
        compiler_params=params(),
        cost_estimate=pl.CostEstimate(flops=20000000, transcendentals=0, bytes_accessed=3000000),
        name="tables",
    )(asked, gate_rows(w_gates, slab))

    cost = pl.pallas_call(
        combine_kernel,
        out_shape=jax.ShapeDtypeStruct((PD * blocks, 128), F32),
        in_specs=[vspec(), vspec()],
        out_specs=vspec(),
        compiler_params=params(),
        name="combine",
    )(answers, targets)
    both = lax.all_gather(cost, "slab", tiled=True)
    ends = owners - 1
    left = lax.ppermute(both, "depth", [(i, i + 1) for i in range(ends)])
    right = lax.ppermute(both, "depth", [(i + 1, i) for i in range(ends)])

    bias = jnp.stack([jnp.tile(bias_z, 16), jnp.tile(bias_c, 16)])
    unit_row = jnp.arange(512, dtype=jnp.int32)[:, None] // 32
    unit_row = ((unit_row // 2) % 2) * 8 + (unit_row // 4) * 2 + unit_row % 2
    score_col = jnp.arange(128, dtype=jnp.int32)[None, :] % 16
    project = jnp.where(unit_row == score_col, jnp.tile(w_out, 16)[:, None], 0.0)
    packed = pl.pallas_call(
        column_kernel,
        out_shape=jax.ShapeDtypeStruct((owners, 128), F32),
        in_specs=[vspec()] * 6,
        out_specs=vspec(),
        compiler_params=params(),
        name="column",
    )(left, both, right, gates, bias, project)
    packed = lax.all_to_all(
        packed.reshape(owners, 1, 128), "depth", split_axis=0, concat_axis=0, tiled=True
    )
    return pl.pallas_call(
        output_kernel,
        out_shape=(
            jax.ShapeDtypeStruct((PD, row_count, cols), F32),
            jax.ShapeDtypeStruct((row_count, cols), F32),
        ),
        in_specs=[vspec()],
        out_specs=(vspec(), vspec()),
        compiler_params=params(),
        name="output",
    )(packed.reshape(cols, 128))


def solution(mesh):
    return jax.shard_map(
        body,
        mesh=mesh,
        in_specs=(
            P("slab", None, None),
            P("depth", None, None),
            P(("depth", "slab"), None),
            P(("depth", "slab")),
            P(("depth", "slab")),
            P(),
            P(),
            P(),
            P(),
        ),
        out_specs=(P("depth", "slab", None), P("slab", None)),
        check_vma=False,
    )
```

time: 113 us -> 110 us (0.973)
  waiting for transfers between devices: 52 us -> 35.4 us
  blocking collectives: 16.9 us -> 27.4 us
  Pallas kernels: 8.26 us -> 11.5 us
  local copies, waits for them, and re-layouts: 4.16 us -> 5.61 us
    all_to_all x2 -> x1, waiting for transfers between devices: 43.6 us -> 24.7 us  [body(): lax.all_to_all(answers.reshape(cols, blocks, 128), 'depth', split_axis=0,...]
    all_to_all x1, blocking collectives: 16.9 us -> 25.5 us  [body(): lax.all_to_all(packed.reshape(owners, 1, 128), 'depth', split_axis=0, con...]
    all_to_all x2 -> x1, starting transfers between devices: 13.3 us -> 6.79 us  [body(): lax.all_to_all(answers.reshape(cols, blocks, 128), 'depth', split_axis=0,...]
    ppermute x0 -> x2, starting transfers between devices: none -> 5.83 us  [the longest x1 3.89 us: body(): right = lax.ppermute(both, 'depth', [(i + 1, i) for i in range(ends)])]
    pallas_call x2 -> x3, Pallas kernels: 5.68 us -> 8.79 us  [the longest x1 4.32 us: body(): pl.pallas_call(answers_of, out_shape=jax.ShapeDtypeStruct((cols * blocks,...]
    ppermute x0 -> x2, waiting for transfers between devices: none -> 2.24 us  [the longest x1 1.96 us: body(): right = lax.ppermute(both, 'depth', [(i + 1, i) for i in range(ends)])]
    unnamed x14 -> x16, local copies, waits for them, and re-layouts: 2.06 us -> 4.26 us
    all_gather x0 -> x1, blocking collectives: none -> 1.85 us  [body(): both = lax.all_gather(cost, 'slab', tiled=True)]
  transfers between devices with their start and end apart: 3 -> 4, of which waited for: 3 -> 4; matrix products, arithmetic and copies ran while one was open for 2% -> 1% of each run, Pallas kernels for 1% -> 4%
where the time goes in v2:
time: 110 us; the launch traced here: 109 us
  waiting for transfers between devices  35.4 us (32%)
  starting transfers between devices  27.6 us (25%)
  blocking collectives  27.4 us (25%)
  Pallas kernels  11.5 us (10%)
  local copies, waits for them, and re-layouts  5.61 us (5%)
  other arithmetic  1.11 us (1%)
    all_to_all x1, blocking collectives, body(): lax.all_to_all(packed.reshape(owners, 1, 128), 'depth', split_axis=0, con...  25.5 us
    all_to_all x1, waiting for transfers between devices, body(): lax.all_to_all(answers.reshape(cols, blocks, 128), 'depth', split_axis=0,...  24.7 us
    all_to_all x1, starting transfers between devices, body(): lax.all_to_all(message, 'depth', split_axis=0, concat_axis=0, tiled=True)  15 us
    all_to_all x1, waiting for transfers between devices, body(): lax.all_to_all(message, 'depth', split_axis=0, concat_axis=0, tiled=True)  8.44 us
    all_to_all x1, starting transfers between devices, body(): lax.all_to_all(answers.reshape(cols, blocks, 128), 'depth', split_axis=0,...  6.79 us
    pallas_call x1, Pallas kernels, body(): pl.pallas_call(answers_of, out_shape=jax.ShapeDtypeStruct((cols * blocks,...  4.32 us
    unnamed x16, local copies, waits for them, and re-layouts  4.26 us
    ppermute x1, starting transfers between devices, body(): right = lax.ppermute(both, 'depth', [(i + 1, i) for i in range(ends)])  3.89 us
  transfers between devices with their start and end apart: 4, of which 4 were waited for; matrix products, arithmetic and copies ran while one was open for 1% of the time, Pallas kernels for 4%

profile of v2, /device:TPU:32, one launch (start us, length us, event | category | flops | bytes accessed | tf_op | source)
XLA Modules:
  0.0 109.4 jit_solution(13276558789775659874)
XLA Ops:
  0.6 0.8 pad_add_fusion
  1.4 0.7 broadcast_in_dim.22
  2.1 15.0 %all-to-all-start = ((s32[128,1,128]{2,1,0:T(1,128)}), s32[128,1,128]{2,1,0:T(1,128)S(1)}, u32[]{:S(2)}, u32[]{:S(2)}) async-start(s32[128,1,128]{2,1,0:T(1,128)} %broadcast_in_dim.22), calls=%async_computation | async-start | bytes 131072 | tf_op jit(solution)/shard_map/all_to_all | solution.py:290
  17.1 0.0 copy-start
  17.1 1.3 %copy-done = bf16[160,32,128]{2,1,0:T(8,128)(2,1)S(1)} copy-done((bf16[160,32,128]{2,1,0:T(8,128)(2,1)S(1)}, bf16[160,32,128]{2,1,0:T(8,128)(2,1)}, u32[]{:S(2)}) %copy-start) | copy-done | bytes 1310744
  18.4 0.0 copy-start.3
  18.4 0.7 copy-done.3
  19.1 0.6 prepare.1
  19.8 8.4 %all-to-all-done = s32[128,1,128]{2,1,0:T(1,128)S(1)} async-done(((s32[128,1,128]{2,1,0:T(1,128)}), s32[128,1,128]{2,1,0:T(1,128)S(1)}, u32[]{:S(2)}, u32[]{:S(2)}) %all-to-all-start) | async-done | bytes 65568 | tf_op jit(solution)/shard_map/all_to_all | solution.py:290
  28.2 4.3 %answer.1 = f32[2048,128]{1,0:T(8,128)} custom-call(s32[128,128]{1,0:T(8,128)S(1)} %bitcast.14, f32[66,32,128]{2,1,0:T(8,128)S(1)} %get-tuple-element.6.refs_1_, bf16[160,32,128]{2,1,0:T(8,128)(2,1)S(1)} %get-tuple-element.7.refs_2_), custom_call_target="tpu_custom_call" | custom-call | tf_op jit(solution)/shard_map/answer/pallas_call | solution.py:313
  32.5 0.0 copy-start.4
  32.6 0.0 copy-start.5
  32.6 0.0 copy-start.6
  32.6 0.0 copy-start.7
  32.6 6.8 %all-to-all-start.1 = ((f32[128,16,128]{2,1,0:T(8,128)}), f32[128,16,128]{2,1,0:T(8,128)S(1)}, u32[]{:S(2)}, u32[]{:S(2)}) async-start(f32[128,16,128]{2,1,0:T(8,128)} %bitcast.2), calls=%async_computation.1 | async-start | bytes 2097152 | tf_op jit(solution)/shard_map/all_to_all | solution.py:326
  39.4 0.0 copy-done.4
  39.4 0.1 reshape.190
  39.5 0.2 pad_dynamic-slice_fusion.1
  39.7 0.1 copy.19
  39.8 0.1 reshape.191
  39.9 0.0 copy-done.5
  39.9 0.1 stack_tile.7
  40.0 0.0 copy-done.6
  40.0 0.1 stack_tile.6
  40.1 0.0 copy-done.7
  40.1 0.1 broadcast_in_dim.23
  40.2 0.1 pad_maximum_fusion.refs_1_
  40.3 0.2 compare_select_fusion.wo_ref
  40.5 3.5 %tables.1 = (f32[128,16,128]{2,1,0:T(8,128)S(1)}, bf16[768,1024]{1,0:T(8,128)(2,1)S(1)}) custom-call(s32[128,128]{1,0:T(8,128)S(1)} %bitcast.15, bf16[2,96,128]{2,1,0:T(8,128)(2,1)S(1)} %pad_maximum_fusion.refs_1_), custom_call_target="tpu_custom_call" | custom-call | flops 20000000 | bytes 3000000 | tf_op jit(solution)/shard_map/tables/pallas_call | solution.py:335
  44.0 0.0 copy-start.1
  44.0 1.0 copy-done.1
  45.0 24.7 %all-to-all-done.1.ans_ref = f32[128,16,128]{2,1,0:T(8,128)S(1)} async-done(((f32[128,16,128]{2,1,0:T(8,128)}), f32[128,16,128]{2,1,0:T(8,128)S(1)}, u32[]{:S(2)}, u32[]{:S(2)}) %all-to-all-start.1) | async-done | bytes 1048608 | tf_op jit(solution)/shard_map/all_to_all | solution.py:326
  69.7 0.0 copy-start.2
  69.7 1.2 %copy-done.2 = f32[128,16,128]{2,1,0:T(8,128)S(1)} copy-done((f32[128,16,128]{2,1,0:T(8,128)S(1)}, f32[128,16,128]{2,1,0:T(8,128)}, u32[]{:S(2)}) %copy-start.2) | copy-done | bytes 1048600
  70.9 1.0 combine.1
  71.9 1.9 %all_gather.3.mid_ref = f32[128,128]{1,0:T(8,128)S(1)} all-gather(f32[64,128]{1,0:T(8,128)S(1)} %combine.1), channel_id=1, replica_groups=mesh['depth'=128,'slab'=2] {'slab'}, dimensions={0}, use_global_device_ids=true | all-gather | bytes 98304 | tf_op jit(solution)/shard_map/all_gather | solution.py:357
  73.7 1.9 %collective-permute-start = (f32[128,128]{1,0:T(8,128)S(1)}, f32[128,128]{1,0:T(8,128)S(1)}, u32[]{:S(2)}, u32[]{:S(2)}) collective-permute-start(f32[128,128]{1,0:T(8,128)S(1)} %all_gather.3.mid_ref), channel_id=1, source_target_pairs={{0,2},{2,4},{4,6},{6,8},{8,10},{10,12},{12,14},{14,16},{16,18},{18... | collective-permute-start | bytes 196616 | tf_op jit(solution)/shard_map/ppermute | solution.py:359
  75.7 3.9 %collective-permute-start.1 = (f32[128,128]{1,0:T(8,128)S(1)}, f32[128,128]{1,0:T(8,128)S(1)}, u32[]{:S(2)}, u32[]{:S(2)}) collective-permute-start(f32[128,128]{1,0:T(8,128)S(1)} %all_gather.3.mid_ref), channel_id=1, source_target_pairs={{2,0},{4,2},{6,4},{8,6},{10,8},{12,10},{14,12},{16,14},{18,16},{20... | collective-permute-start | bytes 196616 | tf_op jit(solution)/shard_map/ppermute | solution.py:360
  79.6 0.3 collective-permute-done.left_ref
  79.9 2.0 %collective-permute-done.1.right_ref = f32[128,128]{1,0:T(8,128)S(1)} collective-permute-done((f32[128,128]{1,0:T(8,128)S(1)}, f32[128,128]{1,0:T(8,128)S(1)}, u32[]{:S(2)}, u32[]{:S(2)}) %collective-permute-start.1) | collective-permute-done | bytes 65568 | tf_op jit(solution)/shard_map/ppermute | solution.py:360
  81.8 1.4 %column.1 = f32[128,128]{1,0:T(8,128)S(1)} custom-call(f32[128,128]{1,0:T(8,128)S(1)} %collective-permute-done.left_ref, f32[128,128]{1,0:T(8,128)S(1)} %all_gather.3.mid_ref, f32[128,128]{1,0:T(8,128)S(1)} %collective-permute-done.1.right_ref, bf16[768,1024]{1,0:T(8,128)(2,1)S(1)} %get-tuple-element.9.w_ref, f32[2,512]{1,0:T(2,128)S(1)} %pad_maximum_fusion.1.bias_ref, ...), custom_call_target="tpu_custom_call" | custom-call | tf_op jit(solution)/shard_map/column/pallas_call | solution.py:367
  83.2 25.5 %all_to_all.15 = f32[128,1,128]{2,1,0:T(1,128)S(1)} all-to-all(f32[128,1,128]{2,1,0:T(1,128)S(1)} %bitcast.16), channel_id=1, replica_groups=mesh['depth'=128,'slab'=2] {'depth'}, dimensions={0} | all-to-all | bytes 131072 | tf_op jit(solution)/shard_map/all_to_all | solution.py:375
  108.7 0.7 output.1
  (10 shorter events, 0.1 us)
Async XLA Ops:
  2.1 26.1 %all-to-all-start = ((s32[128,1,128]{2,1,0:T(1,128)}), s32[128,1,128]{2,1,0:T(1,128)S(1)}, u32[]{:S(2)}, u32[]{:S(2)}) async-start(s32[128,1,128]{2,1,0:T(1,128)} %broadcast_in_dim.22), calls=%async_computation | async-start | bytes 131072 | tf_op jit(solution)/shard_map/all_to_all | solution.py:290
  17.1 1.3 %copy-start = (bf16[160,32,128]{2,1,0:T(8,128)(2,1)S(1)}, bf16[160,32,128]{2,1,0:T(8,128)(2,1)}, u32[]{:S(2)}) copy-start(bf16[160,32,128]{2,1,0:T(8,128)(2,1)} %src_ref.1) | copy-start | bytes 3932164
  18.4 0.7 copy-start.3
  32.5 6.9 %copy-start.4 = (bf16[9,64,8]{1,2,0:T(8,128)(2,1)S(1)}, bf16[9,64,8]{1,2,0:T(8,128)(2,1)}, u32[]{:S(2)}) copy-start(bf16[9,64,8]{1,2,0:T(8,128)(2,1)} %param.14) | copy-start | bytes 27652
  32.6 7.4 %copy-start.5 = (f32[32]{0:T(128)S(1)}, f32[32]{0:T(128)}, u32[]{:S(2)}) copy-start(f32[32]{0:T(128)} %param.16) | copy-start | bytes 388
  32.6 7.4 %copy-start.6 = (f32[32]{0:T(128)S(1)}, f32[32]{0:T(128)}, u32[]{:S(2)}) copy-start(f32[32]{0:T(128)} %param.15) | copy-start | bytes 388
  32.6 7.5 %copy-start.7 = (f32[32]{0:T(128)S(1)}, f32[32]{0:T(128)}, u32[]{:S(2)}) copy-start(f32[32]{0:T(128)} %param.17) | copy-start | bytes 388
  32.6 37.1 %all-to-all-start.1 = ((f32[128,16,128]{2,1,0:T(8,128)}), f32[128,16,128]{2,1,0:T(8,128)S(1)}, u32[]{:S(2)}, u32[]{:S(2)}) async-start(f32[128,16,128]{2,1,0:T(8,128)} %bitcast.2), calls=%async_computation.1 | async-start | bytes 2097152 | tf_op jit(solution)/shard_map/all_to_all | solution.py:326
  44.0 1.0 copy-start.1
  69.7 1.2 %copy-start.2 = (f32[128,16,128]{2,1,0:T(8,128)S(1)}, f32[128,16,128]{2,1,0:T(8,128)}, u32[]{:S(2)}) copy-start(f32[128,16,128]{2,1,0:T(8,128)} %copy-done.1) | copy-start | bytes 3145732
  73.7 6.1 %collective-permute-start = (f32[128,128]{1,0:T(8,128)S(1)}, f32[128,128]{1,0:T(8,128)S(1)}, u32[]{:S(2)}, u32[]{:S(2)}) collective-permute-start(f32[128,128]{1,0:T(8,128)S(1)} %all_gather.3.mid_ref), channel_id=1, source_target_pairs={{0,2},{2,4},{4,6},{6,8},{8,10},{10,12},{12,14},{14,16},{16,18},{18... | collective-permute-start | bytes 196616 | tf_op jit(solution)/shard_map/ppermute | solution.py:359
  75.7 6.2 %collective-permute-start.1 = (f32[128,128]{1,0:T(8,128)S(1)}, f32[128,128]{1,0:T(8,128)S(1)}, u32[]{:S(2)}, u32[]{:S(2)}) collective-permute-start(f32[128,128]{1,0:T(8,128)S(1)} %all_gather.3.mid_ref), channel_id=1, source_target_pairs={{2,0},{4,2},{6,4},{8,6},{10,8},{12,10},{14,12},{16,14},{18,16},{20... | collective-permute-start | bytes 196616 | tf_op jit(solution)/shard_map/ppermute | solution.py:360

commit v3 on v2

--- a/solution.py
+++ b/solution.py
@@ -10,11 +10,22 @@
 MAXSHIFT = 16
 F32 = jnp.float32
 BF16 = jnp.bfloat16
-VMEM_LIMIT = 40 * 1024 * 1024
-
-
-def params():
-    return pltpu.CompilerParams(vmem_limit_bytes=VMEM_LIMIT)
+MIB = 1024 * 1024
+TORUS = (4, 4, 8)
+
+
+def params(mib):
+    return pltpu.CompilerParams(vmem_limit_bytes=mib * MIB)
+
+
+def line_bases():
+    nx, ny, nz = TORUS
+    return [(x * ny + (y - x) % ny) * nz for x in range(nx) for y in range(ny)]
+
+
+def path():
+    nz = TORUS[2]
+    return [base + (n - m) % nz for m, base in enumerate(line_bases()) for n in range(nz)]
 
 
 def vspec():
@@ -92,7 +103,10 @@
             for s in range(2):
                 parts.append(one(b * 8 + il, s))
         block = jnp.concatenate(parts, axis=0).T
-        out_ref[pl.ds(b, cols, stride=owners // 8), :] = block
+        blocks = owners // 8
+        for m, base in enumerate(line_bases()):
+            turned = pltpu.roll(block[m * 8 : m * 8 + 8], (8 - m) % 8, 0)
+            out_ref[pl.ds(base * blocks + b, 8, stride=blocks), :] = turned
         return c
 
     lax.fori_loop(0, owners // 8, step, 0, unroll=2)
@@ -133,8 +147,7 @@
                 for m in range(4):
                     found[m][half] = jnp.where(k == wanted[m], t, found[m][half])
         for m in range(4):
-            for half in range(blocks // 8):
-                target_ref[n * 4 + m, half * 8 : half * 8 + 8, :] = found[m][half]
+            target_ref[n * 4 + m] = jnp.concatenate(found[m], axis=0).astype(BF16)
         return c
 
     lax.fori_loop(0, owners // 4, step, 0)
@@ -158,9 +171,10 @@
 
     def step(o, acc):
         acc = list(acc)
+        targets = target_ref[o].astype(F32)
         for half in range(halves):
             data = ans_ref[o, half * 8 : half * 8 + 8, :]
-            target = target_ref[o, half * 8 : half * 8 + 8, :]
+            target = targets[half * 8 : half * 8 + 8, :]
             for t in range(8):
                 n = t * halves + half
                 acc[n] = acc[n] + jnp.where(target == float(t), data, 0.0)
@@ -262,7 +276,8 @@
 
 
 def output_kernel(x_ref, prob_ref, map_ref):
-    t = x_ref[...].T
+    lines = [pltpu.roll(x_ref[pl.ds(b, 8), :], m % 8, 0) for m, b in enumerate(line_bases())]
+    t = jnp.concatenate(lines, axis=0).T
     for p in range(PD):
         prob_ref[p] = t[p * 2 : p * 2 + 2]
     map_ref[...] = t[8:10]
@@ -283,10 +298,15 @@
     requests = tile_local.shape[0]
     tiles = src_feat.shape[0]
     blocks = owners // 8
-    message = jnp.concatenate(
-        [tile_owner[:, 0], tile_local, col_shift, jnp.zeros((128 - 3 * requests,), jnp.int32)]
-    )
-    message = jnp.broadcast_to(message[None, None, :], (owners, 1, 128))
+    shape = (owners, 1, 128)
+    message = jnp.where(
+        lax.broadcasted_iota(jnp.int32, shape, 2) < 3 * requests,
+        0,
+        lax.broadcasted_iota(jnp.int32, shape, 0),
+    )
+    for n, part in enumerate((tile_owner[:, 0], tile_local, col_shift)):
+        wide = jnp.broadcast_to(part[None, None, :], (owners, 1, requests))
+        message += jnp.pad(wide, ((0, 0), (0, 0), (n * requests, 128 - (n + 1) * requests)))
     asked = lax.all_to_all(message, "depth", split_axis=0, concat_axis=0, tiled=True)
     asked = asked.reshape(owners, 128)
 
@@ -302,7 +322,7 @@
             pltpu.VMEM((row_count * feat, cols), F32),
             pltpu.VMEM((tiles * feat, cols), F32),
         ],
-        compiler_params=params(),
+        compiler_params=params(16),
         cost_estimate=pl.CostEstimate(flops=2000000, transcendentals=0, bytes_accessed=4000000),
         name="prepare",
     )(ref_feat, src_feat)
@@ -320,7 +340,7 @@
             pltpu.SMEM((8, owners), jnp.int32),
             pltpu.SemaphoreType.DMA,
         ],
-        compiler_params=params(),
+        compiler_params=params(10),
         name="answer",
     )(asked, table, channels)
     answers = lax.all_to_all(
@@ -335,13 +355,13 @@
     targets, gates = pl.pallas_call(
         tables_of,
         out_shape=(
-            jax.ShapeDtypeStruct((owners, blocks, 128), F32),
+            jax.ShapeDtypeStruct((owners, blocks, 128), BF16),
             jax.ShapeDtypeStruct((768, 1024), BF16),
         ),
         in_specs=[vspec(), vspec()],
         out_specs=(vspec(), vspec()),
         scratch_shapes=[pltpu.VMEM((requests * blocks, 128), F32)],
-        compiler_params=params(),
+        compiler_params=params(8),
         cost_estimate=pl.CostEstimate(flops=20000000, transcendentals=0, bytes_accessed=3000000),
         name="tables",
     )(asked, gate_rows(w_gates, slab))
@@ -351,13 +371,14 @@
         out_shape=jax.ShapeDtypeStruct((PD * blocks, 128), F32),
         in_specs=[vspec(), vspec()],
         out_specs=vspec(),
-        compiler_params=params(),
+        compiler_params=params(6),
         name="combine",
     )(answers, targets)
     both = lax.all_gather(cost, "slab", tiled=True)
-    ends = owners - 1
-    left = lax.ppermute(both, "depth", [(i, i + 1) for i in range(ends)])
-    right = lax.ppermute(both, "depth", [(i + 1, i) for i in range(ends)])
+    chips = path()
+    pairs = list(zip(chips[:-1], chips[1:]))
+    left = lax.ppermute(both, "depth", pairs)
+    right = lax.ppermute(both, "depth", [(b, a) for a, b in pairs])
 
     bias = jnp.stack([jnp.tile(bias_z, 16), jnp.tile(bias_c, 16)])
     unit_row = jnp.arange(512, dtype=jnp.int32)[:, None] // 32
@@ -369,7 +390,7 @@
         out_shape=jax.ShapeDtypeStruct((owners, 128), F32),
         in_specs=[vspec()] * 6,
         out_specs=vspec(),
-        compiler_params=params(),
+        compiler_params=params(10),
         name="column",
     )(left, both, right, gates, bias, project)
     packed = lax.all_to_all(
@@ -383,7 +404,7 @@
         ),
         in_specs=[vspec()],
         out_specs=(vspec(), vspec()),
-        compiler_params=params(),
+        compiler_params=params(4),
         name="output",
     )(packed.reshape(cols, 128))
 

time: 110 us -> 105 us (0.955)
  blocking collectives: 27.4 us -> 21.6 us
  waiting for transfers between devices: 35.4 us -> 36.6 us
    all_to_all x1, blocking collectives: 25.5 us -> 19.7 us  [body(): lax.all_to_all(packed.reshape(owners, 1, 128), 'depth', split_axis=0, con...]
    unnamed x16 -> x12, local copies, waits for them, and re-layouts: 4.26 us -> 2.05 us
    pad x0 -> x3, local copies, waits for them, and re-layouts: none -> 2.12 us  [body(): jnp.pad(wide, ((0, 0), (0, 0), (n * requests, 128 - (n + 1) * requests)))]
    all_to_all x1, waiting for transfers between devices: 24.7 us -> 25.9 us  [body(): lax.all_to_all(answers.reshape(cols, blocks, 128), 'depth', split_axis=0,...]
where the time goes in v3:
time: 105 us; the launch traced here: 104 us
  waiting for transfers between devices  36.6 us (35%)
  starting transfers between devices  27.6 us (26%)
  blocking collectives  21.6 us (21%)
  Pallas kernels  11.4 us (11%)
  local copies, waits for them, and re-layouts  4.86 us (5%)
    all_to_all x1, waiting for transfers between devices, body(): lax.all_to_all(answers.reshape(cols, blocks, 128), 'depth', split_axis=0,...  25.9 us
    all_to_all x1, blocking collectives, body(): lax.all_to_all(packed.reshape(owners, 1, 128), 'depth', split_axis=0, con...  19.7 us
    all_to_all x1, starting transfers between devices, body(): lax.all_to_all(message, 'depth', split_axis=0, concat_axis=0, tiled=True)  15 us
    all_to_all x1, waiting for transfers between devices, body(): lax.all_to_all(message, 'depth', split_axis=0, concat_axis=0, tiled=True)  8.45 us
    all_to_all x1, starting transfers between devices, body(): lax.all_to_all(answers.reshape(cols, blocks, 128), 'depth', split_axis=0,...  6.76 us
    pallas_call x1, Pallas kernels, body(): pl.pallas_call(answers_of, out_shape=jax.ShapeDtypeStruct((cols * blocks,...  4.37 us
    ppermute x1, starting transfers between devices, body(): right = lax.ppermute(both, 'depth', [(b, a) for a, b in pairs])  3.89 us
    pallas_call x1, Pallas kernels, body(): pl.pallas_call(tables_of, out_shape=(jax.ShapeDtypeStruct((owners, blocks...  3.33 us
  transfers between devices with their start and end apart: 4, of which 4 were waited for; matrix products, arithmetic and copies ran while one was open for 1% of the time, Pallas kernels for 4%

profile of v3, /device:TPU:32, one launch (start us, length us, event | category | flops | bytes accessed | tf_op | source)
XLA Modules:
  0.0 103.8 jit_solution(15209028424268771292)
XLA Ops:
  0.6 0.7 pad.26
  1.4 0.7 pad.24
  2.1 0.7 pad.22
  2.8 0.6 add_add_fusion
  3.4 15.0 %all-to-all-start = ((s32[128,1,128]{2,1,0:T(1,128)}), s32[128,1,128]{2,1,0:T(1,128)S(1)}, u32[]{:S(2)}, u32[]{:S(2)}) async-start(s32[128,1,128]{2,1,0:T(1,128)} %bitcast.1), calls=%async_computation | async-start | bytes 131072 | tf_op jit(solution)/shard_map/all_to_all | solution.py:310
  18.4 0.0 copy-start
  18.4 1.3 %copy-done = bf16[160,32,128]{2,1,0:T(8,128)(2,1)S(1)} copy-done((bf16[160,32,128]{2,1,0:T(8,128)(2,1)S(1)}, bf16[160,32,128]{2,1,0:T(8,128)(2,1)}, u32[]{:S(2)}) %copy-start) | copy-done | bytes 1310744
  19.7 0.0 copy-start.1
  19.7 0.7 copy-done.1
  20.4 0.6 prepare.1
  21.1 8.5 %all-to-all-done = s32[128,1,128]{2,1,0:T(1,128)S(1)} async-done(((s32[128,1,128]{2,1,0:T(1,128)}), s32[128,1,128]{2,1,0:T(1,128)S(1)}, u32[]{:S(2)}, u32[]{:S(2)}) %all-to-all-start) | async-done | bytes 65568 | tf_op jit(solution)/shard_map/all_to_all | solution.py:310
  29.6 4.4 %answer.1 = f32[2048,128]{1,0:T(8,128)} custom-call(s32[128,128]{1,0:T(8,128)S(1)} %bitcast.15, f32[66,32,128]{2,1,0:T(8,128)S(1)} %get-tuple-element.6.refs_1_, bf16[160,32,128]{2,1,0:T(8,128)(2,1)S(1)} %get-tuple-element.7.refs_2_), custom_call_target="tpu_custom_call" | custom-call | tf_op jit(solution)/shard_map/answer/pallas_call | solution.py:333
  33.9 0.0 copy-start.2
  33.9 0.0 copy-start.3
  34.0 0.0 copy-start.4
  34.0 0.0 copy-start.5
  34.0 6.8 %all-to-all-start.1 = ((f32[128,16,128]{2,1,0:T(8,128)}), f32[128,16,128]{2,1,0:T(8,128)S(1)}, u32[]{:S(2)}, u32[]{:S(2)}) async-start(f32[128,16,128]{2,1,0:T(8,128)} %bitcast.3), calls=%async_computation.1 | async-start | bytes 2097152 | tf_op jit(solution)/shard_map/all_to_all | solution.py:346
  40.8 0.0 copy-done.2
  40.8 0.1 reshape.280
  40.9 0.2 pad_dynamic-slice_fusion.1
  41.1 0.1 copy.24
  41.2 0.1 reshape.281
  41.3 0.0 copy-done.3
  41.3 0.1 stack_tile.7
  41.4 0.0 copy-done.4
  41.4 0.1 stack_tile.6
  41.5 0.0 copy-done.5
  41.5 0.1 broadcast_in_dim.18
  41.6 0.1 pad_maximum_fusion.refs_1_
  41.7 0.2 compare_select_fusion.wo_ref
  41.9 3.3 %tables.1 = (bf16[128,16,128]{2,1,0:T(8,128)(2,1)S(1)}, bf16[768,1024]{1,0:T(8,128)(2,1)S(1)}) custom-call(s32[128,128]{1,0:T(8,128)S(1)} %bitcast.16, bf16[2,96,128]{2,1,0:T(8,128)(2,1)S(1)} %pad_maximum_fusion.refs_1_), custom_call_target="tpu_custom_call" | custom-call | flops 20000000 | bytes 3000000 | tf_op jit(solution)/shard_map/tables/pallas_call | solution.py:355
  45.2 25.9 %all-to-all-done.1.ans_ref = f32[128,16,128]{2,1,0:T(8,128)S(1)} async-done(((f32[128,16,128]{2,1,0:T(8,128)}), f32[128,16,128]{2,1,0:T(8,128)S(1)}, u32[]{:S(2)}, u32[]{:S(2)}) %all-to-all-start.1) | async-done | bytes 1048608 | tf_op jit(solution)/shard_map/all_to_all | solution.py:346
  71.1 1.0 combine.1
  72.1 1.9 %all_gather.3.mid_ref = f32[128,128]{1,0:T(8,128)S(1)} all-gather(f32[64,128]{1,0:T(8,128)S(1)} %combine.1), channel_id=1, replica_groups=mesh['depth'=128,'slab'=2] {'slab'}, dimensions={0}, use_global_device_ids=true | all-gather | bytes 98304 | tf_op jit(solution)/shard_map/all_gather | solution.py:377
  74.0 1.9 %collective-permute-start = (f32[128,128]{1,0:T(8,128)S(1)}, f32[128,128]{1,0:T(8,128)S(1)}, u32[]{:S(2)}, u32[]{:S(2)}) collective-permute-start(f32[128,128]{1,0:T(8,128)S(1)} %all_gather.3.mid_ref), channel_id=1, source_target_pairs={{0,2},{2,4},{4,6},{6,8},{8,10},{10,12},{12,14},{14,30},{30,16},{16... | collective-permute-start | bytes 196616 | tf_op jit(solution)/shard_map/ppermute | solution.py:380
  75.9 3.9 %collective-permute-start.1 = (f32[128,128]{1,0:T(8,128)S(1)}, f32[128,128]{1,0:T(8,128)S(1)}, u32[]{:S(2)}, u32[]{:S(2)}) collective-permute-start(f32[128,128]{1,0:T(8,128)S(1)} %all_gather.3.mid_ref), channel_id=1, source_target_pairs={{2,0},{4,2},{6,4},{8,6},{10,8},{12,10},{14,12},{30,14},{16,30},{18... | collective-permute-start | bytes 196616 | tf_op jit(solution)/shard_map/ppermute | solution.py:381
  79.8 0.3 collective-permute-done.left_ref
  80.1 2.0 %collective-permute-done.1.right_ref = f32[128,128]{1,0:T(8,128)S(1)} collective-permute-done((f32[128,128]{1,0:T(8,128)S(1)}, f32[128,128]{1,0:T(8,128)S(1)}, u32[]{:S(2)}, u32[]{:S(2)}) %collective-permute-start.1) | collective-permute-done | bytes 65568 | tf_op jit(solution)/shard_map/ppermute | solution.py:381
  82.1 1.4 %column.1 = f32[128,128]{1,0:T(8,128)S(1)} custom-call(f32[128,128]{1,0:T(8,128)S(1)} %collective-permute-done.left_ref, f32[128,128]{1,0:T(8,128)S(1)} %all_gather.3.mid_ref, f32[128,128]{1,0:T(8,128)S(1)} %collective-permute-done.1.right_ref, bf16[768,1024]{1,0:T(8,128)(2,1)S(1)} %get-tuple-element.9.w_ref, f32[2,512]{1,0:T(2,128)S(1)} %pad_maximum_fusion.1.bias_ref, ...), custom_call_target="tpu_custom_call" | custom-call | tf_op jit(solution)/shard_map/column/pallas_call | solution.py:388
  83.4 19.7 %all_to_all.15 = f32[128,1,128]{2,1,0:T(1,128)S(1)} all-to-all(f32[128,1,128]{2,1,0:T(1,128)S(1)} %bitcast.17), channel_id=1, replica_groups=mesh['depth'=128,'slab'=2] {'depth'}, dimensions={0} | all-to-all | bytes 131072 | tf_op jit(solution)/shard_map/all_to_all | solution.py:396
  103.2 0.7 output.1
  (10 shorter events, 0.1 us)
Async XLA Ops:
  3.4 26.2 %all-to-all-start = ((s32[128,1,128]{2,1,0:T(1,128)}), s32[128,1,128]{2,1,0:T(1,128)S(1)}, u32[]{:S(2)}, u32[]{:S(2)}) async-start(s32[128,1,128]{2,1,0:T(1,128)} %bitcast.1), calls=%async_computation | async-start | bytes 131072 | tf_op jit(solution)/shard_map/all_to_all | solution.py:310
  18.4 1.3 %copy-start = (bf16[160,32,128]{2,1,0:T(8,128)(2,1)S(1)}, bf16[160,32,128]{2,1,0:T(8,128)(2,1)}, u32[]{:S(2)}) copy-start(bf16[160,32,128]{2,1,0:T(8,128)(2,1)} %src_ref.1) | copy-start | bytes 3932164
  19.7 0.7 copy-start.1
  33.9 6.8 %copy-start.2 = (bf16[9,64,8]{1,2,0:T(8,128)(2,1)S(1)}, bf16[9,64,8]{1,2,0:T(8,128)(2,1)}, u32[]{:S(2)}) copy-start(bf16[9,64,8]{1,2,0:T(8,128)(2,1)} %param.14) | copy-start | bytes 27652
  33.9 7.3 %copy-start.3 = (f32[32]{0:T(128)S(1)}, f32[32]{0:T(128)}, u32[]{:S(2)}) copy-start(f32[32]{0:T(128)} %param.16) | copy-start | bytes 388
  34.0 7.4 %copy-start.4 = (f32[32]{0:T(128)S(1)}, f32[32]{0:T(128)}, u32[]{:S(2)}) copy-start(f32[32]{0:T(128)} %param.15) | copy-start | bytes 388
  34.0 7.5 %copy-start.5 = (f32[32]{0:T(128)S(1)}, f32[32]{0:T(128)}, u32[]{:S(2)}) copy-start(f32[32]{0:T(128)} %param.17) | copy-start | bytes 388
  34.0 37.1 %all-to-all-start.1 = ((f32[128,16,128]{2,1,0:T(8,128)}), f32[128,16,128]{2,1,0:T(8,128)S(1)}, u32[]{:S(2)}, u32[]{:S(2)}) async-start(f32[128,16,128]{2,1,0:T(8,128)} %bitcast.3), calls=%async_computation.1 | async-start | bytes 2097152 | tf_op jit(solution)/shard_map/all_to_all | solution.py:346
  74.0 6.1 %collective-permute-start = (f32[128,128]{1,0:T(8,128)S(1)}, f32[128,128]{1,0:T(8,128)S(1)}, u32[]{:S(2)}, u32[]{:S(2)}) collective-permute-start(f32[128,128]{1,0:T(8,128)S(1)} %all_gather.3.mid_ref), channel_id=1, source_target_pairs={{0,2},{2,4},{4,6},{6,8},{8,10},{10,12},{12,14},{14,30},{30,16},{16... | collective-permute-start | bytes 196616 | tf_op jit(solution)/shard_map/ppermute | solution.py:380
  75.9 6.2 %collective-permute-start.1 = (f32[128,128]{1,0:T(8,128)S(1)}, f32[128,128]{1,0:T(8,128)S(1)}, u32[]{:S(2)}, u32[]{:S(2)}) collective-permute-start(f32[128,128]{1,0:T(8,128)S(1)} %all_gather.3.mid_ref), channel_id=1, source_target_pairs={{2,0},{4,2},{6,4},{8,6},{10,8},{12,10},{14,12},{30,14},{16,30},{18... | collective-permute-start | bytes 196616 | tf_op jit(solution)/shard_map/ppermute | solution.py:381

commit v4 on v3

--- a/solution.py
+++ b/solution.py
@@ -6,10 +6,12 @@
 from jax.sharding import PartitionSpec as P
 
 VIEWS = 5
+STEPS = 16384.0
 PD = 4
 MAXSHIFT = 16
 F32 = jnp.float32
 BF16 = jnp.bfloat16
+UNROLL = 4
 MIB = 1024 * 1024
 TORUS = (4, 4, 8)
 
@@ -26,6 +28,20 @@
 def path():
     nz = TORUS[2]
     return [base + (n - m) % nz for m, base in enumerate(line_bases()) for n in range(nz)]
+
+
+def message_kernel(a_ref, b_ref, c_ref, out_ref, a_s, b_s, c_s, sems):
+    copies = [
+        pltpu.make_async_copy(ref, scratch, sems.at[n])
+        for n, (ref, scratch) in enumerate(((a_ref, a_s), (b_ref, b_s), (c_ref, c_s)))
+    ]
+    for copy in copies:
+        copy.start()
+    for copy in copies:
+        copy.wait()
+    rest = jnp.zeros((1, 128 - 3 * a_s.shape[1]), jnp.int32)
+    row = jnp.concatenate([a_s[...], b_s[...], c_s[...], rest], axis=1)
+    out_ref[...] = jnp.broadcast_to(row, out_ref.shape)
 
 
 def vspec():
@@ -66,9 +82,10 @@
     lax.fori_loop(0, tiles, reorder, 0, unroll=8)
 
 
-def answer_kernel(requests, req_ref, tab_ref, srce_ref, out_ref, codes, table, sem):
+def answer_kernel(requests, req_ref, tab_ref, srce_ref, out_ref, flat_s, codes, table, sem):
     owners = req_ref.shape[0]
-    cols = out_ref.shape[-1]
+    cols = tab_ref.shape[-1]
+    blocks = owners // 8
     me = lax.axis_index("depth")
     flat = req_ref[...].T
     owner = flat[0:requests]
@@ -103,13 +120,22 @@
             for s in range(2):
                 parts.append(one(b * 8 + il, s))
         block = jnp.concatenate(parts, axis=0).T
-        blocks = owners // 8
         for m, base in enumerate(line_bases()):
             turned = pltpu.roll(block[m * 8 : m * 8 + 8], (8 - m) % 8, 0)
-            out_ref[pl.ds(base * blocks + b, 8, stride=blocks), :] = turned
+            flat_s[pl.ds(base * blocks + b, 8, stride=blocks), :] = turned
         return c
 
-    lax.fori_loop(0, owners // 8, step, 0, unroll=2)
+    lax.fori_loop(0, blocks, step, 0, unroll=UNROLL)
+
+    def encode(k, c):
+        number = jnp.round(flat_s[pl.ds(k * blocks, blocks), :] * STEPS).astype(jnp.int32)
+        low = number & 255
+        out_ref[k, 0:blocks, :] = (number >> 8).astype(jnp.int16)
+        pair = low[: blocks // 2] * 256 + low[blocks // 2 :] - 32768
+        out_ref[k, blocks : blocks + blocks // 2, :] = pair.astype(jnp.int16)
+        return c
+
+    lax.fori_loop(0, cols, encode, 0, unroll=8)
 
 
 def table_kernel(requests, req_ref, wd_ref, target_ref, gate_ref, keys):
@@ -167,13 +193,17 @@
 
 def combine_kernel(ans_ref, target_ref, out_ref):
     owners = ans_ref.shape[0]
-    halves = ans_ref.shape[1] // 8
+    halves = target_ref.shape[1] // 8
 
     def step(o, acc):
         acc = list(acc)
         targets = target_ref[o].astype(F32)
+        high = ans_ref[o, 0 : halves * 8, :].astype(jnp.int32)
+        pair = ans_ref[o, halves * 8 : halves * 12, :].astype(jnp.int32) + 32768
+        number = high * 256 + jnp.concatenate([pair >> 8, pair & 255], axis=0)
+        number = number.astype(F32)
         for half in range(halves):
-            data = ans_ref[o, half * 8 : half * 8 + 8, :]
+            data = number[half * 8 : half * 8 + 8]
             target = targets[half * 8 : half * 8 + 8, :]
             for t in range(8):
                 n = t * halves + half
@@ -190,7 +220,9 @@
             b = acc[(2 * p + 1) * halves + half]
             a = a + pltpu.roll(a, 120, 1)
             b = b + pltpu.roll(b, 8, 1)
-            out_ref[pl.ds((p * halves + half) * 8, 8), :] = jnp.where(even, a, b) / (VIEWS * 4.0)
+            out_ref[pl.ds((p * halves + half) * 8, 8), :] = jnp.where(even, a, b) / (
+                VIEWS * 4.0 * STEPS
+            )
 
 
 def column_kernel(left_ref, mid_ref, right_ref, w_ref, bias_ref, wo_ref, out_ref):
@@ -298,15 +330,16 @@
     requests = tile_local.shape[0]
     tiles = src_feat.shape[0]
     blocks = owners // 8
-    shape = (owners, 1, 128)
-    message = jnp.where(
-        lax.broadcasted_iota(jnp.int32, shape, 2) < 3 * requests,
-        0,
-        lax.broadcasted_iota(jnp.int32, shape, 0),
-    )
-    for n, part in enumerate((tile_owner[:, 0], tile_local, col_shift)):
-        wide = jnp.broadcast_to(part[None, None, :], (owners, 1, requests))
-        message += jnp.pad(wide, ((0, 0), (0, 0), (n * requests, 128 - (n + 1) * requests)))
+    message = pl.pallas_call(
+        message_kernel,
+        out_shape=jax.ShapeDtypeStruct((owners, 128), jnp.int32),
+        in_specs=[pl.BlockSpec(memory_space=pltpu.HBM)] * 3,
+        out_specs=vspec(),
+        scratch_shapes=[pltpu.VMEM((1, requests), jnp.int32)] * 3 + [pltpu.SemaphoreType.DMA((3,))],
+        compiler_params=params(60),
+        name="message",
+    )(*[v.reshape(1, requests) for v in (tile_owner, tile_local, col_shift)])
+    message = message.reshape(owners, 1, 128)
     asked = lax.all_to_all(message, "depth", split_axis=0, concat_axis=0, tiled=True)
     asked = asked.reshape(owners, 128)
 
@@ -332,10 +365,11 @@
 
     answers = pl.pallas_call(
         answers_of,
-        out_shape=jax.ShapeDtypeStruct((cols * blocks, 128), F32),
+        out_shape=jax.ShapeDtypeStruct((cols, blocks + blocks // 2, 128), jnp.int16),
         in_specs=[vspec(), vspec(), vspec()],
         out_specs=vspec(),
         scratch_shapes=[
+            pltpu.VMEM((cols * blocks, 128), F32),
             pltpu.VMEM((8, owners), jnp.int32),
             pltpu.SMEM((8, owners), jnp.int32),
             pltpu.SemaphoreType.DMA,
@@ -343,9 +377,7 @@
         compiler_params=params(10),
         name="answer",
     )(asked, table, channels)
-    answers = lax.all_to_all(
-        answers.reshape(cols, blocks, 128), "depth", split_axis=0, concat_axis=0, tiled=True
-    )
+    answers = lax.all_to_all(answers, "depth", split_axis=0, concat_axis=0, tiled=True)
 
     slab = lax.axis_index("slab")
 

time: 105 us -> 97.6 us (0.930)
  waiting for transfers between devices: 36.6 us -> 30.9 us
  local copies, waits for them, and re-layouts: 4.86 us -> 2.74 us
  Pallas kernels: 11.4 us -> 12.8 us
    all_to_all x1, waiting for transfers between devices: 25.9 us -> 20.3 us  [body(): lax.all_to_all(answers, 'depth', split_axis=0, concat_axis=0, tiled=True)]
    pad x3 -> x0, local copies, waits for them, and re-layouts: 2.12 us -> none  [body(): jnp.pad(wide, ((0, 0), (0, 0), (n * requests, 128 - (n + 1) * requests)))]
    pallas_call x1 -> x2, Pallas kernels: 4.37 us -> 5.6 us  [the longest x1 4.2 us: body(): pl.pallas_call(answers_of, out_shape=jax.ShapeDtypeStruct((cols, blocks +...]
where the time goes in v4:
time: 97.6 us; the launch traced here: 96.9 us
  waiting for transfers between devices  30.9 us (32%)
  starting transfers between devices  27.6 us (28%)
  blocking collectives  21.6 us (22%)
  Pallas kernels  12.8 us (13%)
  local copies, waits for them, and re-layouts  2.74 us (3%)
    all_to_all x1, waiting for transfers between devices, body(): lax.all_to_all(answers, 'depth', split_axis=0, concat_axis=0, tiled=True)  20.3 us
    all_to_all x1, blocking collectives, body(): lax.all_to_all(packed.reshape(owners, 1, 128), 'depth', split_axis=0, con...  19.8 us
    all_to_all x1, starting transfers between devices, body(): lax.all_to_all(message, 'depth', split_axis=0, concat_axis=0, tiled=True)  15 us
    all_to_all x1, waiting for transfers between devices, body(): lax.all_to_all(message, 'depth', split_axis=0, concat_axis=0, tiled=True)  8.45 us
    all_to_all x1, starting transfers between devices, body(): lax.all_to_all(answers, 'depth', split_axis=0, concat_axis=0, tiled=True)  6.76 us
    pallas_call x1, Pallas kernels, body(): pl.pallas_call(answers_of, out_shape=jax.ShapeDtypeStruct((cols, blocks +...  4.2 us
    ppermute x1, starting transfers between devices, body(): right = lax.ppermute(both, 'depth', [(b, a) for a, b in pairs])  3.92 us
    pallas_call x1, Pallas kernels, body(): pl.pallas_call(tables_of, out_shape=(jax.ShapeDtypeStruct((owners, blocks...  3.33 us
  transfers between devices with their start and end apart: 4, of which 4 were waited for; matrix products, arithmetic and copies ran while one was open for 1% of the time, Pallas kernels for 4%

profile of v4, /device:TPU:32, one launch (start us, length us, event | category | flops | bytes accessed | tf_op | source)
XLA Modules:
  0.0 96.9 jit_solution(17671757432599640089)
XLA Ops:
  0.6 1.4 %message.1 = s32[128,128]{1,0:T(8,128)} custom-call(s32[1,40]{1,0:T(1,128)} %bitcast.26, s32[1,40]{1,0:T(1,128)} %bitcast.27, s32[1,40]{1,0:T(1,128)} %bitcast.28), custom_call_target="tpu_custom_call" | custom-call | tf_op jit(solution)/shard_map/message/pallas_call | solution.py:333
  2.0 15.0 %all-to-all-start = ((s32[128,1,128]{2,1,0:T(1,128)}), s32[128,1,128]{2,1,0:T(1,128)S(1)}, u32[]{:S(2)}, u32[]{:S(2)}) async-start(s32[128,1,128]{2,1,0:T(1,128)} %bitcast.22), calls=%async_computation | async-start | bytes 131072 | tf_op jit(solution)/shard_map/all_to_all | solution.py:343
  17.1 0.0 copy-start
  17.1 1.3 %copy-done = bf16[160,32,128]{2,1,0:T(8,128)(2,1)S(1)} copy-done((bf16[160,32,128]{2,1,0:T(8,128)(2,1)S(1)}, bf16[160,32,128]{2,1,0:T(8,128)(2,1)}, u32[]{:S(2)}) %copy-start) | copy-done | bytes 1310744
  18.4 0.0 copy-start.1
  18.4 0.7 copy-done.1
  19.1 0.6 prepare.1
  19.8 8.5 %all-to-all-done = s32[128,1,128]{2,1,0:T(1,128)S(1)} async-done(((s32[128,1,128]{2,1,0:T(1,128)}), s32[128,1,128]{2,1,0:T(1,128)S(1)}, u32[]{:S(2)}, u32[]{:S(2)}) %all-to-all-start) | async-done | bytes 65568 | tf_op jit(solution)/shard_map/all_to_all | solution.py:343
  28.2 4.2 %answer.1 = s16[128,24,128]{2,1,0:T(8,128)(2,1)} custom-call(s32[128,128]{1,0:T(8,128)S(1)} %bitcast.18, f32[66,32,128]{2,1,0:T(8,128)S(1)} %get-tuple-element.6.refs_1_, bf16[160,32,128]{2,1,0:T(8,128)(2,1)S(1)} %get-tuple-element.7.refs_2_), custom_call_target="tpu_custom_call" | custom-call | tf_op jit(solution)/shard_map/answer/pallas_call | solution.py:366
  32.4 0.0 copy-start.2
  32.4 0.0 copy-start.3
  32.4 0.0 copy-start.4
  32.5 0.0 copy-start.5
  32.5 6.8 %all-to-all-start.1 = ((s16[128,24,128]{2,1,0:T(8,128)(2,1)}), s16[128,24,128]{2,1,0:T(8,128)(2,1)S(1)}, u32[]{:S(2)}, u32[]{:S(2)}) async-start(s16[128,24,128]{2,1,0:T(8,128)(2,1)} %answer.1), calls=%async_computation.1 | async-start | bytes 1572864 | tf_op jit(solution)/shard_map/all_to_all | solution.py:380
  39.2 0.0 copy-done.2
  39.3 0.1 reshape.199
  39.3 0.2 pad_dynamic-slice_fusion.1
  39.6 0.1 copy.20
  39.6 0.1 reshape.200
  39.8 0.0 copy-done.3
  39.8 0.1 stack_tile.7
  39.9 0.0 copy-done.4
  39.9 0.1 stack_tile.6
  39.9 0.0 copy-done.5
  39.9 0.1 broadcast_in_dim.16
  40.1 0.1 pad_maximum_fusion.refs_1_
  40.1 0.2 compare_select_fusion.wo_ref
  40.4 3.3 %tables.1 = (bf16[128,16,128]{2,1,0:T(8,128)(2,1)S(1)}, bf16[768,1024]{1,0:T(8,128)(2,1)S(1)}) custom-call(s32[128,128]{1,0:T(8,128)S(1)} %bitcast.19, bf16[2,96,128]{2,1,0:T(8,128)(2,1)S(1)} %pad_maximum_fusion.refs_1_), custom_call_target="tpu_custom_call" | custom-call | flops 20000000 | bytes 3000000 | tf_op jit(solution)/shard_map/tables/pallas_call | solution.py:387
  43.7 20.3 %all-to-all-done.1.ans_ref = s16[128,24,128]{2,1,0:T(8,128)(2,1)S(1)} async-done(((s16[128,24,128]{2,1,0:T(8,128)(2,1)}), s16[128,24,128]{2,1,0:T(8,128)(2,1)S(1)}, u32[]{:S(2)}, u32[]{:S(2)}) %all-to-all-start.1) | async-done | bytes 786464 | tf_op jit(solution)/shard_map/all_to_all | solution.py:380
  64.0 1.2 %combine.1 = f32[64,128]{1,0:T(8,128)S(1)} custom-call(s16[128,24,128]{2,1,0:T(8,128)(2,1)S(1)} %all-to-all-done.1.ans_ref, bf16[128,16,128]{2,1,0:T(8,128)(2,1)S(1)} %get-tuple-element.8.target_ref), custom_call_target="tpu_custom_call" | custom-call | tf_op jit(solution)/shard_map/combine/pallas_call | solution.py:401
  65.2 1.9 %all_gather.3.mid_ref = f32[128,128]{1,0:T(8,128)S(1)} all-gather(f32[64,128]{1,0:T(8,128)S(1)} %combine.1), channel_id=1, replica_groups=mesh['depth'=128,'slab'=2] {'slab'}, dimensions={0}, use_global_device_ids=true | all-gather | bytes 98304 | tf_op jit(solution)/shard_map/all_gather | solution.py:409
  67.0 1.9 %collective-permute-start = (f32[128,128]{1,0:T(8,128)S(1)}, f32[128,128]{1,0:T(8,128)S(1)}, u32[]{:S(2)}, u32[]{:S(2)}) collective-permute-start(f32[128,128]{1,0:T(8,128)S(1)} %all_gather.3.mid_ref), channel_id=1, source_target_pairs={{0,2},{2,4},{4,6},{6,8},{8,10},{10,12},{12,14},{14,30},{30,16},{16... | collective-permute-start | bytes 196616 | tf_op jit(solution)/shard_map/ppermute | solution.py:412
  69.0 3.9 %collective-permute-start.1 = (f32[128,128]{1,0:T(8,128)S(1)}, f32[128,128]{1,0:T(8,128)S(1)}, u32[]{:S(2)}, u32[]{:S(2)}) collective-permute-start(f32[128,128]{1,0:T(8,128)S(1)} %all_gather.3.mid_ref), channel_id=1, source_target_pairs={{2,0},{4,2},{6,4},{8,6},{10,8},{12,10},{14,12},{30,14},{16,30},{18... | collective-permute-start | bytes 196616 | tf_op jit(solution)/shard_map/ppermute | solution.py:413
  72.9 0.3 collective-permute-done.left_ref
  73.2 1.9 %collective-permute-done.1.right_ref = f32[128,128]{1,0:T(8,128)S(1)} collective-permute-done((f32[128,128]{1,0:T(8,128)S(1)}, f32[128,128]{1,0:T(8,128)S(1)}, u32[]{:S(2)}, u32[]{:S(2)}) %collective-permute-start.1) | collective-permute-done | bytes 65568 | tf_op jit(solution)/shard_map/ppermute | solution.py:413
  75.1 1.4 %column.1 = f32[128,128]{1,0:T(8,128)S(1)} custom-call(f32[128,128]{1,0:T(8,128)S(1)} %collective-permute-done.left_ref, f32[128,128]{1,0:T(8,128)S(1)} %all_gather.3.mid_ref, f32[128,128]{1,0:T(8,128)S(1)} %collective-permute-done.1.right_ref, bf16[768,1024]{1,0:T(8,128)(2,1)S(1)} %get-tuple-element.9.w_ref, f32[2,512]{1,0:T(2,128)S(1)} %pad_maximum_fusion.1.bias_ref, ...), custom_call_target="tpu_custom_call" | custom-call | tf_op jit(solution)/shard_map/column/pallas_call | solution.py:420
  76.5 19.8 %all_to_all.15 = f32[128,1,128]{2,1,0:T(1,128)S(1)} all-to-all(f32[128,1,128]{2,1,0:T(1,128)S(1)} %bitcast.20), channel_id=1, replica_groups=mesh['depth'=128,'slab'=2] {'depth'}, dimensions={0} | all-to-all | bytes 131072 | tf_op jit(solution)/shard_map/all_to_all | solution.py:428
  96.3 0.7 output.1
  (9 shorter events, 0.1 us)
Async XLA Ops:
  2.0 26.2 %all-to-all-start = ((s32[128,1,128]{2,1,0:T(1,128)}), s32[128,1,128]{2,1,0:T(1,128)S(1)}, u32[]{:S(2)}, u32[]{:S(2)}) async-start(s32[128,1,128]{2,1,0:T(1,128)} %bitcast.22), calls=%async_computation | async-start | bytes 131072 | tf_op jit(solution)/shard_map/all_to_all | solution.py:343
  17.1 1.3 %copy-start = (bf16[160,32,128]{2,1,0:T(8,128)(2,1)S(1)}, bf16[160,32,128]{2,1,0:T(8,128)(2,1)}, u32[]{:S(2)}) copy-start(bf16[160,32,128]{2,1,0:T(8,128)(2,1)} %src_ref.1) | copy-start | bytes 3932164
  18.4 0.7 copy-start.1
  32.4 6.8 %copy-start.2 = (bf16[9,64,8]{1,2,0:T(8,128)(2,1)S(1)}, bf16[9,64,8]{1,2,0:T(8,128)(2,1)}, u32[]{:S(2)}) copy-start(bf16[9,64,8]{1,2,0:T(8,128)(2,1)} %param.14) | copy-start | bytes 27652
  32.4 7.3 %copy-start.3 = (f32[32]{0:T(128)S(1)}, f32[32]{0:T(128)}, u32[]{:S(2)}) copy-start(f32[32]{0:T(128)} %param.16) | copy-start | bytes 388
  32.4 7.4 %copy-start.4 = (f32[32]{0:T(128)S(1)}, f32[32]{0:T(128)}, u32[]{:S(2)}) copy-start(f32[32]{0:T(128)} %param.15) | copy-start | bytes 388
  32.5 7.5 %copy-start.5 = (f32[32]{0:T(128)S(1)}, f32[32]{0:T(128)}, u32[]{:S(2)}) copy-start(f32[32]{0:T(128)} %param.17) | copy-start | bytes 388
  32.5 31.5 %all-to-all-start.1 = ((s16[128,24,128]{2,1,0:T(8,128)(2,1)}), s16[128,24,128]{2,1,0:T(8,128)(2,1)S(1)}, u32[]{:S(2)}, u32[]{:S(2)}) async-start(s16[128,24,128]{2,1,0:T(8,128)(2,1)} %answer.1), calls=%async_computation.1 | async-start | bytes 1572864 | tf_op jit(solution)/shard_map/all_to_all | solution.py:380
  67.0 6.1 %collective-permute-start = (f32[128,128]{1,0:T(8,128)S(1)}, f32[128,128]{1,0:T(8,128)S(1)}, u32[]{:S(2)}, u32[]{:S(2)}) collective-permute-start(f32[128,128]{1,0:T(8,128)S(1)} %all_gather.3.mid_ref), channel_id=1, source_target_pairs={{0,2},{2,4},{4,6},{6,8},{8,10},{10,12},{12,14},{14,30},{30,16},{16... | collective-permute-start | bytes 196616 | tf_op jit(solution)/shard_map/ppermute | solution.py:412
  69.0 6.2 %collective-permute-start.1 = (f32[128,128]{1,0:T(8,128)S(1)}, f32[128,128]{1,0:T(8,128)S(1)}, u32[]{:S(2)}, u32[]{:S(2)}) collective-permute-start(f32[128,128]{1,0:T(8,128)S(1)} %all_gather.3.mid_ref), channel_id=1, source_target_pairs={{2,0},{4,2},{6,4},{8,6},{10,8},{12,10},{14,12},{30,14},{16,30},{18... | collective-permute-start | bytes 196616 | tf_op jit(solution)/shard_map/ppermute | solution.py:413

commit v5 on v4

--- a/solution.py
+++ b/solution.py
@@ -12,6 +12,7 @@
 F32 = jnp.float32
 BF16 = jnp.bfloat16
 UNROLL = 4
+PIECES = 4
 MIB = 1024 * 1024
 TORUS = (4, 4, 8)
 
@@ -20,14 +21,15 @@
     return pltpu.CompilerParams(vmem_limit_bytes=mib * MIB)
 
 
-def line_bases():
+def column_of(k):
     nx, ny, nz = TORUS
-    return [(x * ny + (y - x) % ny) * nz for x in range(nx) for y in range(ny)]
+    x, y, z = k // (ny * nz), (k // nz) % ny, k % nz
+    line = x * ny + y + (x % 2) * (ny - 1 - 2 * y)
+    return line * nz + z + (line % 2) * (nz - 1 - 2 * z)
 
 
 def path():
-    nz = TORUS[2]
-    return [base + (n - m) % nz for m, base in enumerate(line_bases()) for n in range(nz)]
+    return sorted(range(TORUS[0] * TORUS[1] * TORUS[2]), key=column_of)
 
 
 def message_kernel(a_ref, b_ref, c_ref, out_ref, a_s, b_s, c_s, sems):
@@ -82,7 +84,7 @@
     lax.fori_loop(0, tiles, reorder, 0, unroll=8)
 
 
-def answer_kernel(requests, req_ref, tab_ref, srce_ref, out_ref, flat_s, codes, table, sem):
+def answer_kernel(requests, req_ref, tab_ref, srce_ref, out_ref, flat_s, coded_s, codes, table, sem, out_sem):
     owners = req_ref.shape[0]
     cols = tab_ref.shape[-1]
     blocks = owners // 8
@@ -119,23 +121,29 @@
         for il in range(8):
             for s in range(2):
                 parts.append(one(b * 8 + il, s))
-        block = jnp.concatenate(parts, axis=0).T
-        for m, base in enumerate(line_bases()):
-            turned = pltpu.roll(block[m * 8 : m * 8 + 8], (8 - m) % 8, 0)
-            flat_s[pl.ds(base * blocks + b, 8, stride=blocks), :] = turned
+        flat_s[pl.ds(b, cols, stride=blocks), :] = jnp.concatenate(parts, axis=0).T
         return c
 
     lax.fori_loop(0, blocks, step, 0, unroll=UNROLL)
 
     def encode(k, c):
-        number = jnp.round(flat_s[pl.ds(k * blocks, blocks), :] * STEPS).astype(jnp.int32)
+        start = pl.multiple_of(column_of(k) * blocks, blocks)
+        number = jnp.round(flat_s[pl.ds(start, blocks), :] * STEPS).astype(jnp.int32)
         low = number & 255
-        out_ref[k, 0:blocks, :] = (number >> 8).astype(jnp.int16)
+        coded_s[k, 0:blocks, :] = (number >> 8).astype(jnp.int16)
         pair = low[: blocks // 2] * 256 + low[blocks // 2 :] - 32768
-        out_ref[k, blocks : blocks + blocks // 2, :] = pair.astype(jnp.int16)
+        coded_s[k, blocks : blocks + blocks // 2, :] = pair.astype(jnp.int16)
         return c
 
-    lax.fori_loop(0, cols, encode, 0, unroll=8)
+    size = cols // PIECES
+    copies = []
+    for n in range(PIECES):
+        lax.fori_loop(n * size, (n + 1) * size, encode, 0, unroll=8)
+        piece = pl.ds(n * size, size)
+        copies.append(pltpu.make_async_copy(coded_s.at[piece], out_ref.at[piece], out_sem.at[n]))
+        copies[-1].start()
+    for copy in copies:
+        copy.wait()
 
 
 def table_kernel(requests, req_ref, wd_ref, target_ref, gate_ref, keys):
@@ -307,9 +315,10 @@
             ]
 
 
-def output_kernel(x_ref, prob_ref, map_ref):
-    lines = [pltpu.roll(x_ref[pl.ds(b, 8), :], m % 8, 0) for m, b in enumerate(line_bases())]
-    t = jnp.concatenate(lines, axis=0).T
+def output_kernel(x_ref, prob_ref, map_ref, ordered):
+    for column, k in enumerate(path()):
+        ordered[column : column + 1, :] = x_ref[k : k + 1, :]
+    t = ordered[...].T
     for p in range(PD):
         prob_ref[p] = t[p * 2 : p * 2 + 2]
     map_ref[...] = t[8:10]
@@ -367,12 +376,14 @@
         answers_of,
         out_shape=jax.ShapeDtypeStruct((cols, blocks + blocks // 2, 128), jnp.int16),
         in_specs=[vspec(), vspec(), vspec()],
-        out_specs=vspec(),
+        out_specs=pl.BlockSpec(memory_space=pl.ANY),
         scratch_shapes=[
             pltpu.VMEM((cols * blocks, 128), F32),
+            pltpu.VMEM((cols, blocks + blocks // 2, 128), jnp.int16),
             pltpu.VMEM((8, owners), jnp.int32),
             pltpu.SMEM((8, owners), jnp.int32),
             pltpu.SemaphoreType.DMA,
+            pltpu.SemaphoreType.DMA((PIECES,)),
         ],
         compiler_params=params(10),
         name="answer",
@@ -436,6 +447,7 @@
         ),
         in_specs=[vspec()],
         out_specs=(vspec(), vspec()),
+        scratch_shapes=[pltpu.VMEM((cols, 128), F32)],
         compiler_params=params(4),
         name="output",
     )(packed.reshape(cols, 128))

time: 97.6 us -> 100 us (1.025)
  Pallas kernels: 12.8 us -> 14.9 us
    pallas_call x1, Pallas kernels: 4.2 us -> 6.19 us  [body(): pl.pallas_call(answers_of, out_shape=jax.ShapeDtypeStruct((cols, blocks +...]
where the time goes in v5:
time: 100 us; the launch traced here: 99.8 us
  waiting for transfers between devices  30.9 us (31%)
  starting transfers between devices  27.6 us (28%)
  blocking collectives  22.5 us (22%)
  Pallas kernels  14.9 us (15%)
  local copies, waits for them, and re-layouts  2.74 us (3%)
    all_to_all x1, blocking collectives, body(): lax.all_to_all(packed.reshape(owners, 1, 128), 'depth', split_axis=0, con...  20.6 us
    all_to_all x1, waiting for transfers between devices, body(): lax.all_to_all(answers, 'depth', split_axis=0, concat_axis=0, tiled=True)  20.3 us
    all_to_all x1, starting transfers between devices, body(): lax.all_to_all(message, 'depth', split_axis=0, concat_axis=0, tiled=True)  15 us
    all_to_all x1, waiting for transfers between devices, body(): lax.all_to_all(message, 'depth', split_axis=0, concat_axis=0, tiled=True)  8.45 us
    all_to_all x1, starting transfers between devices, body(): lax.all_to_all(answers, 'depth', split_axis=0, concat_axis=0, tiled=True)  6.76 us
    pallas_call x1, Pallas kernels, body(): pl.pallas_call(answers_of, out_shape=jax.ShapeDtypeStruct((cols, blocks +...  6.19 us
    ppermute x1, starting transfers between devices, body(): right = lax.ppermute(both, 'depth', [(b, a) for a, b in pairs])  3.92 us
    pallas_call x1, Pallas kernels, body(): pl.pallas_call(tables_of, out_shape=(jax.ShapeDtypeStruct((owners, blocks...  3.33 us
  transfers between devices with their start and end apart: 4, of which 4 were waited for; matrix products, arithmetic and copies ran while one was open for 1% of the time, Pallas kernels for 4%

profile of v5, /device:TPU:32, one launch (start us, length us, event | category | flops | bytes accessed | tf_op | source)
XLA Modules:
  0.0 99.8 jit_solution(3180094591035508393)
XLA Ops:
  0.6 1.4 %message.1 = s32[128,128]{1,0:T(8,128)} custom-call(s32[1,40]{1,0:T(1,128)} %bitcast.26, s32[1,40]{1,0:T(1,128)} %bitcast.27, s32[1,40]{1,0:T(1,128)} %bitcast.28), custom_call_target="tpu_custom_call" | custom-call | tf_op jit(solution)/shard_map/message/pallas_call | solution.py:342
  2.0 15.0 %all-to-all-start = ((s32[128,1,128]{2,1,0:T(1,128)}), s32[128,1,128]{2,1,0:T(1,128)S(1)}, u32[]{:S(2)}, u32[]{:S(2)}) async-start(s32[128,1,128]{2,1,0:T(1,128)} %bitcast.22), calls=%async_computation | async-start | bytes 131072 | tf_op jit(solution)/shard_map/all_to_all | solution.py:352
  17.1 0.0 copy-start
  17.1 1.3 %copy-done = bf16[160,32,128]{2,1,0:T(8,128)(2,1)S(1)} copy-done((bf16[160,32,128]{2,1,0:T(8,128)(2,1)S(1)}, bf16[160,32,128]{2,1,0:T(8,128)(2,1)}, u32[]{:S(2)}) %copy-start) | copy-done | bytes 1310744
  18.4 0.0 copy-start.1
  18.4 0.7 copy-done.1
  19.1 0.6 prepare.1
  19.8 8.5 %all-to-all-done = s32[128,1,128]{2,1,0:T(1,128)S(1)} async-done(((s32[128,1,128]{2,1,0:T(1,128)}), s32[128,1,128]{2,1,0:T(1,128)S(1)}, u32[]{:S(2)}, u32[]{:S(2)}) %all-to-all-start) | async-done | bytes 65568 | tf_op jit(solution)/shard_map/all_to_all | solution.py:352
  28.2 6.2 %answer.1 = s16[128,24,128]{2,1,0:T(8,128)(2,1)} custom-call(s32[128,128]{1,0:T(8,128)S(1)} %bitcast.18, f32[66,32,128]{2,1,0:T(8,128)S(1)} %get-tuple-element.6.refs_1_, bf16[160,32,128]{2,1,0:T(8,128)(2,1)S(1)} %get-tuple-element.7.refs_2_), custom_call_target="tpu_custom_call" | custom-call | tf_op jit(solution)/shard_map/answer/pallas_call | solution.py:375
  34.4 0.0 copy-start.2
  34.4 0.0 copy-start.3
  34.4 0.0 copy-start.4
  34.4 0.0 copy-start.5
  34.5 6.8 %all-to-all-start.1 = ((s16[128,24,128]{2,1,0:T(8,128)(2,1)}), s16[128,24,128]{2,1,0:T(8,128)(2,1)S(1)}, u32[]{:S(2)}, u32[]{:S(2)}) async-start(s16[128,24,128]{2,1,0:T(8,128)(2,1)} %answer.1), calls=%async_computation.1 | async-start | bytes 1572864 | tf_op jit(solution)/shard_map/all_to_all | solution.py:391
  41.2 0.0 copy-done.2
  41.2 0.1 reshape.199
  41.3 0.2 pad_dynamic-slice_fusion.1
  41.6 0.1 copy.20
  41.6 0.1 reshape.200
  41.8 0.0 copy-done.3
  41.8 0.1 stack_tile.7
  41.9 0.0 copy-done.4
  41.9 0.1 stack_tile.6
  41.9 0.0 copy-done.5
  41.9 0.1 broadcast_in_dim.16
  42.0 0.1 pad_maximum_fusion.refs_1_
  42.1 0.2 compare_select_fusion.wo_ref
  42.3 3.3 %tables.1 = (bf16[128,16,128]{2,1,0:T(8,128)(2,1)S(1)}, bf16[768,1024]{1,0:T(8,128)(2,1)S(1)}) custom-call(s32[128,128]{1,0:T(8,128)S(1)} %bitcast.19, bf16[2,96,128]{2,1,0:T(8,128)(2,1)S(1)} %pad_maximum_fusion.refs_1_), custom_call_target="tpu_custom_call" | custom-call | flops 20000000 | bytes 3000000 | tf_op jit(solution)/shard_map/tables/pallas_call | solution.py:398
  45.7 20.3 %all-to-all-done.1.ans_ref = s16[128,24,128]{2,1,0:T(8,128)(2,1)S(1)} async-done(((s16[128,24,128]{2,1,0:T(8,128)(2,1)}), s16[128,24,128]{2,1,0:T(8,128)(2,1)S(1)}, u32[]{:S(2)}, u32[]{:S(2)}) %all-to-all-start.1) | async-done | bytes 786464 | tf_op jit(solution)/shard_map/all_to_all | solution.py:391
  65.9 1.2 %combine.1 = f32[64,128]{1,0:T(8,128)S(1)} custom-call(s16[128,24,128]{2,1,0:T(8,128)(2,1)S(1)} %all-to-all-done.1.ans_ref, bf16[128,16,128]{2,1,0:T(8,128)(2,1)S(1)} %get-tuple-element.8.target_ref), custom_call_target="tpu_custom_call" | custom-call | tf_op jit(solution)/shard_map/combine/pallas_call | solution.py:412
  67.2 1.9 %all_gather.3.mid_ref = f32[128,128]{1,0:T(8,128)S(1)} all-gather(f32[64,128]{1,0:T(8,128)S(1)} %combine.1), channel_id=1, replica_groups=mesh['depth'=128,'slab'=2] {'slab'}, dimensions={0}, use_global_device_ids=true | all-gather | bytes 98304 | tf_op jit(solution)/shard_map/all_gather | solution.py:420
  69.0 1.9 %collective-permute-start = (f32[128,128]{1,0:T(8,128)S(1)}, f32[128,128]{1,0:T(8,128)S(1)}, u32[]{:S(2)}, u32[]{:S(2)}) collective-permute-start(f32[128,128]{1,0:T(8,128)S(1)} %all_gather.3.mid_ref), channel_id=1, source_target_pairs={{0,2},{2,4},{4,6},{6,8},{8,10},{10,12},{12,14},{14,30},{30,28},{28... | collective-permute-start | bytes 196616 | tf_op jit(solution)/shard_map/ppermute | solution.py:423
  71.0 3.9 %collective-permute-start.1 = (f32[128,128]{1,0:T(8,128)S(1)}, f32[128,128]{1,0:T(8,128)S(1)}, u32[]{:S(2)}, u32[]{:S(2)}) collective-permute-start(f32[128,128]{1,0:T(8,128)S(1)} %all_gather.3.mid_ref), channel_id=1, source_target_pairs={{2,0},{4,2},{6,4},{8,6},{10,8},{12,10},{14,12},{30,14},{28,30},{26... | collective-permute-start | bytes 196616 | tf_op jit(solution)/shard_map/ppermute | solution.py:424
  74.9 0.3 collective-permute-done.left_ref
  75.2 1.9 %collective-permute-done.1.right_ref = f32[128,128]{1,0:T(8,128)S(1)} collective-permute-done((f32[128,128]{1,0:T(8,128)S(1)}, f32[128,128]{1,0:T(8,128)S(1)}, u32[]{:S(2)}, u32[]{:S(2)}) %collective-permute-start.1) | collective-permute-done | bytes 65568 | tf_op jit(solution)/shard_map/ppermute | solution.py:424
  77.1 1.4 %column.1 = f32[128,128]{1,0:T(8,128)S(1)} custom-call(f32[128,128]{1,0:T(8,128)S(1)} %collective-permute-done.left_ref, f32[128,128]{1,0:T(8,128)S(1)} %all_gather.3.mid_ref, f32[128,128]{1,0:T(8,128)S(1)} %collective-permute-done.1.right_ref, bf16[768,1024]{1,0:T(8,128)(2,1)S(1)} %get-tuple-element.9.w_ref, f32[2,512]{1,0:T(2,128)S(1)} %pad_maximum_fusion.1.bias_ref, ...), custom_call_target="tpu_custom_call" | custom-call | tf_op jit(solution)/shard_map/column/pallas_call | solution.py:431
  78.5 20.6 %all_to_all.15 = f32[128,1,128]{2,1,0:T(1,128)S(1)} all-to-all(f32[128,1,128]{2,1,0:T(1,128)S(1)} %bitcast.20), channel_id=1, replica_groups=mesh['depth'=128,'slab'=2] {'depth'}, dimensions={0} | all-to-all | bytes 131072 | tf_op jit(solution)/shard_map/all_to_all | solution.py:439
  99.1 0.7 output.1
  (9 shorter events, 0.1 us)
Async XLA Ops:
  2.0 26.2 %all-to-all-start = ((s32[128,1,128]{2,1,0:T(1,128)}), s32[128,1,128]{2,1,0:T(1,128)S(1)}, u32[]{:S(2)}, u32[]{:S(2)}) async-start(s32[128,1,128]{2,1,0:T(1,128)} %bitcast.22), calls=%async_computation | async-start | bytes 131072 | tf_op jit(solution)/shard_map/all_to_all | solution.py:352
  17.1 1.3 %copy-start = (bf16[160,32,128]{2,1,0:T(8,128)(2,1)S(1)}, bf16[160,32,128]{2,1,0:T(8,128)(2,1)}, u32[]{:S(2)}) copy-start(bf16[160,32,128]{2,1,0:T(8,128)(2,1)} %src_ref.1) | copy-start | bytes 3932164
  18.4 0.7 copy-start.1
  34.4 6.8 %copy-start.2 = (bf16[9,64,8]{1,2,0:T(8,128)(2,1)S(1)}, bf16[9,64,8]{1,2,0:T(8,128)(2,1)}, u32[]{:S(2)}) copy-start(bf16[9,64,8]{1,2,0:T(8,128)(2,1)} %param.14) | copy-start | bytes 27652
  34.4 7.3 %copy-start.3 = (f32[32]{0:T(128)S(1)}, f32[32]{0:T(128)}, u32[]{:S(2)}) copy-start(f32[32]{0:T(128)} %param.16) | copy-start | bytes 388
  34.4 7.4 %copy-start.4 = (f32[32]{0:T(128)S(1)}, f32[32]{0:T(128)}, u32[]{:S(2)}) copy-start(f32[32]{0:T(128)} %param.15) | copy-start | bytes 388
  34.4 7.5 %copy-start.5 = (f32[32]{0:T(128)S(1)}, f32[32]{0:T(128)}, u32[]{:S(2)}) copy-start(f32[32]{0:T(128)} %param.17) | copy-start | bytes 388
  34.5 31.5 %all-to-all-start.1 = ((s16[128,24,128]{2,1,0:T(8,128)(2,1)}), s16[128,24,128]{2,1,0:T(8,128)(2,1)S(1)}, u32[]{:S(2)}, u32[]{:S(2)}) async-start(s16[128,24,128]{2,1,0:T(8,128)(2,1)} %answer.1), calls=%async_computation.1 | async-start | bytes 1572864 | tf_op jit(solution)/shard_map/all_to_all | solution.py:391
  69.0 6.1 %collective-permute-start = (f32[128,128]{1,0:T(8,128)S(1)}, f32[128,128]{1,0:T(8,128)S(1)}, u32[]{:S(2)}, u32[]{:S(2)}) collective-permute-start(f32[128,128]{1,0:T(8,128)S(1)} %all_gather.3.mid_ref), channel_id=1, source_target_pairs={{0,2},{2,4},{4,6},{6,8},{8,10},{10,12},{12,14},{14,30},{30,28},{28... | collective-permute-start | bytes 196616 | tf_op jit(solution)/shard_map/ppermute | solution.py:423
  71.0 6.2 %collective-permute-start.1 = (f32[128,128]{1,0:T(8,128)S(1)}, f32[128,128]{1,0:T(8,128)S(1)}, u32[]{:S(2)}, u32[]{:S(2)}) collective-permute-start(f32[128,128]{1,0:T(8,128)S(1)} %all_gather.3.mid_ref), channel_id=1, source_target_pairs={{2,0},{4,2},{6,4},{8,6},{10,8},{12,10},{14,12},{30,14},{28,30},{26... | collective-permute-start | bytes 196616 | tf_op jit(solution)/shard_map/ppermute | solution.py:424

commit v6 on v5

--- a/solution.py
+++ b/solution.py
@@ -11,7 +11,7 @@
 MAXSHIFT = 16
 F32 = jnp.float32
 BF16 = jnp.bfloat16
-UNROLL = 4
+UNROLL = 8
 PIECES = 4
 MIB = 1024 * 1024
 TORUS = (4, 4, 8)
@@ -24,8 +24,8 @@
 def column_of(k):
     nx, ny, nz = TORUS
     x, y, z = k // (ny * nz), (k // nz) % ny, k % nz
-    line = x * ny + y + (x % 2) * (ny - 1 - 2 * y)
-    return line * nz + z + (line % 2) * (nz - 1 - 2 * z)
+    place = x * ny + (ny - 1 - y if x % 2 else y)
+    return z * nx * ny + (nx * ny - 1 - place if z % 2 else place)
 
 
 def path():
@@ -126,19 +126,16 @@
 
     lax.fori_loop(0, blocks, step, 0, unroll=UNROLL)
 
-    def encode(k, c):
-        start = pl.multiple_of(column_of(k) * blocks, blocks)
-        number = jnp.round(flat_s[pl.ds(start, blocks), :] * STEPS).astype(jnp.int32)
-        low = number & 255
-        coded_s[k, 0:blocks, :] = (number >> 8).astype(jnp.int16)
-        pair = low[: blocks // 2] * 256 + low[blocks // 2 :] - 32768
-        coded_s[k, blocks : blocks + blocks // 2, :] = pair.astype(jnp.int16)
-        return c
-
     size = cols // PIECES
     copies = []
     for n in range(PIECES):
-        lax.fori_loop(n * size, (n + 1) * size, encode, 0, unroll=8)
+        for k in range(n * size, (n + 1) * size):
+            start = column_of(k) * blocks
+            number = jnp.round(flat_s[start : start + blocks, :] * STEPS).astype(jnp.int32)
+            low = number & 255
+            coded_s[k, 0:blocks, :] = (number >> 8).astype(jnp.int16)
+            pair = low[: blocks // 2] * 256 + low[blocks // 2 :] - 32768
+            coded_s[k, blocks : blocks + blocks // 2, :] = pair.astype(jnp.int16)
         piece = pl.ds(n * size, size)
         copies.append(pltpu.make_async_copy(coded_s.at[piece], out_ref.at[piece], out_sem.at[n]))
         copies[-1].start()
@@ -233,11 +230,11 @@
             )
 
 
-def column_kernel(left_ref, mid_ref, right_ref, w_ref, bias_ref, wo_ref, out_ref):
+def column_kernel(first_ref, mid_ref, second_ref, w_ref, bias_ref, wo_ref, out_ref):
     rows = mid_ref.shape[0] // 2
     blocks = rows // PD
     x = jnp.concatenate(
-        [ref[pl.ds(j * rows, rows), :] for ref in (left_ref, mid_ref, right_ref) for j in range(2)],
+        [ref[pl.ds(j * rows, rows), :] for ref in (first_ref, mid_ref, second_ref) for j in range(2)],
         axis=1,
     )
     hi = x.astype(BF16)
@@ -324,11 +321,12 @@
     map_ref[...] = t[8:10]
 
 
-def gate_rows(w_gates, slab):
+def gate_rows(w_gates, slab, odd):
     w = w_gates.reshape(3, 3, 2, 32, 8).transpose(0, 1, 4, 2, 3)
     w = jnp.pad(w, ((2, 2), (0, 0), (0, 0), (0, 0), (0, 0)))
     by_row = [lax.dynamic_slice_in_dim(w, 3 - r - 2 * slab, 4, axis=0) for r in range(2)]
     v = jnp.stack(by_row, axis=4).reshape(2, 2, 3, 8, 2, 2, 32)
+    v = jnp.where(odd, v[:, :, ::-1], v)
     v = v.transpose(4, 2, 0, 1, 3, 5, 6).reshape(2, 96, 64)
     return jnp.concatenate([v, v], axis=2)
 
@@ -391,6 +389,8 @@
     answers = lax.all_to_all(answers, "depth", split_axis=0, concat_axis=0, tiled=True)
 
     slab = lax.axis_index("slab")
+    depth = lax.axis_index("depth")
+    odd = (depth // (TORUS[1] * TORUS[2]) + depth // TORUS[2] + depth) % 2 == 1
 
     def tables_of(*refs):
         table_kernel(requests, *refs)
@@ -407,7 +407,7 @@
         compiler_params=params(8),
         cost_estimate=pl.CostEstimate(flops=20000000, transcendentals=0, bytes_accessed=3000000),
         name="tables",
-    )(asked, gate_rows(w_gates, slab))
+    )(asked, gate_rows(w_gates, slab, odd))
 
     cost = pl.pallas_call(
         combine_kernel,
@@ -419,9 +419,12 @@
     )(answers, targets)
     both = lax.all_gather(cost, "slab", tiled=True)
     chips = path()
-    pairs = list(zip(chips[:-1], chips[1:]))
-    left = lax.ppermute(both, "depth", pairs)
-    right = lax.ppermute(both, "depth", [(b, a) for a, b in pairs])
+
+    def exchange(start):
+        pairs = [(chips[i], chips[i + 1]) for i in range(start, owners - 1, 2)]
+        return lax.ppermute(both, "depth", pairs + [(b, a) for a, b in pairs])
+
+    first, second = exchange(1), exchange(0)
 
     bias = jnp.stack([jnp.tile(bias_z, 16), jnp.tile(bias_c, 16)])
     unit_row = jnp.arange(512, dtype=jnp.int32)[:, None] // 32
@@ -435,7 +438,7 @@
         out_specs=vspec(),
         compiler_params=params(10),
         name="column",
-    )(left, both, right, gates, bias, project)
+    )(first, both, second, gates, bias, project)
     packed = lax.all_to_all(
         packed.reshape(owners, 1, 128), "depth", split_axis=0, concat_axis=0, tiled=True
     )

time: 100 us -> 93.8 us (0.938)
  starting transfers between devices: 27.6 us -> 24.1 us
  Pallas kernels: 14.9 us -> 12.4 us
  blocking collectives: 22.5 us -> 20.1 us
  waiting for transfers between devices: 30.9 us -> 32.5 us
    ppermute x2, starting transfers between devices: 5.83 us -> 2.38 us  [exchange(): return lax.ppermute(both, 'depth', pairs + [(b, a) for a, b in pairs])]
    pallas_call x1, Pallas kernels: 6.19 us -> 3.74 us  [body(): pl.pallas_call(answers_of, out_shape=jax.ShapeDtypeStruct((cols, blocks +...]
    all_to_all x1, blocking collectives: 20.6 us -> 18.2 us  [body(): lax.all_to_all(packed.reshape(owners, 1, 128), 'depth', split_axis=0, con...]
    ppermute x2, waiting for transfers between devices: 2.21 us -> 3.88 us  [exchange(): return lax.ppermute(both, 'depth', pairs + [(b, a) for a, b in pairs])]
where the time goes in v6:
time: 93.8 us; the launch traced here: 93.2 us
  waiting for transfers between devices  32.5 us (35%)
  starting transfers between devices  24.1 us (26%)
  blocking collectives  20.1 us (21%)
  Pallas kernels  12.4 us (13%)
  local copies, waits for them, and re-layouts  2.74 us (3%)
    all_to_all x1, waiting for transfers between devices, body(): lax.all_to_all(answers, 'depth', split_axis=0, concat_axis=0, tiled=True)  20.2 us
    all_to_all x1, blocking collectives, body(): lax.all_to_all(packed.reshape(owners, 1, 128), 'depth', split_axis=0, con...  18.2 us
    all_to_all x1, starting transfers between devices, body(): lax.all_to_all(message, 'depth', split_axis=0, concat_axis=0, tiled=True)  15 us
    all_to_all x1, waiting for transfers between devices, body(): lax.all_to_all(message, 'depth', split_axis=0, concat_axis=0, tiled=True)  8.45 us
    all_to_all x1, starting transfers between devices, body(): lax.all_to_all(answers, 'depth', split_axis=0, concat_axis=0, tiled=True)  6.76 us
    ppermute x2, waiting for transfers between devices, exchange(): return lax.ppermute(both, 'depth', pairs + [(b, a) for a, b in pairs])  3.88 us
    pallas_call x1, Pallas kernels, body(): pl.pallas_call(answers_of, out_shape=jax.ShapeDtypeStruct((cols, blocks +...  3.74 us
    pallas_call x1, Pallas kernels, body(): pl.pallas_call(tables_of, out_shape=(jax.ShapeDtypeStruct((owners, blocks...  3.33 us
  transfers between devices with their start and end apart: 4, of which 4 were waited for; matrix products, arithmetic and copies ran while one was open for 1% of the time, Pallas kernels for 4%

profile of v6, /device:TPU:32, one launch (start us, length us, event | category | flops | bytes accessed | tf_op | source)
XLA Modules:
  0.0 93.2 jit_solution(2091727885399632320)
XLA Ops:
  0.6 1.4 %message.1 = s32[128,128]{1,0:T(8,128)} custom-call(s32[1,40]{1,0:T(1,128)} %bitcast.26, s32[1,40]{1,0:T(1,128)} %bitcast.27, s32[1,40]{1,0:T(1,128)} %bitcast.28), custom_call_target="tpu_custom_call" | custom-call | tf_op jit(solution)/shard_map/message/pallas_call | solution.py:340
  2.0 15.0 %all-to-all-start = ((s32[128,1,128]{2,1,0:T(1,128)}), s32[128,1,128]{2,1,0:T(1,128)S(1)}, u32[]{:S(2)}, u32[]{:S(2)}) async-start(s32[128,1,128]{2,1,0:T(1,128)} %bitcast.22), calls=%async_computation | async-start | bytes 131072 | tf_op jit(solution)/shard_map/all_to_all | solution.py:350
  17.1 0.0 copy-start
  17.1 1.3 %copy-done = bf16[160,32,128]{2,1,0:T(8,128)(2,1)S(1)} copy-done((bf16[160,32,128]{2,1,0:T(8,128)(2,1)S(1)}, bf16[160,32,128]{2,1,0:T(8,128)(2,1)}, u32[]{:S(2)}) %copy-start) | copy-done | bytes 1310744
  18.4 0.0 copy-start.1
  18.4 0.7 copy-done.1
  19.1 0.6 prepare.1
  19.8 8.5 %all-to-all-done = s32[128,1,128]{2,1,0:T(1,128)S(1)} async-done(((s32[128,1,128]{2,1,0:T(1,128)}), s32[128,1,128]{2,1,0:T(1,128)S(1)}, u32[]{:S(2)}, u32[]{:S(2)}) %all-to-all-start) | async-done | bytes 65568 | tf_op jit(solution)/shard_map/all_to_all | solution.py:350
  28.2 3.7 %answer.1 = s16[128,24,128]{2,1,0:T(8,128)(2,1)} custom-call(s32[128,128]{1,0:T(8,128)S(1)} %bitcast.18, f32[66,32,128]{2,1,0:T(8,128)S(1)} %get-tuple-element.6.refs_1_, bf16[160,32,128]{2,1,0:T(8,128)(2,1)S(1)} %get-tuple-element.7.refs_2_), custom_call_target="tpu_custom_call" | custom-call | tf_op jit(solution)/shard_map/answer/pallas_call | solution.py:373
  32.0 0.0 copy-start.2
  32.0 0.0 copy-start.3
  32.0 0.0 copy-start.4
  32.0 0.0 copy-start.5
  32.0 6.8 %all-to-all-start.1 = ((s16[128,24,128]{2,1,0:T(8,128)(2,1)}), s16[128,24,128]{2,1,0:T(8,128)(2,1)S(1)}, u32[]{:S(2)}, u32[]{:S(2)}) async-start(s16[128,24,128]{2,1,0:T(8,128)(2,1)} %answer.1), calls=%async_computation.1 | async-start | bytes 1572864 | tf_op jit(solution)/shard_map/all_to_all | solution.py:389
  38.8 0.0 copy-done.2
  38.8 0.1 reshape.199
  38.9 0.2 pad_dynamic-slice_fusion.1
  39.2 0.1 copy.20
  39.3 0.1 reshape.200
  39.4 0.0 copy-done.3
  39.4 0.1 stack_tile.7
  39.5 0.0 copy-done.4
  39.5 0.1 stack_tile.6
  39.6 0.0 copy-done.5
  39.6 0.1 broadcast_in_dim.16
  39.7 0.1 pad_maximum_fusion.1.refs_1_
  39.8 0.2 compare_select_fusion.wo_ref
  40.0 3.3 %tables.1 = (bf16[128,16,128]{2,1,0:T(8,128)(2,1)S(1)}, bf16[768,1024]{1,0:T(8,128)(2,1)S(1)}) custom-call(s32[128,128]{1,0:T(8,128)S(1)} %bitcast.19, bf16[2,96,128]{2,1,0:T(8,128)(2,1)S(1)} %pad_maximum_fusion.1.refs_1_), custom_call_target="tpu_custom_call" | custom-call | flops 20000000 | bytes 3000000 | tf_op jit(solution)/shard_map/tables/pallas_call | solution.py:398
  43.3 20.2 %all-to-all-done.1.ans_ref = s16[128,24,128]{2,1,0:T(8,128)(2,1)S(1)} async-done(((s16[128,24,128]{2,1,0:T(8,128)(2,1)}), s16[128,24,128]{2,1,0:T(8,128)(2,1)S(1)}, u32[]{:S(2)}, u32[]{:S(2)}) %all-to-all-start.1) | async-done | bytes 786464 | tf_op jit(solution)/shard_map/all_to_all | solution.py:389
  63.5 1.2 %combine.1 = f32[64,128]{1,0:T(8,128)S(1)} custom-call(s16[128,24,128]{2,1,0:T(8,128)(2,1)S(1)} %all-to-all-done.1.ans_ref, bf16[128,16,128]{2,1,0:T(8,128)(2,1)S(1)} %get-tuple-element.8.target_ref), custom_call_target="tpu_custom_call" | custom-call | tf_op jit(solution)/shard_map/combine/pallas_call | solution.py:412
  64.7 1.9 %all_gather.3.mid_ref = f32[128,128]{1,0:T(8,128)S(1)} all-gather(f32[64,128]{1,0:T(8,128)S(1)} %combine.1), channel_id=1, replica_groups=mesh['depth'=128,'slab'=2] {'slab'}, dimensions={0}, use_global_device_ids=true | all-gather | bytes 98304 | tf_op jit(solution)/shard_map/all_gather | solution.py:420
  66.6 1.9 %collective-permute-start = (f32[128,128]{1,0:T(8,128)S(1)}, f32[128,128]{1,0:T(8,128)S(1)}, u32[]{:S(2)}, u32[]{:S(2)}) collective-permute-start(f32[128,128]{1,0:T(8,128)S(1)} %all_gather.3.mid_ref), channel_id=1, source_target_pairs={{16,32},{48,112},{96,80},{64,128},{144,160},{176,240},{224,208},{1... | collective-permute-start | bytes 196616 | tf_op jit(solution)/shard_map/ppermute | solution.py:425
  68.5 0.5 collective-permute-start.1
  69.0 3.8 %collective-permute-done.first_ref = f32[128,128]{1,0:T(8,128)S(1)} collective-permute-done((f32[128,128]{1,0:T(8,128)S(1)}, f32[128,128]{1,0:T(8,128)S(1)}, u32[]{:S(2)}, u32[]{:S(2)}) %collective-permute-start) | collective-permute-done | bytes 65568 | tf_op jit(solution)/shard_map/ppermute | solution.py:425
  72.7 0.1 collective-permute-done.1.second_ref
  72.9 1.4 %column.1 = f32[128,128]{1,0:T(8,128)S(1)} custom-call(f32[128,128]{1,0:T(8,128)S(1)} %collective-permute-done.first_ref, f32[128,128]{1,0:T(8,128)S(1)} %all_gather.3.mid_ref, f32[128,128]{1,0:T(8,128)S(1)} %collective-permute-done.1.second_ref, bf16[768,1024]{1,0:T(8,128)(2,1)S(1)} %get-tuple-element.9.w_ref, f32[2,512]{1,0:T(2,128)S(1)} %pad_maximum_fusion.2.bias_ref, ...), custom_call_target="tpu_custom_call" | custom-call | tf_op jit(solution)/shard_map/column/pallas_call | solution.py:434
  74.2 18.2 %all_to_all.15 = f32[128,1,128]{2,1,0:T(1,128)S(1)} all-to-all(f32[128,1,128]{2,1,0:T(1,128)S(1)} %bitcast.20), channel_id=1, replica_groups=mesh['depth'=128,'slab'=2] {'depth'}, dimensions={0} | all-to-all | bytes 131072 | tf_op jit(solution)/shard_map/all_to_all | solution.py:442
  92.5 0.7 output.1
  (10 shorter events, 0.1 us)
Async XLA Ops:
  2.0 26.2 %all-to-all-start = ((s32[128,1,128]{2,1,0:T(1,128)}), s32[128,1,128]{2,1,0:T(1,128)S(1)}, u32[]{:S(2)}, u32[]{:S(2)}) async-start(s32[128,1,128]{2,1,0:T(1,128)} %bitcast.22), calls=%async_computation | async-start | bytes 131072 | tf_op jit(solution)/shard_map/all_to_all | solution.py:350
  17.1 1.3 %copy-start = (bf16[160,32,128]{2,1,0:T(8,128)(2,1)S(1)}, bf16[160,32,128]{2,1,0:T(8,128)(2,1)}, u32[]{:S(2)}) copy-start(bf16[160,32,128]{2,1,0:T(8,128)(2,1)} %src_ref.1) | copy-start | bytes 3932164
  18.4 0.7 copy-start.1
  32.0 6.9 %copy-start.2 = (bf16[9,64,8]{1,2,0:T(8,128)(2,1)S(1)}, bf16[9,64,8]{1,2,0:T(8,128)(2,1)}, u32[]{:S(2)}) copy-start(bf16[9,64,8]{1,2,0:T(8,128)(2,1)} %param.14) | copy-start | bytes 27652
  32.0 7.4 %copy-start.3 = (f32[32]{0:T(128)S(1)}, f32[32]{0:T(128)}, u32[]{:S(2)}) copy-start(f32[32]{0:T(128)} %param.16) | copy-start | bytes 388
  32.0 7.5 %copy-start.4 = (f32[32]{0:T(128)S(1)}, f32[32]{0:T(128)}, u32[]{:S(2)}) copy-start(f32[32]{0:T(128)} %param.15) | copy-start | bytes 388
  32.0 7.6 %copy-start.5 = (f32[32]{0:T(128)S(1)}, f32[32]{0:T(128)}, u32[]{:S(2)}) copy-start(f32[32]{0:T(128)} %param.17) | copy-start | bytes 388
  32.0 31.5 %all-to-all-start.1 = ((s16[128,24,128]{2,1,0:T(8,128)(2,1)}), s16[128,24,128]{2,1,0:T(8,128)(2,1)S(1)}, u32[]{:S(2)}, u32[]{:S(2)}) async-start(s16[128,24,128]{2,1,0:T(8,128)(2,1)} %answer.1), calls=%async_computation.1 | async-start | bytes 1572864 | tf_op jit(solution)/shard_map/all_to_all | solution.py:389
  66.6 6.1 %collective-permute-start = (f32[128,128]{1,0:T(8,128)S(1)}, f32[128,128]{1,0:T(8,128)S(1)}, u32[]{:S(2)}, u32[]{:S(2)}) collective-permute-start(f32[128,128]{1,0:T(8,128)S(1)} %all_gather.3.mid_ref), channel_id=1, source_target_pairs={{16,32},{48,112},{96,80},{64,128},{144,160},{176,240},{224,208},{1... | collective-permute-start | bytes 196616 | tf_op jit(solution)/shard_map/ppermute | solution.py:425
  68.5 4.4 %collective-permute-start.1 = (f32[128,128]{1,0:T(8,128)S(1)}, f32[128,128]{1,0:T(8,128)S(1)}, u32[]{:S(2)}, u32[]{:S(2)}) collective-permute-start(f32[128,128]{1,0:T(8,128)S(1)} %all_gather.3.mid_ref), channel_id=1, source_target_pairs={{0,16},{32,48},{112,96},{80,64},{128,144},{160,176},{240,224},{208... | collective-permute-start | bytes 196616 | tf_op jit(solution)/shard_map/ppermute | solution.py:425

commit v7 on v6

--- a/solution.py
+++ b/solution.py
@@ -6,13 +6,14 @@
 from jax.sharding import PartitionSpec as P
 
 VIEWS = 5
-STEPS = 16384.0
+STEPS = 1618.0
 PD = 4
 MAXSHIFT = 16
 F32 = jnp.float32
 BF16 = jnp.bfloat16
 UNROLL = 8
 PIECES = 4
+WORDS = 10
 MIB = 1024 * 1024
 TORUS = (4, 4, 8)
 
@@ -126,17 +127,25 @@
 
     lax.fori_loop(0, blocks, step, 0, unroll=UNROLL)
 
+    half = blocks // 2
+    place = lax.broadcasted_iota(jnp.int32, (half, cols), 0) * 4
     size = cols // PIECES
     copies = []
     for n in range(PIECES):
         for k in range(n * size, (n + 1) * size):
             start = column_of(k) * blocks
             number = jnp.round(flat_s[start : start + blocks, :] * STEPS).astype(jnp.int32)
-            low = number & 255
-            coded_s[k, 0:blocks, :] = (number >> 8).astype(jnp.int16)
-            pair = low[: blocks // 2] * 256 + low[blocks // 2 :] - 32768
-            coded_s[k, blocks : blocks + blocks // 2, :] = pair.astype(jnp.int16)
-        piece = pl.ds(n * size, size)
+            high = number >> 4
+            low = number & 15
+            at = k * WORDS
+            coded_s[at : at + half, :] = (high[:half] << 16) | (high[half:] & 65535)
+            coded_s[at + half : at + half + 1, :] = jnp.sum(
+                low[:half] << place, axis=0, keepdims=True
+            )
+            coded_s[at + half + 1 : at + WORDS, :] = jnp.sum(
+                low[half:] << place, axis=0, keepdims=True
+            )
+        piece = pl.ds(n * size * WORDS, size * WORDS)
         copies.append(pltpu.make_async_copy(coded_s.at[piece], out_ref.at[piece], out_sem.at[n]))
         copies[-1].start()
     for copy in copies:
@@ -197,26 +206,29 @@
 
 
 def combine_kernel(ans_ref, target_ref, out_ref):
-    owners = ans_ref.shape[0]
+    owners = target_ref.shape[0]
     halves = target_ref.shape[1] // 8
-
-    def step(o, acc):
+    place = lax.broadcasted_iota(jnp.int32, (8, 128), 0) * 4
+
+    def step(n, acc):
         acc = list(acc)
-        targets = target_ref[o].astype(F32)
-        high = ans_ref[o, 0 : halves * 8, :].astype(jnp.int32)
-        pair = ans_ref[o, halves * 8 : halves * 12, :].astype(jnp.int32) + 32768
-        number = high * 256 + jnp.concatenate([pair >> 8, pair & 255], axis=0)
-        number = number.astype(F32)
-        for half in range(halves):
-            data = number[half * 8 : half * 8 + 8]
-            target = targets[half * 8 : half * 8 + 8, :]
-            for t in range(8):
-                n = t * halves + half
-                acc[n] = acc[n] + jnp.where(target == float(t), data, 0.0)
+        start = pl.multiple_of(n * 4 * WORDS, 8)
+        words = ans_ref[pl.ds(start, 4 * WORDS), :]
+        for m in range(4):
+            mine = words[m * WORDS : (m + 1) * WORDS]
+            targets = target_ref[n * 4 + m].astype(F32)
+            high = (mine[:8] >> 16, (mine[:8] << 16) >> 16)
+            for half in range(halves):
+                low = (jnp.broadcast_to(mine[8 + half : 9 + half], (8, 128)) >> place) & 15
+                data = (high[half] * 16 + low).astype(F32)
+                target = targets[half * 8 : half * 8 + 8, :]
+                for t in range(8):
+                    i = t * halves + half
+                    acc[i] = acc[i] + jnp.where(target == float(t), data, 0.0)
         return tuple(acc)
 
     zero = jnp.zeros((8, 128), F32)
-    acc = lax.fori_loop(0, owners, step, (zero,) * (8 * halves), unroll=8)
+    acc = lax.fori_loop(0, owners // 4, step, (zero,) * (8 * halves), unroll=2)
     lane = lax.broadcasted_iota(jnp.int32, (8, 128), 1)
     even = (lane // 8) % 2 == 0
     for p in range(PD):
@@ -372,12 +384,12 @@
 
     answers = pl.pallas_call(
         answers_of,
-        out_shape=jax.ShapeDtypeStruct((cols, blocks + blocks // 2, 128), jnp.int16),
+        out_shape=jax.ShapeDtypeStruct((cols * WORDS, 128), jnp.int32),
         in_specs=[vspec(), vspec(), vspec()],
         out_specs=pl.BlockSpec(memory_space=pl.ANY),
         scratch_shapes=[
             pltpu.VMEM((cols * blocks, 128), F32),
-            pltpu.VMEM((cols, blocks + blocks // 2, 128), jnp.int16),
+            pltpu.VMEM((cols * WORDS, 128), jnp.int32),
             pltpu.VMEM((8, owners), jnp.int32),
             pltpu.SMEM((8, owners), jnp.int32),
             pltpu.SemaphoreType.DMA,
@@ -386,7 +398,9 @@
         compiler_params=params(10),
         name="answer",
     )(asked, table, channels)
-    answers = lax.all_to_all(answers, "depth", split_axis=0, concat_axis=0, tiled=True)
+    answers = lax.all_to_all(
+        answers.reshape(cols, 1, WORDS * 128), "depth", split_axis=0, concat_axis=0, tiled=True
+    )
 
     slab = lax.axis_index("slab")
     depth = lax.axis_index("depth")
@@ -416,7 +430,7 @@
         out_specs=vspec(),
         compiler_params=params(6),
         name="combine",
-    )(answers, targets)
+    )(answers.reshape(owners * WORDS, 128), targets)
     both = lax.all_gather(cost, "slab", tiled=True)
     chips = path()
 

time: 93.8 us -> 91.4 us (0.974)
  waiting for transfers between devices: 32.5 us -> 29.7 us
    all_to_all x1, waiting for transfers between devices: 20.2 us -> 17.4 us  [body(): lax.all_to_all(answers.reshape(cols, 1, WORDS * 128), 'depth', split_axis...]
where the time goes in v7:
time: 91.4 us; the launch traced here: 90.8 us
  waiting for transfers between devices  29.7 us (32%)
  starting transfers between devices  24.2 us (26%)
  blocking collectives  20.2 us (22%)
  Pallas kernels  12.7 us (14%)
  local copies, waits for them, and re-layouts  2.74 us (3%)
    all_to_all x1, blocking collectives, body(): lax.all_to_all(packed.reshape(owners, 1, 128), 'depth', split_axis=0, con...  18.3 us
    all_to_all x1, waiting for transfers between devices, body(): lax.all_to_all(answers.reshape(cols, 1, WORDS * 128), 'depth', split_axis...  17.4 us
    all_to_all x1, starting transfers between devices, body(): lax.all_to_all(message, 'depth', split_axis=0, concat_axis=0, tiled=True)  15 us
    all_to_all x1, waiting for transfers between devices, body(): lax.all_to_all(message, 'depth', split_axis=0, concat_axis=0, tiled=True)  8.45 us
    all_to_all x1, starting transfers between devices, body(): lax.all_to_all(answers.reshape(cols, 1, WORDS * 128), 'depth', split_axis...  6.75 us
    pallas_call x1, Pallas kernels, body(): pl.pallas_call(answers_of, out_shape=jax.ShapeDtypeStruct((cols * WORDS,...  3.85 us
    ppermute x2, waiting for transfers between devices, exchange(): return lax.ppermute(both, 'depth', pairs + [(b, a) for a, b in pairs])  3.84 us
    pallas_call x1, Pallas kernels, body(): pl.pallas_call(tables_of, out_shape=(jax.ShapeDtypeStruct((owners, blocks...  3.33 us
  transfers between devices with their start and end apart: 4, of which 4 were waited for; matrix products, arithmetic and copies ran while one was open for 1% of the time, Pallas kernels for 4%

profile of v7, /device:TPU:32, one launch (start us, length us, event | category | flops | bytes accessed | tf_op | source)
XLA Modules:
  0.0 90.8 jit_solution(17904701499886078062)
XLA Ops:
  0.6 1.4 %message.1 = s32[128,128]{1,0:T(8,128)} custom-call(s32[1,40]{1,0:T(1,128)} %bitcast.29, s32[1,40]{1,0:T(1,128)} %bitcast.30, s32[1,40]{1,0:T(1,128)} %bitcast.31), custom_call_target="tpu_custom_call" | custom-call | tf_op jit(solution)/shard_map/message/pallas_call | solution.py:352
  2.0 15.0 %all-to-all-start = ((s32[128,1,128]{2,1,0:T(1,128)}), s32[128,1,128]{2,1,0:T(1,128)S(1)}, u32[]{:S(2)}, u32[]{:S(2)}) async-start(s32[128,1,128]{2,1,0:T(1,128)} %bitcast.25), calls=%async_computation | async-start | bytes 131072 | tf_op jit(solution)/shard_map/all_to_all | solution.py:362
  17.1 0.0 copy-start
  17.1 1.3 %copy-done = bf16[160,32,128]{2,1,0:T(8,128)(2,1)S(1)} copy-done((bf16[160,32,128]{2,1,0:T(8,128)(2,1)S(1)}, bf16[160,32,128]{2,1,0:T(8,128)(2,1)}, u32[]{:S(2)}) %copy-start) | copy-done | bytes 1310744
  18.4 0.0 copy-start.1
  18.4 0.7 copy-done.1
  19.1 0.6 prepare.1
  19.8 8.5 %all-to-all-done = s32[128,1,128]{2,1,0:T(1,128)S(1)} async-done(((s32[128,1,128]{2,1,0:T(1,128)}), s32[128,1,128]{2,1,0:T(1,128)S(1)}, u32[]{:S(2)}, u32[]{:S(2)}) %all-to-all-start) | async-done | bytes 65568 | tf_op jit(solution)/shard_map/all_to_all | solution.py:362
  28.2 3.8 %answer.1 = s32[1280,128]{1,0:T(8,128)} custom-call(s32[128,128]{1,0:T(8,128)S(1)} %bitcast.21, f32[66,32,128]{2,1,0:T(8,128)S(1)} %get-tuple-element.6.refs_1_, bf16[160,32,128]{2,1,0:T(8,128)(2,1)S(1)} %get-tuple-element.7.refs_2_), custom_call_target="tpu_custom_call" | custom-call | tf_op jit(solution)/shard_map/answer/pallas_call | solution.py:385
  32.1 0.0 copy-start.2
  32.1 0.0 copy-start.3
  32.1 0.0 copy-start.4
  32.1 0.0 copy-start.5
  32.1 6.8 %all-to-all-start.1 = ((s32[128,1,1280]{2,1,0:T(1,128)}), s32[128,1,1280]{2,1,0:T(1,128)S(1)}, u32[]{:S(2)}, u32[]{:S(2)}) async-start(s32[128,1,1280]{2,1,0:T(1,128)} %bitcast.6), calls=%async_computation.1 | async-start | bytes 1310720 | tf_op jit(solution)/shard_map/all_to_all | solution.py:401
  38.9 0.0 copy-done.2
  38.9 0.1 reshape.207
  39.0 0.2 pad_dynamic-slice_fusion.1
  39.3 0.1 copy.21
  39.4 0.1 reshape.208
  39.5 0.0 copy-done.3
  39.5 0.1 stack_tile.7
  39.6 0.0 copy-done.4
  39.6 0.1 stack_tile.6
  39.7 0.0 copy-done.5
  39.7 0.1 broadcast_in_dim.16
  39.8 0.1 pad_maximum_fusion.1.refs_1_
  39.9 0.2 compare_select_fusion.wo_ref
  40.1 3.3 %tables.1 = (bf16[128,16,128]{2,1,0:T(8,128)(2,1)S(1)}, bf16[768,1024]{1,0:T(8,128)(2,1)S(1)}) custom-call(s32[128,128]{1,0:T(8,128)S(1)} %bitcast.22, bf16[2,96,128]{2,1,0:T(8,128)(2,1)S(1)} %pad_maximum_fusion.1.refs_1_), custom_call_target="tpu_custom_call" | custom-call | flops 20000000 | bytes 3000000 | tf_op jit(solution)/shard_map/tables/pallas_call | solution.py:412
  43.4 17.4 %all-to-all-done.1 = s32[128,1,1280]{2,1,0:T(1,128)S(1)} async-done(((s32[128,1,1280]{2,1,0:T(1,128)}), s32[128,1,1280]{2,1,0:T(1,128)S(1)}, u32[]{:S(2)}, u32[]{:S(2)}) %all-to-all-start.1) | async-done | bytes 655392 | tf_op jit(solution)/shard_map/all_to_all | solution.py:401
  60.8 1.4 %combine.1 = f32[64,128]{1,0:T(8,128)S(1)} custom-call(s32[1280,128]{1,0:T(8,128)S(1)} %bitcast.20, bf16[128,16,128]{2,1,0:T(8,128)(2,1)S(1)} %get-tuple-element.8.target_ref), custom_call_target="tpu_custom_call" | custom-call | tf_op jit(solution)/shard_map/combine/pallas_call | solution.py:426
  62.2 1.9 %all_gather.3.mid_ref = f32[128,128]{1,0:T(8,128)S(1)} all-gather(f32[64,128]{1,0:T(8,128)S(1)} %combine.1), channel_id=1, replica_groups=mesh['depth'=128,'slab'=2] {'slab'}, dimensions={0}, use_global_device_ids=true | all-gather | bytes 98304 | tf_op jit(solution)/shard_map/all_gather | solution.py:434
  64.1 1.9 %collective-permute-start = (f32[128,128]{1,0:T(8,128)S(1)}, f32[128,128]{1,0:T(8,128)S(1)}, u32[]{:S(2)}, u32[]{:S(2)}) collective-permute-start(f32[128,128]{1,0:T(8,128)S(1)} %all_gather.3.mid_ref), channel_id=1, source_target_pairs={{16,32},{48,112},{96,80},{64,128},{144,160},{176,240},{224,208},{1... | collective-permute-start | bytes 196616 | tf_op jit(solution)/shard_map/ppermute | solution.py:439
  66.0 0.5 collective-permute-start.1
  66.5 3.7 %collective-permute-done.first_ref = f32[128,128]{1,0:T(8,128)S(1)} collective-permute-done((f32[128,128]{1,0:T(8,128)S(1)}, f32[128,128]{1,0:T(8,128)S(1)}, u32[]{:S(2)}, u32[]{:S(2)}) %collective-permute-start) | collective-permute-done | bytes 65568 | tf_op jit(solution)/shard_map/ppermute | solution.py:439
  70.2 0.1 collective-permute-done.1.second_ref
  70.4 1.4 %column.1 = f32[128,128]{1,0:T(8,128)S(1)} custom-call(f32[128,128]{1,0:T(8,128)S(1)} %collective-permute-done.first_ref, f32[128,128]{1,0:T(8,128)S(1)} %all_gather.3.mid_ref, f32[128,128]{1,0:T(8,128)S(1)} %collective-permute-done.1.second_ref, bf16[768,1024]{1,0:T(8,128)(2,1)S(1)} %get-tuple-element.9.w_ref, f32[2,512]{1,0:T(2,128)S(1)} %pad_maximum_fusion.2.bias_ref, ...), custom_call_target="tpu_custom_call" | custom-call | tf_op jit(solution)/shard_map/column/pallas_call | solution.py:448
  71.7 18.3 %all_to_all.15 = f32[128,1,128]{2,1,0:T(1,128)S(1)} all-to-all(f32[128,1,128]{2,1,0:T(1,128)S(1)} %bitcast.23), channel_id=1, replica_groups=mesh['depth'=128,'slab'=2] {'depth'}, dimensions={0} | all-to-all | bytes 131072 | tf_op jit(solution)/shard_map/all_to_all | solution.py:456
  90.1 0.7 output.1
  (10 shorter events, 0.1 us)
Async XLA Ops:
  2.0 26.2 %all-to-all-start = ((s32[128,1,128]{2,1,0:T(1,128)}), s32[128,1,128]{2,1,0:T(1,128)S(1)}, u32[]{:S(2)}, u32[]{:S(2)}) async-start(s32[128,1,128]{2,1,0:T(1,128)} %bitcast.25), calls=%async_computation | async-start | bytes 131072 | tf_op jit(solution)/shard_map/all_to_all | solution.py:362
  17.1 1.3 %copy-start = (bf16[160,32,128]{2,1,0:T(8,128)(2,1)S(1)}, bf16[160,32,128]{2,1,0:T(8,128)(2,1)}, u32[]{:S(2)}) copy-start(bf16[160,32,128]{2,1,0:T(8,128)(2,1)} %src_ref.1) | copy-start | bytes 3932164
  18.4 0.7 copy-start.1
  32.1 6.9 %copy-start.2 = (bf16[9,64,8]{1,2,0:T(8,128)(2,1)S(1)}, bf16[9,64,8]{1,2,0:T(8,128)(2,1)}, u32[]{:S(2)}) copy-start(bf16[9,64,8]{1,2,0:T(8,128)(2,1)} %param.14) | copy-start | bytes 27652
  32.1 7.4 %copy-start.3 = (f32[32]{0:T(128)S(1)}, f32[32]{0:T(128)}, u32[]{:S(2)}) copy-start(f32[32]{0:T(128)} %param.16) | copy-start | bytes 388
  32.1 7.5 %copy-start.4 = (f32[32]{0:T(128)S(1)}, f32[32]{0:T(128)}, u32[]{:S(2)}) copy-start(f32[32]{0:T(128)} %param.15) | copy-start | bytes 388
  32.1 7.6 %copy-start.5 = (f32[32]{0:T(128)S(1)}, f32[32]{0:T(128)}, u32[]{:S(2)}) copy-start(f32[32]{0:T(128)} %param.17) | copy-start | bytes 388
  32.1 28.7 %all-to-all-start.1 = ((s32[128,1,1280]{2,1,0:T(1,128)}), s32[128,1,1280]{2,1,0:T(1,128)S(1)}, u32[]{:S(2)}, u32[]{:S(2)}) async-start(s32[128,1,1280]{2,1,0:T(1,128)} %bitcast.6), calls=%async_computation.1 | async-start | bytes 1310720 | tf_op jit(solution)/shard_map/all_to_all | solution.py:401
  64.1 6.1 %collective-permute-start = (f32[128,128]{1,0:T(8,128)S(1)}, f32[128,128]{1,0:T(8,128)S(1)}, u32[]{:S(2)}, u32[]{:S(2)}) collective-permute-start(f32[128,128]{1,0:T(8,128)S(1)} %all_gather.3.mid_ref), channel_id=1, source_target_pairs={{16,32},{48,112},{96,80},{64,128},{144,160},{176,240},{224,208},{1... | collective-permute-start | bytes 196616 | tf_op jit(solution)/shard_map/ppermute | solution.py:439
  66.0 4.4 %collective-permute-start.1 = (f32[128,128]{1,0:T(8,128)S(1)}, f32[128,128]{1,0:T(8,128)S(1)}, u32[]{:S(2)}, u32[]{:S(2)}) collective-permute-start(f32[128,128]{1,0:T(8,128)S(1)} %all_gather.3.mid_ref), channel_id=1, source_target_pairs={{0,16},{32,48},{112,96},{80,64},{128,144},{160,176},{240,224},{208... | collective-permute-start | bytes 196616 | tf_op jit(solution)/shard_map/ppermute | solution.py:439

commit v8 on v7

--- a/solution.py
+++ b/solution.py
@@ -11,8 +11,8 @@
 MAXSHIFT = 16
 F32 = jnp.float32
 BF16 = jnp.bfloat16
-UNROLL = 8
-PIECES = 4
+UNROLL = 16
+PIECES = 8
 WORDS = 10
 MIB = 1024 * 1024
 TORUS = (4, 4, 8)
@@ -228,7 +228,7 @@
         return tuple(acc)
 
     zero = jnp.zeros((8, 128), F32)
-    acc = lax.fori_loop(0, owners // 4, step, (zero,) * (8 * halves), unroll=2)
+    acc = lax.fori_loop(0, owners // 4, step, (zero,) * (8 * halves), unroll=4)
     lane = lax.broadcasted_iota(jnp.int32, (8, 128), 1)
     even = (lane // 8) % 2 == 0
     for p in range(PD):

time: 91.4 us -> 91.2 us (level)
  no operation moved by 1% of the time
where the time goes in v8:
time: 91.2 us; the launch traced here: 90.5 us
  waiting for transfers between devices  29.7 us (33%)
  starting transfers between devices  24.2 us (27%)
  blocking collectives  20.2 us (22%)
  Pallas kernels  12.5 us (14%)
  local copies, waits for them, and re-layouts  2.74 us (3%)
    all_to_all x1, blocking collectives, body(): lax.all_to_all(packed.reshape(owners, 1, 128), 'depth', split_axis=0, con...  18.3 us
    all_to_all x1, waiting for transfers between devices, body(): lax.all_to_all(answers.reshape(cols, 1, WORDS * 128), 'depth', split_axis...  17.4 us
    all_to_all x1, starting transfers between devices, body(): lax.all_to_all(message, 'depth', split_axis=0, concat_axis=0, tiled=True)  15 us
    all_to_all x1, waiting for transfers between devices, body(): lax.all_to_all(message, 'depth', split_axis=0, concat_axis=0, tiled=True)  8.45 us
    all_to_all x1, starting transfers between devices, body(): lax.all_to_all(answers.reshape(cols, 1, WORDS * 128), 'depth', split_axis...  6.75 us
    ppermute x2, waiting for transfers between devices, exchange(): return lax.ppermute(both, 'depth', pairs + [(b, a) for a, b in pairs])  3.84 us
    pallas_call x1, Pallas kernels, body(): pl.pallas_call(answers_of, out_shape=jax.ShapeDtypeStruct((cols * WORDS,...  3.63 us
    pallas_call x1, Pallas kernels, body(): pl.pallas_call(tables_of, out_shape=(jax.ShapeDtypeStruct((owners, blocks...  3.33 us
  transfers between devices with their start and end apart: 4, of which 4 were waited for; matrix products, arithmetic and copies ran while one was open for 1% of the time, Pallas kernels for 4%

profile of v8, /device:TPU:32, one launch (start us, length us, event | category | flops | bytes accessed | tf_op | source)
XLA Modules:
  0.0 90.5 jit_solution(5852751783847251582)
XLA Ops:
  0.6 1.4 %message.1 = s32[128,128]{1,0:T(8,128)} custom-call(s32[1,40]{1,0:T(1,128)} %bitcast.29, s32[1,40]{1,0:T(1,128)} %bitcast.30, s32[1,40]{1,0:T(1,128)} %bitcast.31), custom_call_target="tpu_custom_call" | custom-call | tf_op jit(solution)/shard_map/message/pallas_call | solution.py:352
  2.0 15.0 %all-to-all-start = ((s32[128,1,128]{2,1,0:T(1,128)}), s32[128,1,128]{2,1,0:T(1,128)S(1)}, u32[]{:S(2)}, u32[]{:S(2)}) async-start(s32[128,1,128]{2,1,0:T(1,128)} %bitcast.25), calls=%async_computation | async-start | bytes 131072 | tf_op jit(solution)/shard_map/all_to_all | solution.py:362
  17.1 0.0 copy-start
  17.1 1.3 %copy-done = bf16[160,32,128]{2,1,0:T(8,128)(2,1)S(1)} copy-done((bf16[160,32,128]{2,1,0:T(8,128)(2,1)S(1)}, bf16[160,32,128]{2,1,0:T(8,128)(2,1)}, u32[]{:S(2)}) %copy-start) | copy-done | bytes 1310744
  18.4 0.0 copy-start.1
  18.4 0.7 copy-done.1
  19.1 0.6 prepare.1
  19.8 8.5 %all-to-all-done = s32[128,1,128]{2,1,0:T(1,128)S(1)} async-done(((s32[128,1,128]{2,1,0:T(1,128)}), s32[128,1,128]{2,1,0:T(1,128)S(1)}, u32[]{:S(2)}, u32[]{:S(2)}) %all-to-all-start) | async-done | bytes 65568 | tf_op jit(solution)/shard_map/all_to_all | solution.py:362
  28.2 3.6 %answer.1 = s32[1280,128]{1,0:T(8,128)} custom-call(s32[128,128]{1,0:T(8,128)S(1)} %bitcast.21, f32[66,32,128]{2,1,0:T(8,128)S(1)} %get-tuple-element.6.refs_1_, bf16[160,32,128]{2,1,0:T(8,128)(2,1)S(1)} %get-tuple-element.7.refs_2_), custom_call_target="tpu_custom_call" | custom-call | tf_op jit(solution)/shard_map/answer/pallas_call | solution.py:385
  31.8 0.0 copy-start.2
  31.9 0.0 copy-start.3
  31.9 0.0 copy-start.4
  31.9 0.0 copy-start.5
  31.9 6.8 %all-to-all-start.1 = ((s32[128,1,1280]{2,1,0:T(1,128)}), s32[128,1,1280]{2,1,0:T(1,128)S(1)}, u32[]{:S(2)}, u32[]{:S(2)}) async-start(s32[128,1,1280]{2,1,0:T(1,128)} %bitcast.6), calls=%async_computation.1 | async-start | bytes 1310720 | tf_op jit(solution)/shard_map/all_to_all | solution.py:401
  38.7 0.0 copy-done.2
  38.7 0.1 reshape.207
  38.8 0.2 pad_dynamic-slice_fusion.1
  39.1 0.1 copy.21
  39.1 0.1 reshape.208
  39.3 0.0 copy-done.3
  39.3 0.1 stack_tile.7
  39.4 0.0 copy-done.4
  39.4 0.1 stack_tile.6
  39.4 0.0 copy-done.5
  39.4 0.1 broadcast_in_dim.16
  39.5 0.1 pad_maximum_fusion.1.refs_1_
  39.6 0.2 compare_select_fusion.wo_ref
  39.8 3.3 %tables.1 = (bf16[128,16,128]{2,1,0:T(8,128)(2,1)S(1)}, bf16[768,1024]{1,0:T(8,128)(2,1)S(1)}) custom-call(s32[128,128]{1,0:T(8,128)S(1)} %bitcast.22, bf16[2,96,128]{2,1,0:T(8,128)(2,1)S(1)} %pad_maximum_fusion.1.refs_1_), custom_call_target="tpu_custom_call" | custom-call | flops 20000000 | bytes 3000000 | tf_op jit(solution)/shard_map/tables/pallas_call | solution.py:412
  43.2 17.4 %all-to-all-done.1 = s32[128,1,1280]{2,1,0:T(1,128)S(1)} async-done(((s32[128,1,1280]{2,1,0:T(1,128)}), s32[128,1,1280]{2,1,0:T(1,128)S(1)}, u32[]{:S(2)}, u32[]{:S(2)}) %all-to-all-start.1) | async-done | bytes 655392 | tf_op jit(solution)/shard_map/all_to_all | solution.py:401
  60.6 1.4 %combine.1 = f32[64,128]{1,0:T(8,128)S(1)} custom-call(s32[1280,128]{1,0:T(8,128)S(1)} %bitcast.20, bf16[128,16,128]{2,1,0:T(8,128)(2,1)S(1)} %get-tuple-element.8.target_ref), custom_call_target="tpu_custom_call" | custom-call | tf_op jit(solution)/shard_map/combine/pallas_call | solution.py:426
  62.0 1.9 %all_gather.3.mid_ref = f32[128,128]{1,0:T(8,128)S(1)} all-gather(f32[64,128]{1,0:T(8,128)S(1)} %combine.1), channel_id=1, replica_groups=mesh['depth'=128,'slab'=2] {'slab'}, dimensions={0}, use_global_device_ids=true | all-gather | bytes 98304 | tf_op jit(solution)/shard_map/all_gather | solution.py:434
  63.8 1.9 %collective-permute-start = (f32[128,128]{1,0:T(8,128)S(1)}, f32[128,128]{1,0:T(8,128)S(1)}, u32[]{:S(2)}, u32[]{:S(2)}) collective-permute-start(f32[128,128]{1,0:T(8,128)S(1)} %all_gather.3.mid_ref), channel_id=1, source_target_pairs={{16,32},{48,112},{96,80},{64,128},{144,160},{176,240},{224,208},{1... | collective-permute-start | bytes 196616 | tf_op jit(solution)/shard_map/ppermute | solution.py:439
  65.7 0.5 collective-permute-start.1
  66.2 3.7 %collective-permute-done.first_ref = f32[128,128]{1,0:T(8,128)S(1)} collective-permute-done((f32[128,128]{1,0:T(8,128)S(1)}, f32[128,128]{1,0:T(8,128)S(1)}, u32[]{:S(2)}, u32[]{:S(2)}) %collective-permute-start) | collective-permute-done | bytes 65568 | tf_op jit(solution)/shard_map/ppermute | solution.py:439
  70.0 0.1 collective-permute-done.1.second_ref
  70.1 1.4 %column.1 = f32[128,128]{1,0:T(8,128)S(1)} custom-call(f32[128,128]{1,0:T(8,128)S(1)} %collective-permute-done.first_ref, f32[128,128]{1,0:T(8,128)S(1)} %all_gather.3.mid_ref, f32[128,128]{1,0:T(8,128)S(1)} %collective-permute-done.1.second_ref, bf16[768,1024]{1,0:T(8,128)(2,1)S(1)} %get-tuple-element.9.w_ref, f32[2,512]{1,0:T(2,128)S(1)} %pad_maximum_fusion.2.bias_ref, ...), custom_call_target="tpu_custom_call" | custom-call | tf_op jit(solution)/shard_map/column/pallas_call | solution.py:448
  71.5 18.3 %all_to_all.15 = f32[128,1,128]{2,1,0:T(1,128)S(1)} all-to-all(f32[128,1,128]{2,1,0:T(1,128)S(1)} %bitcast.23), channel_id=1, replica_groups=mesh['depth'=128,'slab'=2] {'depth'}, dimensions={0} | all-to-all | bytes 131072 | tf_op jit(solution)/shard_map/all_to_all | solution.py:456
  89.8 0.7 output.1
  (10 shorter events, 0.1 us)
Async XLA Ops:
  2.0 26.2 %all-to-all-start = ((s32[128,1,128]{2,1,0:T(1,128)}), s32[128,1,128]{2,1,0:T(1,128)S(1)}, u32[]{:S(2)}, u32[]{:S(2)}) async-start(s32[128,1,128]{2,1,0:T(1,128)} %bitcast.25), calls=%async_computation | async-start | bytes 131072 | tf_op jit(solution)/shard_map/all_to_all | solution.py:362
  17.1 1.3 %copy-start = (bf16[160,32,128]{2,1,0:T(8,128)(2,1)S(1)}, bf16[160,32,128]{2,1,0:T(8,128)(2,1)}, u32[]{:S(2)}) copy-start(bf16[160,32,128]{2,1,0:T(8,128)(2,1)} %src_ref.1) | copy-start | bytes 3932164
  18.4 0.7 copy-start.1
  31.8 6.9 %copy-start.2 = (bf16[9,64,8]{1,2,0:T(8,128)(2,1)S(1)}, bf16[9,64,8]{1,2,0:T(8,128)(2,1)}, u32[]{:S(2)}) copy-start(bf16[9,64,8]{1,2,0:T(8,128)(2,1)} %param.14) | copy-start | bytes 27652
  31.9 7.4 %copy-start.3 = (f32[32]{0:T(128)S(1)}, f32[32]{0:T(128)}, u32[]{:S(2)}) copy-start(f32[32]{0:T(128)} %param.16) | copy-start | bytes 388
  31.9 7.5 %copy-start.4 = (f32[32]{0:T(128)S(1)}, f32[32]{0:T(128)}, u32[]{:S(2)}) copy-start(f32[32]{0:T(128)} %param.15) | copy-start | bytes 388
  31.9 7.6 %copy-start.5 = (f32[32]{0:T(128)S(1)}, f32[32]{0:T(128)}, u32[]{:S(2)}) copy-start(f32[32]{0:T(128)} %param.17) | copy-start | bytes 388
  31.9 28.7 %all-to-all-start.1 = ((s32[128,1,1280]{2,1,0:T(1,128)}), s32[128,1,1280]{2,1,0:T(1,128)S(1)}, u32[]{:S(2)}, u32[]{:S(2)}) async-start(s32[128,1,1280]{2,1,0:T(1,128)} %bitcast.6), calls=%async_computation.1 | async-start | bytes 1310720 | tf_op jit(solution)/shard_map/all_to_all | solution.py:401
  63.8 6.1 %collective-permute-start = (f32[128,128]{1,0:T(8,128)S(1)}, f32[128,128]{1,0:T(8,128)S(1)}, u32[]{:S(2)}, u32[]{:S(2)}) collective-permute-start(f32[128,128]{1,0:T(8,128)S(1)} %all_gather.3.mid_ref), channel_id=1, source_target_pairs={{16,32},{48,112},{96,80},{64,128},{144,160},{176,240},{224,208},{1... | collective-permute-start | bytes 196616 | tf_op jit(solution)/shard_map/ppermute | solution.py:439
  65.7 4.4 %collective-permute-start.1 = (f32[128,128]{1,0:T(8,128)S(1)}, f32[128,128]{1,0:T(8,128)S(1)}, u32[]{:S(2)}, u32[]{:S(2)}) collective-permute-start(f32[128,128]{1,0:T(8,128)S(1)} %all_gather.3.mid_ref), channel_id=1, source_target_pairs={{0,16},{32,48},{112,96},{80,64},{128,144},{160,176},{240,224},{208... | collective-permute-start | bytes 196616 | tf_op jit(solution)/shard_map/ppermute | solution.py:439

commit v9 on v8

--- a/solution.py
+++ b/solution.py
@@ -333,12 +333,12 @@
     map_ref[...] = t[8:10]
 
 
-def gate_rows(w_gates, slab, odd):
+def gate_rows(w_gates, slab, turned):
     w = w_gates.reshape(3, 3, 2, 32, 8).transpose(0, 1, 4, 2, 3)
     w = jnp.pad(w, ((2, 2), (0, 0), (0, 0), (0, 0), (0, 0)))
     by_row = [lax.dynamic_slice_in_dim(w, 3 - r - 2 * slab, 4, axis=0) for r in range(2)]
     v = jnp.stack(by_row, axis=4).reshape(2, 2, 3, 8, 2, 2, 32)
-    v = jnp.where(odd, v[:, :, ::-1], v)
+    v = jnp.where(turned, v[:, :, ::-1], v)
     v = v.transpose(4, 2, 0, 1, 3, 5, 6).reshape(2, 96, 64)
     return jnp.concatenate([v, v], axis=2)
 
@@ -404,7 +404,7 @@
 
     slab = lax.axis_index("slab")
     depth = lax.axis_index("depth")
-    odd = (depth // (TORUS[1] * TORUS[2]) + depth // TORUS[2] + depth) % 2 == 1
+    even = (depth // (TORUS[1] * TORUS[2]) + depth // TORUS[2] + depth) % 2 == 0
 
     def tables_of(*refs):
         table_kernel(requests, *refs)
@@ -421,7 +421,7 @@
         compiler_params=params(8),
         cost_estimate=pl.CostEstimate(flops=20000000, transcendentals=0, bytes_accessed=3000000),
         name="tables",
-    )(asked, gate_rows(w_gates, slab, odd))
+    )(asked, gate_rows(w_gates, slab, even))
 
     cost = pl.pallas_call(
         combine_kernel,
@@ -438,7 +438,7 @@
         pairs = [(chips[i], chips[i + 1]) for i in range(start, owners - 1, 2)]
         return lax.ppermute(both, "depth", pairs + [(b, a) for a, b in pairs])
 
-    first, second = exchange(1), exchange(0)
+    first, second = exchange(0), exchange(1)
 
     bias = jnp.stack([jnp.tile(bias_z, 16), jnp.tile(bias_c, 16)])
     unit_row = jnp.arange(512, dtype=jnp.int32)[:, None] // 32

time: 91.2 us -> 90.8 us (level)
  no operation moved by 1% of the time
where the time goes in v9:
time: 90.8 us; the launch traced here: 90.2 us
  waiting for transfers between devices  29.8 us (33%)
  starting transfers between devices  24 us (26%)
  blocking collectives  19.9 us (22%)
  Pallas kernels  12.5 us (14%)
  local copies, waits for them, and re-layouts  2.74 us (3%)
    all_to_all x1, blocking collectives, body(): lax.all_to_all(packed.reshape(owners, 1, 128), 'depth', split_axis=0, con...  18.1 us
    all_to_all x1, waiting for transfers between devices, body(): lax.all_to_all(answers.reshape(cols, 1, WORDS * 128), 'depth', split_axis...  17.4 us
    all_to_all x1, starting transfers between devices, body(): lax.all_to_all(message, 'depth', split_axis=0, concat_axis=0, tiled=True)  15 us
    all_to_all x1, waiting for transfers between devices, body(): lax.all_to_all(message, 'depth', split_axis=0, concat_axis=0, tiled=True)  8.45 us
    all_to_all x1, starting transfers between devices, body(): lax.all_to_all(answers.reshape(cols, 1, WORDS * 128), 'depth', split_axis...  6.75 us
    ppermute x2, waiting for transfers between devices, exchange(): return lax.ppermute(both, 'depth', pairs + [(b, a) for a, b in pairs])  3.92 us
    pallas_call x1, Pallas kernels, body(): pl.pallas_call(answers_of, out_shape=jax.ShapeDtypeStruct((cols * WORDS,...  3.63 us
    pallas_call x1, Pallas kernels, body(): pl.pallas_call(tables_of, out_shape=(jax.ShapeDtypeStruct((owners, blocks...  3.33 us
  transfers between devices with their start and end apart: 4, of which 4 were waited for; matrix products, arithmetic and copies ran while one was open for 1% of the time, Pallas kernels for 4%

profile of v9, /device:TPU:32, one launch (start us, length us, event | category | flops | bytes accessed | tf_op | source)
XLA Modules:
  0.0 90.2 jit_solution(10700586394611232653)
XLA Ops:
  0.6 1.4 %message.1 = s32[128,128]{1,0:T(8,128)} custom-call(s32[1,40]{1,0:T(1,128)} %bitcast.29, s32[1,40]{1,0:T(1,128)} %bitcast.30, s32[1,40]{1,0:T(1,128)} %bitcast.31), custom_call_target="tpu_custom_call" | custom-call | tf_op jit(solution)/shard_map/message/pallas_call | solution.py:352
  2.0 15.0 %all-to-all-start = ((s32[128,1,128]{2,1,0:T(1,128)}), s32[128,1,128]{2,1,0:T(1,128)S(1)}, u32[]{:S(2)}, u32[]{:S(2)}) async-start(s32[128,1,128]{2,1,0:T(1,128)} %bitcast.25), calls=%async_computation | async-start | bytes 131072 | tf_op jit(solution)/shard_map/all_to_all | solution.py:362
  17.1 0.0 copy-start
  17.1 1.3 %copy-done = bf16[160,32,128]{2,1,0:T(8,128)(2,1)S(1)} copy-done((bf16[160,32,128]{2,1,0:T(8,128)(2,1)S(1)}, bf16[160,32,128]{2,1,0:T(8,128)(2,1)}, u32[]{:S(2)}) %copy-start) | copy-done | bytes 1310744
  18.4 0.0 copy-start.1
  18.4 0.7 copy-done.1
  19.1 0.6 prepare.1
  19.8 8.5 %all-to-all-done = s32[128,1,128]{2,1,0:T(1,128)S(1)} async-done(((s32[128,1,128]{2,1,0:T(1,128)}), s32[128,1,128]{2,1,0:T(1,128)S(1)}, u32[]{:S(2)}, u32[]{:S(2)}) %all-to-all-start) | async-done | bytes 65568 | tf_op jit(solution)/shard_map/all_to_all | solution.py:362
  28.2 3.6 %answer.1 = s32[1280,128]{1,0:T(8,128)} custom-call(s32[128,128]{1,0:T(8,128)S(1)} %bitcast.21, f32[66,32,128]{2,1,0:T(8,128)S(1)} %get-tuple-element.6.refs_1_, bf16[160,32,128]{2,1,0:T(8,128)(2,1)S(1)} %get-tuple-element.7.refs_2_), custom_call_target="tpu_custom_call" | custom-call | tf_op jit(solution)/shard_map/answer/pallas_call | solution.py:385
  31.8 0.0 copy-start.2
  31.9 0.0 copy-start.3
  31.9 0.0 copy-start.4
  31.9 0.0 copy-start.5
  31.9 6.8 %all-to-all-start.1 = ((s32[128,1,1280]{2,1,0:T(1,128)}), s32[128,1,1280]{2,1,0:T(1,128)S(1)}, u32[]{:S(2)}, u32[]{:S(2)}) async-start(s32[128,1,1280]{2,1,0:T(1,128)} %bitcast.6), calls=%async_computation.1 | async-start | bytes 1310720 | tf_op jit(solution)/shard_map/all_to_all | solution.py:401
  38.7 0.0 copy-done.2
  38.7 0.1 reshape.207
  38.8 0.2 pad_dynamic-slice_fusion.1
  39.1 0.1 copy.21
  39.1 0.1 reshape.208
  39.3 0.0 copy-done.3
  39.3 0.1 stack_tile.7
  39.4 0.0 copy-done.4
  39.4 0.1 stack_tile.6
  39.4 0.0 copy-done.5
  39.4 0.1 broadcast_in_dim.16
  39.5 0.1 pad_maximum_fusion.1.refs_1_
  39.6 0.2 compare_select_fusion.wo_ref
  39.8 3.3 %tables.1 = (bf16[128,16,128]{2,1,0:T(8,128)(2,1)S(1)}, bf16[768,1024]{1,0:T(8,128)(2,1)S(1)}) custom-call(s32[128,128]{1,0:T(8,128)S(1)} %bitcast.22, bf16[2,96,128]{2,1,0:T(8,128)(2,1)S(1)} %pad_maximum_fusion.1.refs_1_), custom_call_target="tpu_custom_call" | custom-call | flops 20000000 | bytes 3000000 | tf_op jit(solution)/shard_map/tables/pallas_call | solution.py:412
  43.2 17.4 %all-to-all-done.1 = s32[128,1,1280]{2,1,0:T(1,128)S(1)} async-done(((s32[128,1,1280]{2,1,0:T(1,128)}), s32[128,1,1280]{2,1,0:T(1,128)S(1)}, u32[]{:S(2)}, u32[]{:S(2)}) %all-to-all-start.1) | async-done | bytes 655392 | tf_op jit(solution)/shard_map/all_to_all | solution.py:401
  60.6 1.4 %combine.1 = f32[64,128]{1,0:T(8,128)S(1)} custom-call(s32[1280,128]{1,0:T(8,128)S(1)} %bitcast.20, bf16[128,16,128]{2,1,0:T(8,128)(2,1)S(1)} %get-tuple-element.8.target_ref), custom_call_target="tpu_custom_call" | custom-call | tf_op jit(solution)/shard_map/combine/pallas_call | solution.py:426
  62.0 1.9 %all_gather.3.mid_ref = f32[128,128]{1,0:T(8,128)S(1)} all-gather(f32[64,128]{1,0:T(8,128)S(1)} %combine.1), channel_id=1, replica_groups=mesh['depth'=128,'slab'=2] {'slab'}, dimensions={0}, use_global_device_ids=true | all-gather | bytes 98304 | tf_op jit(solution)/shard_map/all_gather | solution.py:434
  63.8 0.1 collective-permute-start
  63.9 2.2 %collective-permute-start.1 = (f32[128,128]{1,0:T(8,128)S(1)}, f32[128,128]{1,0:T(8,128)S(1)}, u32[]{:S(2)}, u32[]{:S(2)}) collective-permute-start(f32[128,128]{1,0:T(8,128)S(1)} %all_gather.3.mid_ref), channel_id=1, source_target_pairs={{16,32},{48,112},{96,80},{64,128},{144,160},{176,240},{224,208},{1... | collective-permute-start | bytes 196616 | tf_op jit(solution)/shard_map/ppermute | solution.py:439
  66.1 2.0 %collective-permute-done.first_ref = f32[128,128]{1,0:T(8,128)S(1)} collective-permute-done((f32[128,128]{1,0:T(8,128)S(1)}, f32[128,128]{1,0:T(8,128)S(1)}, u32[]{:S(2)}, u32[]{:S(2)}) %collective-permute-start) | collective-permute-done | bytes 65568 | tf_op jit(solution)/shard_map/ppermute | solution.py:439
  68.1 1.9 %collective-permute-done.1.second_ref = f32[128,128]{1,0:T(8,128)S(1)} collective-permute-done((f32[128,128]{1,0:T(8,128)S(1)}, f32[128,128]{1,0:T(8,128)S(1)}, u32[]{:S(2)}, u32[]{:S(2)}) %collective-permute-start.1) | collective-permute-done | bytes 65568 | tf_op jit(solution)/shard_map/ppermute | solution.py:439
  70.0 1.4 %column.1 = f32[128,128]{1,0:T(8,128)S(1)} custom-call(f32[128,128]{1,0:T(8,128)S(1)} %collective-permute-done.first_ref, f32[128,128]{1,0:T(8,128)S(1)} %all_gather.3.mid_ref, f32[128,128]{1,0:T(8,128)S(1)} %collective-permute-done.1.second_ref, bf16[768,1024]{1,0:T(8,128)(2,1)S(1)} %get-tuple-element.9.w_ref, f32[2,512]{1,0:T(2,128)S(1)} %pad_maximum_fusion.2.bias_ref, ...), custom_call_target="tpu_custom_call" | custom-call | tf_op jit(solution)/shard_map/column/pallas_call | solution.py:448
  71.4 18.1 %all_to_all.15 = f32[128,1,128]{2,1,0:T(1,128)S(1)} all-to-all(f32[128,1,128]{2,1,0:T(1,128)S(1)} %bitcast.23), channel_id=1, replica_groups=mesh['depth'=128,'slab'=2] {'depth'}, dimensions={0} | all-to-all | bytes 131072 | tf_op jit(solution)/shard_map/all_to_all | solution.py:456
  89.5 0.7 output.1
  (10 shorter events, 0.1 us)
Async XLA Ops:
  2.0 26.2 %all-to-all-start = ((s32[128,1,128]{2,1,0:T(1,128)}), s32[128,1,128]{2,1,0:T(1,128)S(1)}, u32[]{:S(2)}, u32[]{:S(2)}) async-start(s32[128,1,128]{2,1,0:T(1,128)} %bitcast.25), calls=%async_computation | async-start | bytes 131072 | tf_op jit(solution)/shard_map/all_to_all | solution.py:362
  17.1 1.3 %copy-start = (bf16[160,32,128]{2,1,0:T(8,128)(2,1)S(1)}, bf16[160,32,128]{2,1,0:T(8,128)(2,1)}, u32[]{:S(2)}) copy-start(bf16[160,32,128]{2,1,0:T(8,128)(2,1)} %src_ref.1) | copy-start | bytes 3932164
  18.4 0.7 copy-start.1
  31.8 6.9 %copy-start.2 = (bf16[9,64,8]{1,2,0:T(8,128)(2,1)S(1)}, bf16[9,64,8]{1,2,0:T(8,128)(2,1)}, u32[]{:S(2)}) copy-start(bf16[9,64,8]{1,2,0:T(8,128)(2,1)} %param.14) | copy-start | bytes 27652
  31.9 7.4 %copy-start.3 = (f32[32]{0:T(128)S(1)}, f32[32]{0:T(128)}, u32[]{:S(2)}) copy-start(f32[32]{0:T(128)} %param.16) | copy-start | bytes 388
  31.9 7.5 %copy-start.4 = (f32[32]{0:T(128)S(1)}, f32[32]{0:T(128)}, u32[]{:S(2)}) copy-start(f32[32]{0:T(128)} %param.15) | copy-start | bytes 388
  31.9 7.6 %copy-start.5 = (f32[32]{0:T(128)S(1)}, f32[32]{0:T(128)}, u32[]{:S(2)}) copy-start(f32[32]{0:T(128)} %param.17) | copy-start | bytes 388
  31.9 28.7 %all-to-all-start.1 = ((s32[128,1,1280]{2,1,0:T(1,128)}), s32[128,1,1280]{2,1,0:T(1,128)S(1)}, u32[]{:S(2)}, u32[]{:S(2)}) async-start(s32[128,1,1280]{2,1,0:T(1,128)} %bitcast.6), calls=%async_computation.1 | async-start | bytes 1310720 | tf_op jit(solution)/shard_map/all_to_all | solution.py:401
  63.8 4.3 %collective-permute-start = (f32[128,128]{1,0:T(8,128)S(1)}, f32[128,128]{1,0:T(8,128)S(1)}, u32[]{:S(2)}, u32[]{:S(2)}) collective-permute-start(f32[128,128]{1,0:T(8,128)S(1)} %all_gather.3.mid_ref), channel_id=1, source_target_pairs={{0,16},{32,48},{112,96},{80,64},{128,144},{160,176},{240,224},{208... | collective-permute-start | bytes 196616 | tf_op jit(solution)/shard_map/ppermute | solution.py:439
  63.9 6.2 %collective-permute-start.1 = (f32[128,128]{1,0:T(8,128)S(1)}, f32[128,128]{1,0:T(8,128)S(1)}, u32[]{:S(2)}, u32[]{:S(2)}) collective-permute-start(f32[128,128]{1,0:T(8,128)S(1)} %all_gather.3.mid_ref), channel_id=1, source_target_pairs={{16,32},{48,112},{96,80},{64,128},{144,160},{176,240},{224,208},{1... | collective-permute-start | bytes 196616 | tf_op jit(solution)/shard_map/ppermute | solution.py:439
